TPU v7x, 256 devices: a whole 4x4x8 slice. The times are simulated.
256 devices in a mesh: img: 8 (over z_hi, core), band: 8 (over z_lo, x), pw: 4 (over y).
Axes of the slice: x: 4, y: 4, z: 8 (z_hi: 4, z_lo: 2; z = z_hi * 2 + z_lo), core: 2. Of those that a mesh axis runs over, the one named last changes fastest.
Arguments:
- coefficients: bfloat16 [8, 1024, 32, 2048], P('img', None, ('band', 'pw')), may hold values from -6 to 6
- rotation: bfloat16 [8, 1024, 256], P('img'), may hold values from -0.1875 to 0.1875
- positions: int32 [8, 3, 256], P('img'), may hold values from 0 to 63, as said below
- start_pos: int32 [3, 256], replicated, may hold values from 0 to 63, as said below
- end_pos: int32 [3, 256], replicated, may hold values from 0 to 63, as said below
- species: int32 [256], replicated, may hold values from 0 to 3
- depth: float32 [4], replicated, may hold values from 0.5 to 3
Outputs:
- correction: bfloat16 [8, 256, 32, 2048], P('img', None, ('band', 'pw'))
- ritz_values: float32 [8, 256], P('img')
- band_force: float32 [8, 3, 256], P('img')
- along_force: float32 [8], P('img')
Inputs may be any that keep to these rules, and one draw needn't show every extreme that they name: `positions`: grid index of each atom's centre along each dimension. `start_pos`: grid index of each atom's centre along each dimension. `end_pos`: grid index of each atom's centre along each dimension.
All inputs are finite; a program needn't handle non-finite values.
Results may differ from a plain program's by a relative error of at most 0.012.
The roundings to bfloat16 on the way count: a program that leaves them out, or rounds other values in their place, can miss the bound.
Values may be sent and summed in bfloat16 or wider, within the bound.
No kernel may reach another device: no remote copies, remote signals or barrier semaphores. Data moves between devices by JAX's collectives and lax.ppermute only.
A program may use at most 128 MiB of HBM per device.

v0:
```python
import math

import jax
import jax.numpy as jnp
import numpy as np
from jax import lax
from jax.experimental import pallas as pl
from jax.experimental.pallas import tpu as pltpu
from jax.sharding import PartitionSpec as P

G = 64
W = 32
BANDS = 1024
BLOCK = 256
SPECIES = 4
NPW = W * W * W
PEERS = 32
OWN = BLOCK // PEERS // 2
HALF = BLOCK // 2
PITCH = 2 * G
ROWS = 136

kinetic_scale = 0.01
sigma_cells = 3.0
spring_constant = 2.0
epsilon = 1e-06

f32 = jnp.float32
bf16 = jnp.bfloat16
GRID_AXES = ("band", "pw")


def host_phases():
    turns = np.mod((np.arange(W) - W // 2)[:, None] * np.arange(G)[None, :], G)
    return turns.astype(np.float32) * np.float32(2.0 * math.pi / G)


def host_tables():
    angle = host_phases()
    cosine, sine = np.cos(angle), np.sin(angle)
    s = np.float32(1.0 / math.sqrt(W))
    fwd = np.stack([np.stack([cosine, sine], 1), np.stack([-sine, cosine], 1)], 0) * s
    t = np.float32(math.sqrt(W) / G)
    c2, s2 = cosine.T * t, sine.T * t
    inv = np.stack([np.stack([c2, -s2], 1), np.stack([s2, c2], 1)], 0)
    left = fwd.transpose(2, 3, 0, 1).reshape(2 * G, 2 * W)
    left_inv = inv.transpose(2, 3, 0, 1).reshape(2 * W, 2 * G)
    eye = np.eye(2, dtype=np.float32)
    z_fwd = np.einsum("cjdn,pq->pcjdqn", fwd, eye).reshape(4 * W, 4 * G)
    z_inv = np.einsum("dncj,pq->dpnqcj", inv, eye).reshape(4 * G, 4 * W)
    return [np.asarray(a, dtype=bf16) for a in (z_fwd, left, left_inv, z_inv)]


def host_pack():
    move = np.zeros((2, 2, 64, 2, 2, 64), np.float32)
    for h in range(2):
        for y in range(2):
            move[h, y, np.arange(64), y, h, np.arange(64)] = 1.0
    return move.reshape(256, 256)


def host_unpack():
    plain = host_pack().T
    e = np.arange(64)
    turn = np.zeros((64, 64), np.float32)
    turn[(e + 32) % 64, e] = np.where(e < 32, 1.0, -1.0)
    whole = np.kron(np.eye(4, dtype=np.float32), turn)
    return np.concatenate([plain, plain @ whole], 1)


def split_two(value):
    high = value.astype(bf16)
    return high, (value - high.astype(f32)).astype(bf16)


def split_three(value):
    high = value.astype(bf16)
    rest = value - high.astype(f32)
    middle = rest.astype(bf16)
    return high, middle, (rest - middle.astype(f32)).astype(bf16)


def dot(a, b):
    return jnp.dot(a, b, preferred_element_type=f32)


def dot_nt(a, b):
    return lax.dot_general(a, b, (((1,), (1,)), ((), ())), preferred_element_type=f32)


def iota(shape, dim):
    return lax.broadcasted_iota(jnp.int32, shape, dim)


def orbitals_kernel(rot_ref, coeff_ref, pack_ref, out_ref, wide_ref):
    step = pl.program_id(0)
    both = lax.dot_general(
        rot_ref[...], coeff_ref[...], (((0,), (0,)), ((), ())), preferred_element_type=f32
    ).astype(bf16)
    lanes = both.shape[1]
    for j in range(lanes // 128):
        at = slice(128 * j, 128 * j + 128)
        pair = jnp.concatenate([both[:HALF, at], both[HALF:, at]], 1)
        moved = dot(pair, pack_ref[...])
        y = step * (lanes // 64) + 2 * j
        wide_ref[pl.ds(y, HALF, stride=W), :] = moved[:, :128]
        wide_ref[pl.ds(y + 1, HALF, stride=W), :] = moved[:, 128:]

    @pl.when(step == pl.num_programs(0) - 1)
    def _():
        out_ref[...] = wide_ref[...].astype(bf16)


def own_orbitals(rotation, coeff):
    lanes = 512
    full = lambda k: (0, 0)
    return pl.pallas_call(
        orbitals_kernel,
        grid=(2048 // lanes,),
        in_specs=[
            pl.BlockSpec((BANDS, BLOCK), full),
            pl.BlockSpec((BANDS, lanes), lambda k: (0, k)),
            pl.BlockSpec((256, 256), full),
        ],
        out_specs=pl.BlockSpec((HALF * W, 128), full),
        out_shape=jax.ShapeDtypeStruct((HALF * W, 128), bf16),
        scratch_shapes=[pltpu.VMEM((HALF * W, 128), f32)],
        compiler_params=pltpu.CompilerParams(vmem_limit_bytes=40 << 20),
        name="orbitals",
    )(rotation, coeff, jnp.asarray(host_pack(), bf16))


def gaussian(position, rows):
    cells = iota((rows, position.shape[1]), 0) & (G - 1)
    offset = (((cells - position + G // 2) & (G - 1)) - G // 2).astype(f32)
    return jnp.exp(-offset * offset / (2.0 * sigma_cells * sigma_cells)), offset


def strengths(species, depth_ref):
    strength = jnp.zeros(species.shape, f32)
    for kind in range(SPECIES):
        strength = jnp.where(species == kind, depth_ref[kind], strength)
    return strength


def potential_kernel(depth_ref, pos_ref, species_ref, out_ref, gy_ref):
    strength = strengths(species_ref[...], depth_ref)
    gauss_x, _ = gaussian(pos_ref[0:1, :], G)
    gauss_x = gauss_x * strength
    gy_ref[...], _ = gaussian(pos_ref[1:2, :], G)
    gauss_z, _ = gaussian(pos_ref[2:3, :], 2 * G)
    z_high, z_low = split_two(gauss_z)
    per = 8

    def some(i, carry):
        for k in range(per):
            m = i * per + k
            value = gauss_x * gy_ref[pl.ds(m, 1), :]
            high, low = split_two(value)
            out_ref[pl.ds(pl.multiple_of(m * G, G), G), :] = (
                dot_nt(high, z_high) + dot_nt(high, z_low) + dot_nt(low, z_high)
            )
        return carry

    lax.fori_loop(0, G // per, some, 0)


def vmem(count):
    return [pl.BlockSpec(memory_space=pltpu.VMEM)] * count


def grid_potential(depth, pos, species):
    return pl.pallas_call(
        potential_kernel,
        in_specs=[pl.BlockSpec(memory_space=pltpu.SMEM)] + vmem(2),
        out_specs=vmem(1)[0],
        out_shape=jax.ShapeDtypeStruct((G * G, 128), f32),
        scratch_shapes=[pltpu.VMEM((G, 256), f32)],
        compiler_params=pltpu.CompilerParams(vmem_limit_bytes=40 << 20),
        name="potential",
    )(depth, pos, species)


def transform_kernel(
    orb_ref, pot_ref, zf_ref, left_ref, left_inv_ref, zi_ref,
    out_ref, ritz_ref, dens_ref,
    mid_ref, ham_ref, num_ref, den_ref,
):
    group = 2
    rows = group * OWN * W

    def forward(i, carry):
        x = i * group
        zin = orb_ref[pl.ds(pl.multiple_of(x * OWN * W, rows), rows), :]
        along_z = dot(zin, zf_ref[...]).astype(bf16)
        parts = []
        for g in range(group * OWN):
            piece = along_z[W * g : W * g + W]
            parts.append(jnp.concatenate([piece[:, :128], piece[:, 128:]], 0))
        along_y = dot(left_ref[...], jnp.concatenate(parts, 1))
        for g in range(group * OWN):
            xx, tt = x + g // OWN, g % OWN
            at = pl.multiple_of((tt * W + xx) * PITCH, 8)
            mid_ref[pl.ds(at, 2 * G), :] = along_y[:, 128 * g : 128 * g + 128]
        return carry

    lax.fori_loop(0, W // group, forward, 0)

    def space(m, carry):
        parts = []
        for tt in range(OWN):
            base = tt * W * PITCH + m
            parts.append(
                jnp.concatenate(
                    [mid_ref[pl.ds(base + c * G, W, stride=PITCH), :] for c in range(2)], 0
                ).astype(bf16)
            )
        in_space = dot(left_ref[...], jnp.concatenate(parts, 1))
        at = pl.multiple_of(m * G, G)
        potential = pot_ref[pl.ds(at, G), :]
        potential = jnp.concatenate([potential, potential], 0)
        density = jnp.zeros((2 * G, 128), f32)
        weighted = []
        for tt in range(OWN):
            one = in_space[:, 128 * tt : 128 * tt + 128]
            density = density + one * one
            weighted.append((one * potential).astype(bf16))
        dens_ref[pl.ds(at, G), :] = (density[:G] + density[G:]) * (1.0 / BLOCK)
        back = dot(left_inv_ref[...], jnp.concatenate(weighted, 1))
        for tt in range(OWN):
            base = tt * W * PITCH + m
            for c in range(2):
                mid_ref[pl.ds(base + c * G, W, stride=PITCH), :] = back[
                    W * c : W * c + W, 128 * tt : 128 * tt + 128
                ]
        return carry

    lax.fori_loop(0, G, space, 0)

    lane = iota((W, 128), 1)
    wave_y = iota((W, 128), 0) - W // 2
    wave_z = (lane & (W - 1)) - W // 2
    plane = wave_y * wave_y + wave_z * wave_z

    def kinetic(x):
        wave_x = x - W // 2
        return (kinetic_scale * 0.5) * (plane + wave_x * wave_x).astype(f32)

    num_ref[...] = jnp.zeros_like(num_ref)
    den_ref[...] = jnp.zeros_like(den_ref)

    def backward(i, carry):
        x = i * group
        parts = []
        for g in range(group * OWN):
            xx, tt = x + g // OWN, g % OWN
            at = pl.multiple_of((tt * W + xx) * PITCH, 8)
            parts.append(mid_ref[pl.ds(at, 2 * G), :].astype(bf16))
        back_y = dot(left_inv_ref[...], jnp.concatenate(parts, 1)).astype(bf16)
        parts = []
        for g in range(group * OWN):
            piece = back_y[:, 128 * g : 128 * g + 128]
            parts.append(jnp.concatenate([piece[:W], piece[W:]], 1))
        local = dot(jnp.concatenate(parts, 0), zi_ref[...])
        for g in range(group * OWN):
            xx, tt = x + g // OWN, g % OWN
            at = pl.multiple_of((xx * OWN + tt) * W, W)
            orbital = orb_ref[pl.ds(at, W), :].astype(f32)
            ham = kinetic(xx) * orbital + local[W * g : W * g + W]
            ham_ref[pl.ds(at, W), :] = ham
            num_ref[pl.ds(tt * W, W), :] += orbital * ham
            den_ref[pl.ds(tt * W, W), :] += orbital * orbital
        return carry

    lax.fori_loop(0, W // group, backward, 0)

    lane_row = iota((1, 128), 1)
    low = lane_row < 64
    ritz_row = jnp.zeros((1, 128), f32)
    ritz = []
    for tt in range(OWN):
        halves = []
        num = jnp.sum(num_ref[pl.ds(tt * W, W), :], 0, keepdims=True)
        den = jnp.sum(den_ref[pl.ds(tt * W, W), :], 0, keepdims=True)
        for p in range(2):
            mine = low if p == 0 else jnp.logical_not(low)
            top = jnp.sum(jnp.where(mine, num, 0.0), 1, keepdims=True)
            bottom = jnp.sum(jnp.where(mine, den, 0.0), 1, keepdims=True)
            value = (top / NPW) / (bottom / NPW + epsilon)
            halves.append(value)
            ritz_row = jnp.where(lane_row == 32 + p * OWN + tt, value, ritz_row)
        ritz.append(jnp.where(low, halves[0], halves[1]))
    ritz_ref[...] = jnp.broadcast_to(ritz_row, (8, 128))

    def finish(x, carry):
        kin = kinetic(x)
        scale = 1.0 / (1.0 + kin)
        for tt in range(OWN):
            at = pl.multiple_of((x * OWN + tt) * W, W)
            orbital = orb_ref[pl.ds(at, W), :].astype(f32)
            residual = ham_ref[pl.ds(at, W), :] - ritz[tt] * orbital
            out_ref[pl.ds(at, W), :] = (residual * scale).astype(bf16)
        return carry

    lax.fori_loop(0, W, finish, 0, unroll=2)


def searched(orbitals, potential):
    z_fwd, left, left_inv, z_inv = host_tables()
    return pl.pallas_call(
        transform_kernel,
        in_specs=vmem(6),
        out_specs=vmem(3),
        out_shape=[
            jax.ShapeDtypeStruct((W * OWN * W, 128), bf16),
            jax.ShapeDtypeStruct((8, 128), f32),
            jax.ShapeDtypeStruct((G * G, 128), f32),
        ],
        scratch_shapes=[
            pltpu.VMEM((OWN * W * PITCH, 128), f32),
            pltpu.VMEM((W * OWN * W, 128), f32),
            pltpu.VMEM((OWN * W, 128), f32),
            pltpu.VMEM((OWN * W, 128), f32),
        ],
        compiler_params=pltpu.CompilerParams(vmem_limit_bytes=48 << 20),
        name="transform",
    )(orbitals, potential, z_fwd, left, left_inv, z_inv)


def force_kernel(
    depth_ref, dens_ref, pos_ref, species_ref, ritz_ref, out_ref, gy_ref, gyo_ref, wide_ref
):
    strength = strengths(species_ref[...], depth_ref)
    gauss_x, offset_x = gaussian(pos_ref[0:1, :], G)
    gauss_y, offset_y = gaussian(pos_ref[1:2, :], G)
    gauss_z, offset_z = gaussian(pos_ref[2:3, :], 2 * G)
    gy_ref[...] = gauss_y
    gyo_ref[...] = gauss_y * offset_y
    high, low = split_two(jnp.concatenate([gauss_z, gauss_z * offset_z], 1))
    both = jnp.concatenate([high, low], 0)
    per = 4

    def some(i, carry):
        sum_x, sum_y, sum_z = carry
        at = pl.multiple_of(i * per * G, per * G)
        d_high, d_low = split_two(dens_ref[pl.ds(at, per * G), :])
        moments = dot(jnp.concatenate([d_high, d_high], 1), both) + dot(d_low, high)
        for k in range(per):
            gy = gy_ref[pl.ds(i * per + k, 1), :]
            gyo = gyo_ref[pl.ds(i * per + k, 1), :]
            plain = moments[G * k : G * k + G, :256]
            sum_x = sum_x + plain * gy
            sum_y = sum_y + plain * gyo
            sum_z = sum_z + moments[G * k : G * k + G, 256:] * gy
        return sum_x, sum_y, sum_z

    zero = jnp.zeros((G, 256), f32)
    sum_x, sum_y, sum_z = lax.fori_loop(0, G // per, some, (zero, zero, zero))
    factor = -strength / (sigma_cells * sigma_cells)
    force = [
        factor * jnp.sum(gauss_x * offset_x * sum_x, 0, keepdims=True),
        factor * jnp.sum(gauss_x * sum_y, 0, keepdims=True),
        factor * jnp.sum(gauss_x * sum_z, 0, keepdims=True),
    ]
    peer, atom = iota((PEERS, 256), 0), iota((PEERS, 256), 1)
    from_atom, lane = iota((256, 128), 0), iota((256, 128), 1)
    parts = [part.astype(f32) for part in split_three(ritz_ref[0:1, :])]
    totals = [jnp.broadcast_to(part, (PEERS, 128)) for part in parts]
    for alpha in range(3):
        own = jnp.where(atom // 8 == peer, force[alpha], 0.0)
        choose = jnp.where((from_atom & 7) + 8 * alpha == lane, 1.0, 0.0).astype(bf16)
        for k, part in enumerate(split_three(own)):
            totals[k] = totals[k] + dot(part, choose)
    wide_ref[...] = jnp.zeros_like(wide_ref)
    for k in range(3):
        wide_ref[pl.ds(k, PEERS, stride=8), :] = totals[k]
    out_ref[...] = wide_ref[...].reshape(PEERS, 8, 128).astype(bf16)


def force_parts(depth, density, pos, species, ritz):
    return pl.pallas_call(
        force_kernel,
        in_specs=[pl.BlockSpec(memory_space=pltpu.SMEM)] + vmem(4),
        out_specs=vmem(1)[0],
        out_shape=jax.ShapeDtypeStruct((PEERS, 8, 128), bf16),
        scratch_shapes=[
            pltpu.VMEM((G, 256), f32),
            pltpu.VMEM((G, 256), f32),
            pltpu.VMEM((PEERS * 8, 128), f32),
        ],
        compiler_params=pltpu.CompilerParams(vmem_limit_bytes=40 << 20),
        name="force",
    )(depth, density, pos, species, ritz)


def intersect_kernel(
    search_ref, unpack_ref, coeff_ref, extra_ref, out_ref, flat_ref, wide_ref, pair_ref
):
    step = pl.program_id(0)

    @pl.when(step == 0)
    def _():
        wide_ref[...] = search_ref[...].astype(f32)
        for j in range(W // 2):
            even = wide_ref[pl.ds(2 * j, HALF, stride=W), :]
            odd = wide_ref[pl.ds(2 * j + 1, HALF, stride=W), :]
            moved = dot(jnp.concatenate([even, odd], 1).astype(bf16), unpack_ref[...]).astype(bf16)
            at = slice(128 * j, 128 * j + 128)
            for q in range(4):
                pair_ref[HALF * q : HALF * q + HALF, at] = moved[:, 128 * q : 128 * q + 128]
        flat_ref[...] = pair_ref[: 2 * HALF, :]
        out_ref[:, 128:, :] = extra_ref[...]

    part = (dot_nt(pair_ref[...], coeff_ref[...]) * (1.0 / NPW)).astype(bf16)
    tiles = coeff_ref.shape[0] // 128
    for j in range(tiles):
        out_ref[:, pl.ds(pl.multiple_of((step * tiles + j) * 16, 16), 16), :] = part[
            :, 128 * j : 128 * j + 128
        ].reshape(PEERS, 16, 128)


def own_intersections(search, coeff, extra):
    some = 256
    full2 = lambda k: (0, 0)
    full3 = lambda k: (0, 0, 0)
    return pl.pallas_call(
        intersect_kernel,
        grid=(BANDS // some,),
        in_specs=[
            pl.BlockSpec((HALF * W, 128), full2),
            pl.BlockSpec((256, 512), full2),
            pl.BlockSpec((some, 2048), lambda k: (k, 0)),
            pl.BlockSpec((PEERS, 8, 128), full3),
        ],
        out_specs=[
            pl.BlockSpec((PEERS, ROWS, 128), full3),
            pl.BlockSpec((BLOCK, 2048), full2),
        ],
        out_shape=[
            jax.ShapeDtypeStruct((PEERS, ROWS, 128), bf16),
            jax.ShapeDtypeStruct((BLOCK, 2048), bf16),
        ],
        scratch_shapes=[
            pltpu.VMEM((HALF * W, 128), f32),
            pltpu.VMEM((2 * BLOCK, 2048), bf16),
        ],
        compiler_params=pltpu.CompilerParams(vmem_limit_bytes=48 << 20),
        name="intersect",
    )(search, jnp.asarray(host_unpack(), bf16), coeff, extra)


def total_kernel(in_ref, out_ref):
    for r in range(8):
        at = slice(16 * r, 16 * r + 16)
        total = in_ref[0, at, :].astype(f32)
        for peer in range(1, PEERS):
            total = total + in_ref[peer, at, :].astype(f32)
        total = total.astype(bf16)
        for peer in range(PEERS):
            out_ref[peer, at, :] = total
    extra = in_ref[0, 128:, :].astype(f32)
    for peer in range(1, PEERS):
        extra = extra + in_ref[peer, 128:, :].astype(f32)
    high, middle, low = split_three(extra[0:1] + extra[1:2] + extra[2:3])
    row = iota((8, 128), 0)
    parts = jnp.where(row == 0, high.astype(f32), 0.0)
    parts = jnp.where(row == 1, middle.astype(f32), parts)
    parts = jnp.where(row == 2, low.astype(f32), parts).astype(bf16)
    for peer in range(PEERS):
        out_ref[peer, 128:, :] = parts


def totals_for_all(arrived):
    return pl.pallas_call(
        total_kernel,
        in_specs=vmem(1),
        out_specs=vmem(1)[0],
        out_shape=jax.ShapeDtypeStruct((PEERS, ROWS, 128), bf16),
        compiler_params=pltpu.CompilerParams(vmem_limit_bytes=40 << 20),
        name="total",
    )(arrived)


def wrap_offset(values):
    return ((values + G // 2) & (G - 1)) - G // 2


def project_kernel(
    image_ref, whole_ref, first_ref, coeff_ref, flat_ref, pos_ref, before_ref, after_ref,
    start_ref, end_ref, out_ref, ritz_ref, push_ref, along_ref, inter_ref,
):
    step = pl.program_id(0)

    @pl.when(step == 0)
    def _():
        for j in range(8):
            inter_ref[:, 128 * j : 128 * j + 128] = whole_ref[:, 16 * j : 16 * j + 16, :].reshape(
                2 * BLOCK, 128
            )

    projected = dot(inter_ref[...], coeff_ref[...])
    lanes = projected.shape[1]
    first = (iota((BLOCK, 128), 1) & 63) < 32
    for j in range(lanes // 128):
        at = slice(128 * j, 128 * j + 128)
        turned = projected[BLOCK:, at]
        turned = jnp.where(first, -pltpu.roll(turned, 96, 1), pltpu.roll(turned, 32, 1))
        out_ref[:, at] = (flat_ref[:, at].astype(f32) - (projected[:BLOCK, at] + turned)).astype(bf16)

    @pl.when(step == pl.num_programs(0) - 1)
    def _():
        lane, column = iota((128, 256), 0), iota((128, 256), 1)
        peer, at = iota((PEERS, 256), 0), iota((PEERS, 256), 1)

        def row_of(ref, base, lane_wanted, peer_wanted):
            choose = jnp.where(lane == lane_wanted, 1.0, 0.0).astype(bf16)
            total = jnp.zeros((1, 256), f32)
            parts = ref[:, base : base + 8, :].astype(f32)
            for k in range(3):
                here = dot(parts[:, k, :].astype(bf16), choose)
                here = jnp.where(peer == peer_wanted, here, 0.0)
                total = total + jnp.sum(here, 0, keepdims=True)
            return total

        ritz_ref[...] = row_of(
            first_ref, 0, 32 + OWN * (column // HALF) + column % OWN, at % HALF // OWN
        )
        pos = pos_ref[...]
        image = image_ref[0]
        before = jnp.where(image == 0, start_ref[...], before_ref[...])
        after = jnp.where(image == image_ref[1] - 1, end_ref[...], after_ref[...])
        ahead = wrap_offset(after - pos).astype(f32)
        behind = wrap_offset(pos - before).astype(f32)
        raw = ahead + behind
        entries = pos.shape[0] * pos.shape[1]

        def mean_square(value):
            return jnp.sum(jnp.sum(value * value, 1, keepdims=True), 0, keepdims=True) / entries

        tangent = raw * lax.rsqrt(mean_square(raw) + epsilon) * (1.0 / math.sqrt(entries))
        length_ahead = jnp.sqrt(entries * (mean_square(ahead) + epsilon))
        length_behind = jnp.sqrt(entries * (mean_square(behind) + epsilon))
        force = jnp.concatenate(
            [row_of(whole_ref, 128, 8 * alpha + (column & 7), at // 8) for alpha in range(3)], 0
        )
        along = jnp.sum(jnp.sum(force * tangent, 1, keepdims=True), 0, keepdims=True)
        push_ref[...] = (
            force - along * tangent + spring_constant * (length_ahead - length_behind) * tangent
        )
        along_ref[...] = along


def corrected(image, whole, arrived, coeff, flat, pos, before, after, start_pos, end_pos):
    lanes = 256
    full2 = lambda k: (0, 0)
    full3 = lambda k: (0, 0, 0)
    small = pl.BlockSpec((3, 256), full2)
    return pl.pallas_call(
        project_kernel,
        grid=(2048 // lanes,),
        in_specs=[
            pl.BlockSpec(memory_space=pltpu.SMEM),
            pl.BlockSpec((PEERS, ROWS, 128), full3),
            pl.BlockSpec((PEERS, 8, 128), lambda k: (0, 16, 0)),
            pl.BlockSpec((BANDS, lanes), lambda k: (0, k)),
            pl.BlockSpec((BLOCK, lanes), lambda k: (0, k)),
            small, small, small, small, small,
        ],
        out_specs=[
            pl.BlockSpec((BLOCK, lanes), lambda k: (0, k)),
            pl.BlockSpec((1, 256), full2),
            pl.BlockSpec((3, 256), full2),
            pl.BlockSpec((1, 1), full2),
        ],
        out_shape=[
            jax.ShapeDtypeStruct((BLOCK, 2048), bf16),
            jax.ShapeDtypeStruct((1, 256), f32),
            jax.ShapeDtypeStruct((3, 256), f32),
            jax.ShapeDtypeStruct((1, 1), f32),
        ],
        scratch_shapes=[pltpu.VMEM((2 * BLOCK, BANDS), bf16)],
        compiler_params=pltpu.CompilerParams(vmem_limit_bytes=48 << 20),
        name="project",
    )(image, whole, arrived, coeff, flat, pos, before, after, start_pos, end_pos)


def exchanged(array):
    return lax.all_to_all(array, GRID_AXES, split_axis=0, concat_axis=0, tiled=True)


def passed_along(block, axis, distance):
    devices = range(lax.axis_size(axis))
    route = [(i - distance, i) for i in devices if i - distance in devices]
    return lax.ppermute(block, axis, route)


def body(coefficients, rotation, positions, start_pos, end_pos, species, depth):
    coeff = coefficients.reshape(BANDS, 2048)
    pos = positions[0]
    kinds = species.reshape(1, -1)
    orbitals = own_orbitals(rotation[0], coeff)
    vectors = exchanged(orbitals.reshape(PEERS, OWN * W, 128))
    before = passed_along(pos, "img", 1)
    after = passed_along(pos, "img", -1)
    potential = grid_potential(depth, pos, kinds)
    search, ritz, density = searched(vectors.reshape(W * OWN * W, 128), potential)
    own_search = exchanged(search.reshape(PEERS, OWN * W, 128))
    extra = force_parts(depth, density, pos, kinds, ritz)
    parts, flat = own_intersections(own_search.reshape(HALF * W, 128), coeff, extra)
    arrived = exchanged(parts)
    whole = exchanged(totals_for_all(arrived))
    image = jnp.stack([lax.axis_index("img"), lax.axis_size("img")]).astype(jnp.int32)
    correction, ritz_values, push, along = corrected(
        image, whole, arrived, coeff, flat, pos, before, after, start_pos, end_pos
    )
    return (correction.reshape(1, BLOCK, 1, 2048), ritz_values, push[None], along.reshape(1))


def solution(mesh):
    in_specs = (
        P("img", None, GRID_AXES, None),
        P("img", None, None),
        P("img", None, None),
        P(),
        P(),
        P(),
        P(),
    )
    out_specs = (
        P("img", None, GRID_AXES, None),
        P("img", None),
        P("img", None, None),
        P("img"),
    )
    return jax.shard_map(body, mesh=mesh, in_specs=in_specs, out_specs=out_specs, check_vma=False)
```

profile of v0, /device:TPU:67, one launch (start us, length us, event | category | flops | bytes accessed | tf_op | source)
XLA Modules:
  0.0 160.4 jit_solution(16920314127492779706)
XLA Ops:
  0.6 0.0 copy-start
  0.6 2.2 %copy-done = bf16[1,1024,1,2048]{3,1,2,0:T(8,128)(2,1)S(1)} copy-done((bf16[1,1024,1,2048]{3,1,2,0:T(8,128)(2,1)S(1)}, bf16[1,1024,1,2048]{3,1,2,0:T(8,128)(2,1)}, u32[]{:S(2)}) %copy-start) | copy-done | bytes 4194328
  2.8 0.0 copy-start.3
  2.8 1.0 copy-done.3
  3.9 0.0 copy-start.5
  3.9 0.9 copy-done.5
  4.8 4.9 %orbitals.1 = bf16[4096,128]{1,0:T(8,128)(2,1)} custom-call(bf16[1024,256]{1,0:T(8,128)(2,1)S(1)} %bitcast.20, bf16[1024,2048]{1,0:T(8,128)(2,1)S(1)} %bitcast.16, bf16[256,256]{1,0:T(8,128)(2,1)S(1)} %copy-done.5), custom_call_target="tpu_custom_call" | custom-call | tf_op jit(solution)/shard_map/orbitals/pallas_call | solution.py:117
  9.6 0.0 copy-start.14
  9.6 0.0 copy-start.12
  9.6 0.0 copy-start.13
  9.6 8.5 %all-to-all-start = ((bf16[32,128,128]{2,1,0:T(8,128)(2,1)}), bf16[32,128,128]{2,1,0:T(8,128)(2,1)S(1)}, u32[]{:S(2)}, u32[]{:S(2)}) async-start(bf16[32,128,128]{2,1,0:T(8,128)(2,1)} %bitcast.3), calls=%async_computation | async-start | bytes 2097152 | tf_op jit(solution)/shard_map/all_to_all | solution.py:588
  18.2 0.0 copy-done.14
  18.2 0.0 copy-start.6
  18.2 0.0 copy-start.7
  18.2 0.0 copy-start.8
  18.2 0.0 copy-start.9
  18.2 0.0 copy-done.12
  18.3 0.0 copy-done.13
  18.3 5.9 %potential.1.pot_ref = f32[4096,128]{1,0:T(8,128)S(1)} custom-call(f32[4]{0:T(128)S(1)} %copy-done.13, s32[3,256]{1,0:T(4,128)S(1)} %bitcast.21, s32[1,256]{1,0:T(1,128)S(1)} %bitcast.26), custom_call_target="tpu_custom_call" | custom-call | tf_op jit(solution)/shard_map/potential/pallas_call | solution.py:173
  24.2 0.0 copy-start.1
  24.2 1.3 copy-done.1
  25.6 6.6 %all-to-all-done = bf16[32,128,128]{2,1,0:T(8,128)(2,1)S(1)} async-done(((bf16[32,128,128]{2,1,0:T(8,128)(2,1)}), bf16[32,128,128]{2,1,0:T(8,128)(2,1)S(1)}, u32[]{:S(2)}, u32[]{:S(2)}) %all-to-all-start) | async-done | bytes 1048608 | tf_op jit(solution)/shard_map/all_to_all | solution.py:588
  32.1 0.0 copy-done.6
  32.1 0.0 copy-done.7
  32.1 0.0 copy-done.8
  32.1 0.0 copy-done.9
  32.1 48.2 %transform.1 = (bf16[4096,128]{1,0:T(8,128)(2,1)S(1)}, f32[8,128]{1,0:T(8,128)S(1)}, f32[4096,128]{1,0:T(8,128)S(1)}) custom-call(bf16[4096,128]{1,0:T(8,128)(2,1)S(1)} %bitcast.17, f32[4096,128]{1,0:T(8,128)} %copy-done.1, bf16[128,256]{1,0:T(8,128)(2,1)S(1)} %copy-done.6, bf16[128,64]{1,0:T(8,128)(2,1)S(1)} %copy-done.8, bf16[64,128]{1,0:T(8,128)(2,1)S(1)} %copy-done.9, ...), custom_call_target="tpu_custom_call" | custom-call | tf_op jit(solution)/shard_map/transform/pallas_call | solution.py:310
  80.3 0.0 copy-start.2
  80.3 1.0 copy-done.2
  81.3 6.6 %all-to-all-start.1 = ((bf16[32,128,128]{2,1,0:T(8,128)(2,1)}), bf16[32,128,128]{2,1,0:T(8,128)(2,1)S(1)}, u32[]{:S(2)}, u32[]{:S(2)}) async-start(bf16[32,128,128]{2,1,0:T(8,128)(2,1)} %bitcast.19), calls=%async_computation.1 | async-start | bytes 2097152 | tf_op jit(solution)/shard_map/all_to_all | solution.py:588
  87.9 0.0 copy-start.4
  87.9 5.8 %force.1.extra_ref = bf16[32,8,128]{2,1,0:T(8,128)(2,1)S(1)} custom-call(f32[4]{0:T(128)S(1)} %copy-done.13, f32[4096,128]{1,0:T(8,128)S(1)} %get-tuple-element.14.dens_ref, s32[3,256]{1,0:T(4,128)S(1)} %bitcast.22, s32[1,256]{1,0:T(1,128)S(1)} %bitcast.27, f32[8,128]{1,0:T(8,128)S(1)} %get-tuple-element.15.ritz_ref), custom_call_target="tpu_custom_call" | custom-call | tf_op jit(solution)/shard_map/force/pallas_call | solution.py:381
  93.6 7.8 %all-to-all-done.1 = bf16[32,128,128]{2,1,0:T(8,128)(2,1)S(1)} async-done(((bf16[32,128,128]{2,1,0:T(8,128)(2,1)}), bf16[32,128,128]{2,1,0:T(8,128)(2,1)S(1)}, u32[]{:S(2)}, u32[]{:S(2)}) %all-to-all-start.1) | async-done | bytes 1048608 | tf_op jit(solution)/shard_map/all_to_all | solution.py:588
  101.4 0.0 copy-done.4
  101.4 6.8 %intersect.1 = (bf16[32,136,128]{2,1,0:T(8,128)(2,1)S(1)}, bf16[256,2048]{1,0:T(8,128)(2,1)S(1)}) custom-call(bf16[4096,128]{1,0:T(8,128)(2,1)S(1)} %bitcast.18, bf16[256,512]{1,0:T(8,128)(2,1)S(1)} %copy-done.4, bf16[1024,2048]{1,0:T(8,128)(2,1)} %bitcast.14, bf16[32,8,128]{2,1,0:T(8,128)(2,1)S(1)} %force.1.extra_ref), custom_call_target="tpu_custom_call" | custom-call | tf_op jit(solution)/shard_map/intersect/pallas_call | solution.py:426
  108.2 19.8 %all_to_all.20.in_ref.first_ref = bf16[32,136,128]{2,1,0:T(8,128)(2,1)S(1)} all-to-all(bf16[32,136,128]{2,1,0:T(8,128)(2,1)S(1)} %get-tuple-element.16), channel_id=1, replica_groups=mesh['img'=8,'band'=8,'pw'=4] {'band','pw'}, dimensions={0} | all-to-all | bytes 2228224 | tf_op jit(solution)/shard_map/all_to_all | solution.py:588
  128.0 1.2 total.1
  129.2 5.5 %all-to-all-start.3 = ((bf16[32,136,128]{2,1,0:T(8,128)(2,1)}), bf16[32,136,128]{2,1,0:T(8,128)(2,1)S(1)}, u32[]{:S(2)}, u32[]{:S(2)}) async-start(bf16[32,136,128]{2,1,0:T(8,128)(2,1)} %total.1), calls=%async_computation.3 | async-start | bytes 2228224 | tf_op jit(solution)/shard_map/all_to_all | solution.py:588
  134.7 9.0 %collective-permute-start = (s32[3,256]{1,0:T(4,128)S(1)}, s32[3,256]{1,0:T(4,128)S(1)}, u32[]{:S(2)}, u32[]{:S(2)}) collective-permute-start(s32[3,256]{1,0:T(4,128)S(1)} %bitcast.23), channel_id=1, source_target_pairs={{0,32},{32,64},{64,96},{96,128},{128,160},{160,192},{192,224},{1,3... | collective-permute-start | bytes 9224 | tf_op jit(solution)/shard_map/ppermute | solution.py:594
  143.7 1.9 %collective-permute-start.1 = (s32[3,256]{1,0:T(4,128)S(1)}, s32[3,256]{1,0:T(4,128)S(1)}, u32[]{:S(2)}, u32[]{:S(2)}) collective-permute-start(s32[3,256]{1,0:T(4,128)S(1)} %bitcast.24), channel_id=1, source_target_pairs={{32,0},{64,32},{96,64},{128,96},{160,128},{192,160},{224,192},{33,... | collective-permute-start | bytes 9224 | tf_op jit(solution)/shard_map/ppermute | solution.py:594
  145.6 0.1 pad_add_fusion.image_ref
  145.7 0.0 collective-permute-done.before_ref
  145.7 5.3 %collective-permute-done.1.after_ref = s32[3,256]{1,0:T(4,128)S(1)} collective-permute-done((s32[3,256]{1,0:T(4,128)S(1)}, s32[3,256]{1,0:T(4,128)S(1)}, u32[]{:S(2)}, u32[]{:S(2)}) %collective-permute-start.1) | collective-permute-done | bytes 3104 | tf_op jit(solution)/shard_map/ppermute | solution.py:594
  151.0 0.0 all-to-all-done.3.whole_ref
  151.0 0.0 copy-done.10
  151.0 0.0 copy-done.11
  151.0 8.8 %project.1 = (bf16[256,2048]{1,0:T(8,128)(2,1)}, f32[1,256]{1,0:T(1,128)}, f32[3,256]{1,0:T(4,128)S(1)}, f32[1,1]{1,0:T(1,128)}) custom-call(s32[2]{0:T(128)S(1)} %pad_add_fusion.image_ref, bf16[32,136,128]{2,1,0:T(8,128)(2,1)S(1)} %all-to-all-done.3.whole_ref, bf16[32,136,128]{2,1,0:T(8,128)(2,1)S(1)} %all_to_all.20.in_ref.first_ref, ...), custom_call_target="tpu_custom_call" | custom-call | tf_op jit(solution)/shard_map/project/pallas_call | solution.py:558
  159.8 0.6 copy.17
  (3 shorter events, 0.0 us)
Async XLA Ops:
  0.6 2.2 %copy-start = (bf16[1,1024,1,2048]{3,1,2,0:T(8,128)(2,1)S(1)}, bf16[1,1024,1,2048]{3,1,2,0:T(8,128)(2,1)}, u32[]{:S(2)}) copy-start(bf16[1,1024,1,2048]{3,1,2,0:T(8,128)(2,1)} %param.13) | copy-start | bytes 12582916
  2.8 1.0 copy-start.3
  3.9 0.9 copy-start.5
  9.6 8.6 %copy-start.14 = (s32[1,3,256]{2,0,1:T(1,128)S(1)}, s32[1,3,256]{2,0,1:T(1,128)}, u32[]{:S(2)}) copy-start(s32[1,3,256]{2,0,1:T(1,128)} %param.15) | copy-start | bytes 9220
  9.6 8.6 %copy-start.12 = (s32[256]{0:T(256)S(1)}, s32[256]{0:T(256)}, u32[]{:S(2)}) copy-start(s32[256]{0:T(256)} %param.18) | copy-start | bytes 3076
  9.6 8.6 %copy-start.13 = (f32[4]{0:T(128)S(1)}, f32[4]{0:T(128)}, u32[]{:S(2)}) copy-start(f32[4]{0:T(128)} %depth_ref.3) | copy-start | bytes 52
  9.6 22.5 %all-to-all-start = ((bf16[32,128,128]{2,1,0:T(8,128)(2,1)}), bf16[32,128,128]{2,1,0:T(8,128)(2,1)S(1)}, u32[]{:S(2)}, u32[]{:S(2)}) async-start(bf16[32,128,128]{2,1,0:T(8,128)(2,1)} %bitcast.3), calls=%async_computation | async-start | bytes 2097152 | tf_op jit(solution)/shard_map/all_to_all | solution.py:588
  18.2 13.9 %copy-start.6 = (bf16[128,256]{1,0:T(8,128)(2,1)S(1)}, bf16[128,256]{1,0:T(8,128)(2,1)}, u32[]{:S(2)}) copy-start(bf16[128,256]{1,0:T(8,128)(2,1)} %constant.21.clone.zf_ref) | copy-start | bytes 196612
  18.2 13.9 %copy-start.7 = (bf16[256,128]{1,0:T(8,128)(2,1)S(1)}, bf16[256,128]{1,0:T(8,128)(2,1)}, u32[]{:S(2)}) copy-start(bf16[256,128]{1,0:T(8,128)(2,1)} %constant.24.clone.zi_ref) | copy-start | bytes 196612
  18.2 13.9 %copy-start.8 = (bf16[128,64]{1,0:T(8,128)(2,1)S(1)}, bf16[128,64]{1,0:T(8,128)(2,1)}, u32[]{:S(2)}) copy-start(bf16[128,64]{1,0:T(8,128)(2,1)} %constant.22.clone.left_ref) | copy-start | bytes 49156
  18.2 13.9 %copy-start.9 = (bf16[64,128]{1,0:T(8,128)(2,1)S(1)}, bf16[64,128]{1,0:T(8,128)(2,1)}, u32[]{:S(2)}) copy-start(bf16[64,128]{1,0:T(8,128)(2,1)} %constant.23.clone.left_inv_ref) | copy-start | bytes 49156
  24.2 1.4 copy-start.1
  80.3 1.0 copy-start.2
  81.3 20.1 %all-to-all-start.1 = ((bf16[32,128,128]{2,1,0:T(8,128)(2,1)}), bf16[32,128,128]{2,1,0:T(8,128)(2,1)S(1)}, u32[]{:S(2)}, u32[]{:S(2)}) async-start(bf16[32,128,128]{2,1,0:T(8,128)(2,1)} %bitcast.19), calls=%async_computation.1 | async-start | bytes 2097152 | tf_op jit(solution)/shard_map/all_to_all | solution.py:588
  87.9 13.6 %copy-start.4 = (bf16[256,512]{1,0:T(8,128)(2,1)S(1)}, bf16[256,512]{1,0:T(8,128)(2,1)}, u32[]{:S(2)}) copy-start(bf16[256,512]{1,0:T(8,128)(2,1)} %constant.25.clone.unpack_ref) | copy-start | bytes 786436
  129.2 21.8 %copy-start.10 = (s32[3,256]{1,0:T(4,128)S(1)}, s32[3,256]{1,0:T(4,128)}, u32[]{:S(2)}) copy-start(s32[3,256]{1,0:T(4,128)} %start_ref.1) | copy-start | bytes 9220
  129.2 21.8 %copy-start.11 = (s32[3,256]{1,0:T(4,128)S(1)}, s32[3,256]{1,0:T(4,128)}, u32[]{:S(2)}) copy-start(s32[3,256]{1,0:T(4,128)} %end_ref.1) | copy-start | bytes 9220
  129.2 21.8 %all-to-all-start.3 = ((bf16[32,136,128]{2,1,0:T(8,128)(2,1)}), bf16[32,136,128]{2,1,0:T(8,128)(2,1)S(1)}, u32[]{:S(2)}, u32[]{:S(2)}) async-start(bf16[32,136,128]{2,1,0:T(8,128)(2,1)} %total.1), calls=%async_computation.3 | async-start | bytes 2228224 | tf_op jit(solution)/shard_map/all_to_all | solution.py:588
  134.7 11.0 %collective-permute-start = (s32[3,256]{1,0:T(4,128)S(1)}, s32[3,256]{1,0:T(4,128)S(1)}, u32[]{:S(2)}, u32[]{:S(2)}) collective-permute-start(s32[3,256]{1,0:T(4,128)S(1)} %bitcast.23), channel_id=1, source_target_pairs={{0,32},{32,64},{64,96},{96,128},{128,160},{160,192},{192,224},{1,3... | collective-permute-start | bytes 9224 | tf_op jit(solution)/shard_map/ppermute | solution.py:594
  143.7 7.3 %collective-permute-start.1 = (s32[3,256]{1,0:T(4,128)S(1)}, s32[3,256]{1,0:T(4,128)S(1)}, u32[]{:S(2)}, u32[]{:S(2)}) collective-permute-start(s32[3,256]{1,0:T(4,128)S(1)} %bitcast.24), channel_id=1, source_target_pairs={{32,0},{64,32},{96,64},{128,96},{160,128},{192,160},{224,192},{33,... | collective-permute-start | bytes 9224 | tf_op jit(solution)/shard_map/ppermute | solution.py:594
where the time goes:
time: 162 us; the launch traced here: 160 us
  Pallas kernels  81.5 us (50%)
  starting transfers between devices  31.5 us (19%)
  blocking collectives  19.8 us (12%)
  waiting for transfers between devices  19.7 us (12%)
  local copies, waits for them, and re-layouts  7.08 us (4%)
    pallas_call x1, Pallas kernels, searched(): pl.pallas_call(transform_kernel, in_specs=vmem(6), out_specs=vmem(3), out...  48.2 us
    all_to_all x3, starting transfers between devices, exchanged(): lax.all_to_all(array, GRID_AXES, split_axis=0, concat_axis=0, tiled=True)  20.6 us
    all_to_all x1, blocking collectives, exchanged(): lax.all_to_all(array, GRID_AXES, split_axis=0, concat_axis=0, tiled=True)  19.8 us
    all_to_all x3, waiting for transfers between devices, exchanged(): lax.all_to_all(array, GRID_AXES, split_axis=0, concat_axis=0, tiled=True)  14.4 us
    ppermute x2, starting transfers between devices, passed_along(): return lax.ppermute(block, axis, route)  10.9 us
    pallas_call x1, Pallas kernels, corrected(): pl.pallas_call(project_kernel, grid=(2048 // lanes,), in_specs=[pl.BlockS...  8.81 us
    unnamed x32, local copies, waits for them, and re-layouts  7.08 us
    pallas_call x1, Pallas kernels, own_intersections(): pl.pallas_call(intersect_kernel, grid=(BANDS // some,), in_specs=[pl.Bloc...  6.77 us
  transfers between devices with their start and end apart: 5, of which 3 were waited for; matrix products, arithmetic and copies ran while one was open for 0% of the time, Pallas kernels for 7%

commit v1 on v0

--- a/solution.py
+++ b/solution.py
@@ -17,7 +17,10 @@
 PEERS = 32
 OWN = BLOCK // PEERS // 2
 HALF = BLOCK // 2
-PITCH = 2 * G
+PITCH = 2 * G + 1
+GROUP = 32
+MB = 16
+SU = 1
 ROWS = 136
 
 kinetic_scale = 0.01
@@ -184,9 +187,9 @@
 def transform_kernel(
     orb_ref, pot_ref, zf_ref, left_ref, left_inv_ref, zi_ref,
     out_ref, ritz_ref, dens_ref,
-    mid_ref, ham_ref, num_ref, den_ref,
+    mid_ref, ret_ref, ham_ref, num_ref, den_ref,
 ):
-    group = 2
+    group = GROUP
     rows = group * OWN * W
 
     def forward(i, carry):
@@ -200,42 +203,44 @@
         along_y = dot(left_ref[...], jnp.concatenate(parts, 1))
         for g in range(group * OWN):
             xx, tt = x + g // OWN, g % OWN
-            at = pl.multiple_of((tt * W + xx) * PITCH, 8)
+            at = (tt * W + xx) * PITCH
             mid_ref[pl.ds(at, 2 * G), :] = along_y[:, 128 * g : 128 * g + 128]
         return carry
 
     lax.fori_loop(0, W // group, forward, 0)
 
-    def space(m, carry):
+    def space(i, carry):
         parts = []
-        for tt in range(OWN):
-            base = tt * W * PITCH + m
+        for k in range(MB * OWN):
+            base = (k % OWN) * W * PITCH + i * MB + k // OWN
             parts.append(
                 jnp.concatenate(
                     [mid_ref[pl.ds(base + c * G, W, stride=PITCH), :] for c in range(2)], 0
                 ).astype(bf16)
             )
         in_space = dot(left_ref[...], jnp.concatenate(parts, 1))
-        at = pl.multiple_of(m * G, G)
-        potential = pot_ref[pl.ds(at, G), :]
-        potential = jnp.concatenate([potential, potential], 0)
-        density = jnp.zeros((2 * G, 128), f32)
         weighted = []
-        for tt in range(OWN):
-            one = in_space[:, 128 * tt : 128 * tt + 128]
-            density = density + one * one
-            weighted.append((one * potential).astype(bf16))
-        dens_ref[pl.ds(at, G), :] = (density[:G] + density[G:]) * (1.0 / BLOCK)
+        for mm in range(MB):
+            at = pl.multiple_of((i * MB + mm) * G, G)
+            potential = pot_ref[pl.ds(at, G), :]
+            potential = jnp.concatenate([potential, potential], 0)
+            density = jnp.zeros((2 * G, 128), f32)
+            for tt in range(OWN):
+                k = mm * OWN + tt
+                one = in_space[:, 128 * k : 128 * k + 128]
+                density = density + one * one
+                weighted.append((one * potential).astype(bf16))
+            dens_ref[pl.ds(at, G), :] = (density[:G] + density[G:]) * (1.0 / BLOCK)
         back = dot(left_inv_ref[...], jnp.concatenate(weighted, 1))
-        for tt in range(OWN):
-            base = tt * W * PITCH + m
+        for k in range(MB * OWN):
+            base = (k % OWN) * W * PITCH + i * MB + k // OWN
             for c in range(2):
-                mid_ref[pl.ds(base + c * G, W, stride=PITCH), :] = back[
-                    W * c : W * c + W, 128 * tt : 128 * tt + 128
+                ret_ref[pl.ds(base + c * G, W, stride=PITCH), :] = back[
+                    W * c : W * c + W, 128 * k : 128 * k + 128
                 ]
         return carry
 
-    lax.fori_loop(0, G, space, 0)
+    lax.fori_loop(0, G // MB, space, 0, unroll=SU)
 
     lane = iota((W, 128), 1)
     wave_y = iota((W, 128), 0) - W // 2
@@ -254,8 +259,8 @@
         parts = []
         for g in range(group * OWN):
             xx, tt = x + g // OWN, g % OWN
-            at = pl.multiple_of((tt * W + xx) * PITCH, 8)
-            parts.append(mid_ref[pl.ds(at, 2 * G), :].astype(bf16))
+            at = (tt * W + xx) * PITCH
+            parts.append(ret_ref[pl.ds(at, 2 * G), :].astype(bf16))
         back_y = dot(left_inv_ref[...], jnp.concatenate(parts, 1)).astype(bf16)
         parts = []
         for g in range(group * OWN):
@@ -317,6 +322,7 @@
             jax.ShapeDtypeStruct((G * G, 128), f32),
         ],
         scratch_shapes=[
+            pltpu.VMEM((OWN * W * PITCH, 128), f32),
             pltpu.VMEM((OWN * W * PITCH, 128), f32),
             pltpu.VMEM((W * OWN * W, 128), f32),
             pltpu.VMEM((OWN * W, 128), f32),

time: 162 us -> 124 us (0.77)
  Pallas kernels: 81.5 us -> 42.8 us
    pallas_call x1, Pallas kernels: 48.2 us -> 9.51 us  [searched(): pl.pallas_call(transform_kernel, in_specs=vmem(6), out_specs=vmem(3), out...]
  transfers between devices with their start and end apart: 5 -> 5, of which waited for: 3 -> 3; matrix products, arithmetic and copies ran while one was open for 0% -> 0% of each run, Pallas kernels for 7% -> 10%
where the time goes in v1:
time: 124 us; the launch traced here: 122 us
  Pallas kernels  42.8 us (35%)
  starting transfers between devices  31.5 us (25%)
  blocking collectives  19.8 us (16%)
  waiting for transfers between devices  19.7 us (16%)
  local copies, waits for them, and re-layouts  7.08 us (6%)
    all_to_all x3, starting transfers between devices, exchanged(): lax.all_to_all(array, GRID_AXES, split_axis=0, concat_axis=0, tiled=True)  20.6 us
    all_to_all x1, blocking collectives, exchanged(): lax.all_to_all(array, GRID_AXES, split_axis=0, concat_axis=0, tiled=True)  19.8 us
    all_to_all x3, waiting for transfers between devices, exchanged(): lax.all_to_all(array, GRID_AXES, split_axis=0, concat_axis=0, tiled=True)  14.4 us
    ppermute x2, starting transfers between devices, passed_along(): return lax.ppermute(block, axis, route)  10.9 us
    pallas_call x1, Pallas kernels, searched(): pl.pallas_call(transform_kernel, in_specs=vmem(6), out_specs=vmem(3), out...  9.51 us
    pallas_call x1, Pallas kernels, corrected(): pl.pallas_call(project_kernel, grid=(2048 // lanes,), in_specs=[pl.BlockS...  8.81 us
    unnamed x32, local copies, waits for them, and re-layouts  7.08 us
    pallas_call x1, Pallas kernels, own_intersections(): pl.pallas_call(intersect_kernel, grid=(BANDS // some,), in_specs=[pl.Bloc...  6.77 us
  transfers between devices with their start and end apart: 5, of which 3 were waited for; matrix products, arithmetic and copies ran while one was open for 0% of the time, Pallas kernels for 10%

profile of v1, /device:TPU:67, one launch (start us, length us, event | category | flops | bytes accessed | tf_op | source)
XLA Modules:
  0.0 121.7 jit_solution(15808317423244382375)
XLA Ops:
  0.6 0.0 copy-start
  0.6 2.2 %copy-done = bf16[1,1024,1,2048]{3,1,2,0:T(8,128)(2,1)S(1)} copy-done((bf16[1,1024,1,2048]{3,1,2,0:T(8,128)(2,1)S(1)}, bf16[1,1024,1,2048]{3,1,2,0:T(8,128)(2,1)}, u32[]{:S(2)}) %copy-start) | copy-done | bytes 4194328
  2.8 0.0 copy-start.3
  2.8 1.0 copy-done.3
  3.9 0.0 copy-start.5
  3.9 0.9 copy-done.5
  4.8 4.9 %orbitals.1 = bf16[4096,128]{1,0:T(8,128)(2,1)} custom-call(bf16[1024,256]{1,0:T(8,128)(2,1)S(1)} %bitcast.20, bf16[1024,2048]{1,0:T(8,128)(2,1)S(1)} %bitcast.16, bf16[256,256]{1,0:T(8,128)(2,1)S(1)} %copy-done.5), custom_call_target="tpu_custom_call" | custom-call | tf_op jit(solution)/shard_map/orbitals/pallas_call | solution.py:120
  9.6 0.0 copy-start.14
  9.6 0.0 copy-start.12
  9.6 0.0 copy-start.13
  9.6 8.5 %all-to-all-start = ((bf16[32,128,128]{2,1,0:T(8,128)(2,1)}), bf16[32,128,128]{2,1,0:T(8,128)(2,1)S(1)}, u32[]{:S(2)}, u32[]{:S(2)}) async-start(bf16[32,128,128]{2,1,0:T(8,128)(2,1)} %bitcast.3), calls=%async_computation | async-start | bytes 2097152 | tf_op jit(solution)/shard_map/all_to_all | solution.py:594
  18.2 0.0 copy-done.14
  18.2 0.0 copy-start.6
  18.2 0.0 copy-start.7
  18.2 0.0 copy-start.8
  18.2 0.0 copy-start.9
  18.2 0.0 copy-done.12
  18.3 0.0 copy-done.13
  18.3 5.9 %potential.1.pot_ref = f32[4096,128]{1,0:T(8,128)S(1)} custom-call(f32[4]{0:T(128)S(1)} %copy-done.13, s32[3,256]{1,0:T(4,128)S(1)} %bitcast.21, s32[1,256]{1,0:T(1,128)S(1)} %bitcast.26), custom_call_target="tpu_custom_call" | custom-call | tf_op jit(solution)/shard_map/potential/pallas_call | solution.py:176
  24.2 1.3 %copy-done.1 = f32[4096,128]{1,0:T(8,128)} copy-done((f32[4096,128]{1,0:T(8,128)}, f32[4096,128]{1,0:T(8,128)S(1)}, u32[]{:S(2)}) %copy-start.1) | copy-done | bytes 2097176
  25.6 6.6 %all-to-all-done = bf16[32,128,128]{2,1,0:T(8,128)(2,1)S(1)} async-done(((bf16[32,128,128]{2,1,0:T(8,128)(2,1)}), bf16[32,128,128]{2,1,0:T(8,128)(2,1)S(1)}, u32[]{:S(2)}, u32[]{:S(2)}) %all-to-all-start) | async-done | bytes 1048608 | tf_op jit(solution)/shard_map/all_to_all | solution.py:594
  32.1 0.0 copy-done.6
  32.1 0.0 copy-done.7
  32.1 0.0 copy-done.8
  32.1 0.0 copy-done.9
  32.1 9.5 %transform.1 = (bf16[4096,128]{1,0:T(8,128)(2,1)S(1)}, f32[8,128]{1,0:T(8,128)S(1)}, f32[4096,128]{1,0:T(8,128)S(1)}) custom-call(bf16[4096,128]{1,0:T(8,128)(2,1)S(1)} %bitcast.17, f32[4096,128]{1,0:T(8,128)} %copy-done.1, bf16[128,256]{1,0:T(8,128)(2,1)S(1)} %copy-done.6, bf16[128,64]{1,0:T(8,128)(2,1)S(1)} %copy-done.8, bf16[64,128]{1,0:T(8,128)(2,1)S(1)} %copy-done.9, ...), custom_call_target="tpu_custom_call" | custom-call | tf_op jit(solution)/shard_map/transform/pallas_call | solution.py:315
  41.6 0.0 copy-start.2
  41.7 1.0 copy-done.2
  42.6 6.6 %all-to-all-start.1 = ((bf16[32,128,128]{2,1,0:T(8,128)(2,1)}), bf16[32,128,128]{2,1,0:T(8,128)(2,1)S(1)}, u32[]{:S(2)}, u32[]{:S(2)}) async-start(bf16[32,128,128]{2,1,0:T(8,128)(2,1)} %bitcast.19), calls=%async_computation.1 | async-start | bytes 2097152 | tf_op jit(solution)/shard_map/all_to_all | solution.py:594
  49.2 0.0 copy-start.4
  49.2 5.8 %force.1.extra_ref = bf16[32,8,128]{2,1,0:T(8,128)(2,1)S(1)} custom-call(f32[4]{0:T(128)S(1)} %copy-done.13, f32[4096,128]{1,0:T(8,128)S(1)} %get-tuple-element.14.dens_ref, s32[3,256]{1,0:T(4,128)S(1)} %bitcast.22, s32[1,256]{1,0:T(1,128)S(1)} %bitcast.27, f32[8,128]{1,0:T(8,128)S(1)} %get-tuple-element.15.ritz_ref), custom_call_target="tpu_custom_call" | custom-call | tf_op jit(solution)/shard_map/force/pallas_call | solution.py:387
  55.0 7.8 %all-to-all-done.1 = bf16[32,128,128]{2,1,0:T(8,128)(2,1)S(1)} async-done(((bf16[32,128,128]{2,1,0:T(8,128)(2,1)}), bf16[32,128,128]{2,1,0:T(8,128)(2,1)S(1)}, u32[]{:S(2)}, u32[]{:S(2)}) %all-to-all-start.1) | async-done | bytes 1048608 | tf_op jit(solution)/shard_map/all_to_all | solution.py:594
  62.8 0.0 copy-done.4
  62.8 6.8 %intersect.1 = (bf16[32,136,128]{2,1,0:T(8,128)(2,1)S(1)}, bf16[256,2048]{1,0:T(8,128)(2,1)S(1)}) custom-call(bf16[4096,128]{1,0:T(8,128)(2,1)S(1)} %bitcast.18, bf16[256,512]{1,0:T(8,128)(2,1)S(1)} %copy-done.4, bf16[1024,2048]{1,0:T(8,128)(2,1)} %bitcast.14, bf16[32,8,128]{2,1,0:T(8,128)(2,1)S(1)} %force.1.extra_ref), custom_call_target="tpu_custom_call" | custom-call | tf_op jit(solution)/shard_map/intersect/pallas_call | solution.py:432
  69.5 19.8 %all_to_all.20.in_ref.first_ref = bf16[32,136,128]{2,1,0:T(8,128)(2,1)S(1)} all-to-all(bf16[32,136,128]{2,1,0:T(8,128)(2,1)S(1)} %get-tuple-element.16), channel_id=1, replica_groups=mesh['img'=8,'band'=8,'pw'=4] {'band','pw'}, dimensions={0} | all-to-all | bytes 2228224 | tf_op jit(solution)/shard_map/all_to_all | solution.py:594
  89.3 1.2 %total.1 = bf16[32,136,128]{2,1,0:T(8,128)(2,1)} custom-call(bf16[32,136,128]{2,1,0:T(8,128)(2,1)S(1)} %all_to_all.20.in_ref.first_ref), custom_call_target="tpu_custom_call" | custom-call | tf_op jit(solution)/shard_map/total/pallas_call | solution.py:480
  90.6 0.0 copy-start.10
  90.6 5.5 %all-to-all-start.3 = ((bf16[32,136,128]{2,1,0:T(8,128)(2,1)}), bf16[32,136,128]{2,1,0:T(8,128)(2,1)S(1)}, u32[]{:S(2)}, u32[]{:S(2)}) async-start(bf16[32,136,128]{2,1,0:T(8,128)(2,1)} %total.1), calls=%async_computation.3 | async-start | bytes 2228224 | tf_op jit(solution)/shard_map/all_to_all | solution.py:594
  96.0 9.0 %collective-permute-start = (s32[3,256]{1,0:T(4,128)S(1)}, s32[3,256]{1,0:T(4,128)S(1)}, u32[]{:S(2)}, u32[]{:S(2)}) collective-permute-start(s32[3,256]{1,0:T(4,128)S(1)} %bitcast.23), channel_id=1, source_target_pairs={{0,32},{32,64},{64,96},{96,128},{128,160},{160,192},{192,224},{1,3... | collective-permute-start | bytes 9224 | tf_op jit(solution)/shard_map/ppermute | solution.py:600
  105.0 1.9 %collective-permute-start.1 = (s32[3,256]{1,0:T(4,128)S(1)}, s32[3,256]{1,0:T(4,128)S(1)}, u32[]{:S(2)}, u32[]{:S(2)}) collective-permute-start(s32[3,256]{1,0:T(4,128)S(1)} %bitcast.24), channel_id=1, source_target_pairs={{32,0},{64,32},{96,64},{128,96},{160,128},{192,160},{224,192},{33,... | collective-permute-start | bytes 9224 | tf_op jit(solution)/shard_map/ppermute | solution.py:600
  106.9 0.1 pad_add_fusion.image_ref
  107.0 0.0 collective-permute-done.before_ref
  107.0 5.3 %collective-permute-done.1.after_ref = s32[3,256]{1,0:T(4,128)S(1)} collective-permute-done((s32[3,256]{1,0:T(4,128)S(1)}, s32[3,256]{1,0:T(4,128)S(1)}, u32[]{:S(2)}, u32[]{:S(2)}) %collective-permute-start.1) | collective-permute-done | bytes 3104 | tf_op jit(solution)/shard_map/ppermute | solution.py:600
  112.3 0.0 all-to-all-done.3.whole_ref
  112.3 0.0 copy-done.10
  112.3 0.0 copy-done.11
  112.4 8.8 %project.1 = (bf16[256,2048]{1,0:T(8,128)(2,1)}, f32[1,256]{1,0:T(1,128)}, f32[3,256]{1,0:T(4,128)S(1)}, f32[1,1]{1,0:T(1,128)}) custom-call(s32[2]{0:T(128)S(1)} %pad_add_fusion.image_ref, bf16[32,136,128]{2,1,0:T(8,128)(2,1)S(1)} %all-to-all-done.3.whole_ref, bf16[32,136,128]{2,1,0:T(8,128)(2,1)S(1)} %all_to_all.20.in_ref.first_ref, ...), custom_call_target="tpu_custom_call" | custom-call | tf_op jit(solution)/shard_map/project/pallas_call | solution.py:564
  121.2 0.6 copy.17
  (3 shorter events, 0.0 us)
Async XLA Ops:
  0.6 2.2 %copy-start = (bf16[1,1024,1,2048]{3,1,2,0:T(8,128)(2,1)S(1)}, bf16[1,1024,1,2048]{3,1,2,0:T(8,128)(2,1)}, u32[]{:S(2)}) copy-start(bf16[1,1024,1,2048]{3,1,2,0:T(8,128)(2,1)} %param.13) | copy-start | bytes 12582916
  2.8 1.0 copy-start.3
  3.9 0.9 copy-start.5
  9.6 8.6 %copy-start.14 = (s32[1,3,256]{2,0,1:T(1,128)S(1)}, s32[1,3,256]{2,0,1:T(1,128)}, u32[]{:S(2)}) copy-start(s32[1,3,256]{2,0,1:T(1,128)} %param.15) | copy-start | bytes 9220
  9.6 8.6 %copy-start.12 = (s32[256]{0:T(256)S(1)}, s32[256]{0:T(256)}, u32[]{:S(2)}) copy-start(s32[256]{0:T(256)} %param.18) | copy-start | bytes 3076
  9.6 8.6 %copy-start.13 = (f32[4]{0:T(128)S(1)}, f32[4]{0:T(128)}, u32[]{:S(2)}) copy-start(f32[4]{0:T(128)} %depth_ref.3) | copy-start | bytes 52
  9.6 22.5 %all-to-all-start = ((bf16[32,128,128]{2,1,0:T(8,128)(2,1)}), bf16[32,128,128]{2,1,0:T(8,128)(2,1)S(1)}, u32[]{:S(2)}, u32[]{:S(2)}) async-start(bf16[32,128,128]{2,1,0:T(8,128)(2,1)} %bitcast.3), calls=%async_computation | async-start | bytes 2097152 | tf_op jit(solution)/shard_map/all_to_all | solution.py:594
  18.2 13.9 %copy-start.6 = (bf16[128,256]{1,0:T(8,128)(2,1)S(1)}, bf16[128,256]{1,0:T(8,128)(2,1)}, u32[]{:S(2)}) copy-start(bf16[128,256]{1,0:T(8,128)(2,1)} %constant.21.clone.zf_ref) | copy-start | bytes 196612
  18.2 13.9 %copy-start.7 = (bf16[256,128]{1,0:T(8,128)(2,1)S(1)}, bf16[256,128]{1,0:T(8,128)(2,1)}, u32[]{:S(2)}) copy-start(bf16[256,128]{1,0:T(8,128)(2,1)} %constant.24.clone.zi_ref) | copy-start | bytes 196612
  18.2 13.9 %copy-start.8 = (bf16[128,64]{1,0:T(8,128)(2,1)S(1)}, bf16[128,64]{1,0:T(8,128)(2,1)}, u32[]{:S(2)}) copy-start(bf16[128,64]{1,0:T(8,128)(2,1)} %constant.22.clone.left_ref) | copy-start | bytes 49156
  18.2 13.9 %copy-start.9 = (bf16[64,128]{1,0:T(8,128)(2,1)S(1)}, bf16[64,128]{1,0:T(8,128)(2,1)}, u32[]{:S(2)}) copy-start(bf16[64,128]{1,0:T(8,128)(2,1)} %constant.23.clone.left_inv_ref) | copy-start | bytes 49156
  24.2 1.4 %copy-start.1 = (f32[4096,128]{1,0:T(8,128)}, f32[4096,128]{1,0:T(8,128)S(1)}, u32[]{:S(2)}) copy-start(f32[4096,128]{1,0:T(8,128)S(1)} %potential.1.pot_ref) | copy-start | bytes 6291460
  41.6 1.0 copy-start.2
  42.6 20.1 %all-to-all-start.1 = ((bf16[32,128,128]{2,1,0:T(8,128)(2,1)}), bf16[32,128,128]{2,1,0:T(8,128)(2,1)S(1)}, u32[]{:S(2)}, u32[]{:S(2)}) async-start(bf16[32,128,128]{2,1,0:T(8,128)(2,1)} %bitcast.19), calls=%async_computation.1 | async-start | bytes 2097152 | tf_op jit(solution)/shard_map/all_to_all | solution.py:594
  49.2 13.6 %copy-start.4 = (bf16[256,512]{1,0:T(8,128)(2,1)S(1)}, bf16[256,512]{1,0:T(8,128)(2,1)}, u32[]{:S(2)}) copy-start(bf16[256,512]{1,0:T(8,128)(2,1)} %constant.25.clone.unpack_ref) | copy-start | bytes 786436
  90.6 21.8 %copy-start.10 = (s32[3,256]{1,0:T(4,128)S(1)}, s32[3,256]{1,0:T(4,128)}, u32[]{:S(2)}) copy-start(s32[3,256]{1,0:T(4,128)} %start_ref.1) | copy-start | bytes 9220
  90.6 21.8 %copy-start.11 = (s32[3,256]{1,0:T(4,128)S(1)}, s32[3,256]{1,0:T(4,128)}, u32[]{:S(2)}) copy-start(s32[3,256]{1,0:T(4,128)} %end_ref.1) | copy-start | bytes 9220
  90.6 21.8 %all-to-all-start.3 = ((bf16[32,136,128]{2,1,0:T(8,128)(2,1)}), bf16[32,136,128]{2,1,0:T(8,128)(2,1)S(1)}, u32[]{:S(2)}, u32[]{:S(2)}) async-start(bf16[32,136,128]{2,1,0:T(8,128)(2,1)} %total.1), calls=%async_computation.3 | async-start | bytes 2228224 | tf_op jit(solution)/shard_map/all_to_all | solution.py:594
  96.0 11.0 %collective-permute-start = (s32[3,256]{1,0:T(4,128)S(1)}, s32[3,256]{1,0:T(4,128)S(1)}, u32[]{:S(2)}, u32[]{:S(2)}) collective-permute-start(s32[3,256]{1,0:T(4,128)S(1)} %bitcast.23), channel_id=1, source_target_pairs={{0,32},{32,64},{64,96},{96,128},{128,160},{160,192},{192,224},{1,3... | collective-permute-start | bytes 9224 | tf_op jit(solution)/shard_map/ppermute | solution.py:600
  105.0 7.3 %collective-permute-start.1 = (s32[3,256]{1,0:T(4,128)S(1)}, s32[3,256]{1,0:T(4,128)S(1)}, u32[]{:S(2)}, u32[]{:S(2)}) collective-permute-start(s32[3,256]{1,0:T(4,128)S(1)} %bitcast.24), channel_id=1, source_target_pairs={{32,0},{64,32},{96,64},{128,96},{160,128},{192,160},{224,192},{33,... | collective-permute-start | bytes 9224 | tf_op jit(solution)/shard_map/ppermute | solution.py:600

commit v2 on v1

--- a/solution.py
+++ b/solution.py
@@ -22,6 +22,9 @@
 MB = 16
 SU = 1
 ROWS = 136
+CHUNKS = 2
+FETCHES = 2
+LINE = W + 1
 
 kinetic_scale = 0.01
 sigma_cells = 3.0
@@ -54,23 +57,6 @@
     return [np.asarray(a, dtype=bf16) for a in (z_fwd, left, left_inv, z_inv)]
 
 
-def host_pack():
-    move = np.zeros((2, 2, 64, 2, 2, 64), np.float32)
-    for h in range(2):
-        for y in range(2):
-            move[h, y, np.arange(64), y, h, np.arange(64)] = 1.0
-    return move.reshape(256, 256)
-
-
-def host_unpack():
-    plain = host_pack().T
-    e = np.arange(64)
-    turn = np.zeros((64, 64), np.float32)
-    turn[(e + 32) % 64, e] = np.where(e < 32, 1.0, -1.0)
-    whole = np.kron(np.eye(4, dtype=np.float32), turn)
-    return np.concatenate([plain, plain @ whole], 1)
-
-
 def split_two(value):
     high = value.astype(bf16)
     return high, (value - high.astype(f32)).astype(bf16)
@@ -95,42 +81,80 @@
     return lax.broadcasted_iota(jnp.int32, shape, dim)
 
 
-def orbitals_kernel(rot_ref, coeff_ref, pack_ref, out_ref, wide_ref):
-    step = pl.program_id(0)
-    both = lax.dot_general(
-        rot_ref[...], coeff_ref[...], (((0,), (0,)), ((), ())), preferred_element_type=f32
-    ).astype(bf16)
-    lanes = both.shape[1]
-    for j in range(lanes // 128):
-        at = slice(128 * j, 128 * j + 128)
-        pair = jnp.concatenate([both[:HALF, at], both[HALF:, at]], 1)
-        moved = dot(pair, pack_ref[...])
-        y = step * (lanes // 64) + 2 * j
-        wide_ref[pl.ds(y, HALF, stride=W), :] = moved[:, :128]
-        wide_ref[pl.ds(y + 1, HALF, stride=W), :] = moved[:, 128:]
-
-    @pl.when(step == pl.num_programs(0) - 1)
-    def _():
-        out_ref[...] = wide_ref[...].astype(bf16)
+def orbitals_kernel(
+    rot_hbm, coeff_hbm, out_hbm, coeff_ref, rot_ref, turned_ref, wide_ref, out_ref, sems
+):
+    lanes = 2048 // CHUNKS
+
+    def fetch(k):
+        at = pl.ds(k * lanes, lanes)
+        return pltpu.make_async_copy(coeff_hbm.at[:, at], coeff_ref.at[:, at], sems.at[k])
+
+    turned = pltpu.make_async_copy(rot_hbm, rot_ref, sems.at[CHUNKS])
+    turned.start()
+    for k in range(CHUNKS):
+        fetch(k).start()
+    source, target = iota((256, 256), 0), iota((256, 256), 1)
+    same = (source & 63) == (target & 63)
+    same &= (source >> 7) == ((target >> 6) & 1)
+    same &= ((source >> 6) & 1) == (target >> 7)
+    pack = jnp.where(same, 1.0, 0.0).astype(bf16)
+    turned.wait()
+    turned_ref[...] = rot_ref[...].T
+    for k in range(CHUNKS):
+        fetch(k).wait()
+        both = dot(turned_ref[...], coeff_ref[:, k * lanes : (k + 1) * lanes]).astype(bf16)
+        for j in range(lanes // 128):
+            at = slice(128 * j, 128 * j + 128)
+            pair = jnp.concatenate([both[:HALF, at], both[HALF:, at]], 1)
+            moved = dot(pair, pack)
+            y = k * (lanes // 64) + 2 * j
+            wide_ref[pl.ds(y, HALF, stride=LINE), :] = moved[:, :128]
+            wide_ref[pl.ds(y + 1, HALF, stride=LINE), :] = moved[:, 128:]
+    parts = 4
+    rows = HALF * W // parts
+
+    def send(k):
+        at = pl.ds(k * rows, rows)
+        return pltpu.make_async_copy(out_ref.at[at], out_hbm.at[at], sems.at[CHUNKS + 1 + k])
+
+    for k in range(parts):
+        for t in range(k * HALF // parts, (k + 1) * HALF // parts):
+            out_ref[t * W : t * W + W, :] = wide_ref[t * LINE : t * LINE + W, :].astype(bf16)
+        send(k).start()
+    for k in range(parts):
+        send(k).wait()
 
 
 def own_orbitals(rotation, coeff):
-    lanes = 512
-    full = lambda k: (0, 0)
     return pl.pallas_call(
         orbitals_kernel,
-        grid=(2048 // lanes,),
-        in_specs=[
-            pl.BlockSpec((BANDS, BLOCK), full),
-            pl.BlockSpec((BANDS, lanes), lambda k: (0, k)),
-            pl.BlockSpec((256, 256), full),
-        ],
-        out_specs=pl.BlockSpec((HALF * W, 128), full),
-        out_shape=jax.ShapeDtypeStruct((HALF * W, 128), bf16),
-        scratch_shapes=[pltpu.VMEM((HALF * W, 128), f32)],
-        compiler_params=pltpu.CompilerParams(vmem_limit_bytes=40 << 20),
+        in_specs=hbm(2),
+        out_specs=hbm(1)[0],
+        out_shape=pltpu.HBM((HALF * W, 128), bf16),
+        scratch_shapes=[
+            pltpu.VMEM((BANDS, 2048), bf16),
+            pltpu.VMEM((BANDS, BLOCK), bf16),
+            pltpu.VMEM((BLOCK, BANDS), bf16),
+            pltpu.VMEM((HALF * LINE, 128), f32),
+            pltpu.VMEM((HALF * W, 128), bf16),
+            pltpu.SemaphoreType.DMA((CHUNKS + 5,)),
+        ],
+        compiler_params=pltpu.CompilerParams(vmem_limit_bytes=20 << 20),
         name="orbitals",
-    )(rotation, coeff, jnp.asarray(host_pack(), bf16))
+    )(in_hbm(rotation), in_hbm(coeff))
+
+
+def in_hbm(array):
+    return pltpu.with_memory_space_constraint(array, pltpu.HBM)
+
+
+def hbm(count):
+    return [pl.BlockSpec(memory_space=pltpu.HBM)] * count
+
+
+def vmem(count):
+    return [pl.BlockSpec(memory_space=pltpu.VMEM)] * count
 
 
 def gaussian(position, rows):
@@ -168,10 +192,6 @@
     lax.fori_loop(0, G // per, some, 0)
 
 
-def vmem(count):
-    return [pl.BlockSpec(memory_space=pltpu.VMEM)] * count
-
-
 def grid_potential(depth, pos, species):
     return pl.pallas_call(
         potential_kernel,
@@ -179,15 +199,15 @@
         out_specs=vmem(1)[0],
         out_shape=jax.ShapeDtypeStruct((G * G, 128), f32),
         scratch_shapes=[pltpu.VMEM((G, 256), f32)],
-        compiler_params=pltpu.CompilerParams(vmem_limit_bytes=40 << 20),
+        compiler_params=pltpu.CompilerParams(vmem_limit_bytes=10 << 20),
         name="potential",
     )(depth, pos, species)
 
 
 def transform_kernel(
     orb_ref, pot_ref, zf_ref, left_ref, left_inv_ref, zi_ref,
-    out_ref, ritz_ref, dens_ref,
-    mid_ref, ret_ref, ham_ref, num_ref, den_ref,
+    out_hbm, dens_hbm, ritz_ref,
+    mid_ref, ham_ref, num_ref, den_ref, dens_ref, out_ref, sems,
 ):
     group = GROUP
     rows = group * OWN * W
@@ -235,12 +255,14 @@
         for k in range(MB * OWN):
             base = (k % OWN) * W * PITCH + i * MB + k // OWN
             for c in range(2):
-                ret_ref[pl.ds(base + c * G, W, stride=PITCH), :] = back[
+                mid_ref[pl.ds(base + c * G, W, stride=PITCH), :] = back[
                     W * c : W * c + W, 128 * k : 128 * k + 128
                 ]
         return carry
 
     lax.fori_loop(0, G // MB, space, 0, unroll=SU)
+    keep = pltpu.make_async_copy(dens_ref, dens_hbm, sems.at[4])
+    keep.start()
 
     lane = iota((W, 128), 1)
     wave_y = iota((W, 128), 0) - W // 2
@@ -260,7 +282,7 @@
         for g in range(group * OWN):
             xx, tt = x + g // OWN, g % OWN
             at = (tt * W + xx) * PITCH
-            parts.append(ret_ref[pl.ds(at, 2 * G), :].astype(bf16))
+            parts.append(mid_ref[pl.ds(at, 2 * G), :].astype(bf16))
         back_y = dot(left_inv_ref[...], jnp.concatenate(parts, 1)).astype(bf16)
         parts = []
         for g in range(group * OWN):
@@ -297,17 +319,26 @@
         ritz.append(jnp.where(low, halves[0], halves[1]))
     ritz_ref[...] = jnp.broadcast_to(ritz_row, (8, 128))
 
-    def finish(x, carry):
+    parts = 4
+    rows = W * OWN * W // parts
+
+    def send(k):
+        at = pl.ds(k * rows, rows)
+        return pltpu.make_async_copy(out_ref.at[at], out_hbm.at[at], sems.at[k])
+
+    for x in range(W):
         kin = kinetic(x)
         scale = 1.0 / (1.0 + kin)
         for tt in range(OWN):
-            at = pl.multiple_of((x * OWN + tt) * W, W)
-            orbital = orb_ref[pl.ds(at, W), :].astype(f32)
-            residual = ham_ref[pl.ds(at, W), :] - ritz[tt] * orbital
-            out_ref[pl.ds(at, W), :] = (residual * scale).astype(bf16)
-        return carry
-
-    lax.fori_loop(0, W, finish, 0, unroll=2)
+            at = pl.ds((x * OWN + tt) * W, W)
+            orbital = orb_ref[at, :].astype(f32)
+            residual = ham_ref[at, :] - ritz[tt] * orbital
+            out_ref[at, :] = (residual * scale).astype(bf16)
+        if (x + 1) % (W // parts) == 0:
+            send(x // (W // parts)).start()
+    for k in range(parts):
+        send(k).wait()
+    keep.wait()
 
 
 def searched(orbitals, potential):
@@ -315,20 +346,22 @@
     return pl.pallas_call(
         transform_kernel,
         in_specs=vmem(6),
-        out_specs=vmem(3),
+        out_specs=hbm(2) + vmem(1),
         out_shape=[
-            jax.ShapeDtypeStruct((W * OWN * W, 128), bf16),
+            pltpu.HBM((W * OWN * W, 128), bf16),
+            pltpu.HBM((G * G, 128), f32),
             jax.ShapeDtypeStruct((8, 128), f32),
-            jax.ShapeDtypeStruct((G * G, 128), f32),
         ],
         scratch_shapes=[
-            pltpu.VMEM((OWN * W * PITCH, 128), f32),
             pltpu.VMEM((OWN * W * PITCH, 128), f32),
             pltpu.VMEM((W * OWN * W, 128), f32),
             pltpu.VMEM((OWN * W, 128), f32),
             pltpu.VMEM((OWN * W, 128), f32),
-        ],
-        compiler_params=pltpu.CompilerParams(vmem_limit_bytes=48 << 20),
+            pltpu.VMEM((G * G, 128), f32),
+            pltpu.VMEM((W * OWN * W, 128), bf16),
+            pltpu.SemaphoreType.DMA((5,)),
+        ],
+        compiler_params=pltpu.CompilerParams(vmem_limit_bytes=30 << 20),
         name="transform",
     )(orbitals, potential, z_fwd, left, left_inv, z_inv)
 
@@ -394,65 +427,71 @@
             pltpu.VMEM((G, 256), f32),
             pltpu.VMEM((PEERS * 8, 128), f32),
         ],
-        compiler_params=pltpu.CompilerParams(vmem_limit_bytes=40 << 20),
+        compiler_params=pltpu.CompilerParams(vmem_limit_bytes=10 << 20),
         name="force",
     )(depth, density, pos, species, ritz)
 
 
 def intersect_kernel(
-    search_ref, unpack_ref, coeff_ref, extra_ref, out_ref, flat_ref, wide_ref, pair_ref
+    search_ref, extra_ref, coeff_hbm, out_ref, flat_ref,
+    coeff_ref, wide_ref, pair_ref, sems,
 ):
-    step = pl.program_id(0)
-
-    @pl.when(step == 0)
-    def _():
-        wide_ref[...] = search_ref[...].astype(f32)
-        for j in range(W // 2):
-            even = wide_ref[pl.ds(2 * j, HALF, stride=W), :]
-            odd = wide_ref[pl.ds(2 * j + 1, HALF, stride=W), :]
-            moved = dot(jnp.concatenate([even, odd], 1).astype(bf16), unpack_ref[...]).astype(bf16)
-            at = slice(128 * j, 128 * j + 128)
-            for q in range(4):
-                pair_ref[HALF * q : HALF * q + HALF, at] = moved[:, 128 * q : 128 * q + 128]
-        flat_ref[...] = pair_ref[: 2 * HALF, :]
-        out_ref[:, 128:, :] = extra_ref[...]
-
-    part = (dot_nt(pair_ref[...], coeff_ref[...]) * (1.0 / NPW)).astype(bf16)
-    tiles = coeff_ref.shape[0] // 128
-    for j in range(tiles):
-        out_ref[:, pl.ds(pl.multiple_of((step * tiles + j) * 16, 16), 16), :] = part[
-            :, 128 * j : 128 * j + 128
-        ].reshape(PEERS, 16, 128)
+    bands = BANDS // FETCHES
+
+    def fetch(k):
+        at = pl.ds(k * bands, bands)
+        return pltpu.make_async_copy(coeff_hbm.at[at], coeff_ref.at[at], sems.at[k])
+
+    for k in range(FETCHES):
+        fetch(k).start()
+    source, target = iota((256, 512), 0), iota((256, 512), 1)
+    part, element = target >> 7, target & 63
+    turned = part >> 1
+    same = (source & 63) == (element ^ (turned * 32))
+    same &= (source >> 7) == ((target >> 6) & 1)
+    same &= ((source >> 6) & 1) == (part & 1)
+    sign = jnp.where((turned == 1) & (element >= 32), -1.0, 1.0)
+    unpack = jnp.where(same, sign, 0.0).astype(bf16)
+    for t in range(HALF):
+        wide_ref[t * LINE : t * LINE + W, :] = search_ref[t * W : t * W + W, :].astype(f32)
+    out_ref[:, 128:, :] = extra_ref[...]
+    for j in range(W // 2):
+        even = wide_ref[pl.ds(2 * j, HALF, stride=LINE), :]
+        odd = wide_ref[pl.ds(2 * j + 1, HALF, stride=LINE), :]
+        moved = dot(jnp.concatenate([even, odd], 1).astype(bf16), unpack).astype(bf16)
+        at = slice(128 * j, 128 * j + 128)
+        for q in range(4):
+            piece = moved[:, 128 * q : 128 * q + 128]
+            pair_ref[HALF * q : HALF * q + HALF, at] = piece
+            if q < 2:
+                flat_ref[HALF * q : HALF * q + HALF, at] = piece
+    for k in range(FETCHES):
+        fetch(k).wait()
+        part = dot_nt(pair_ref[...], coeff_ref[bands * k : bands * k + bands, :])
+        part = (part * (1.0 / NPW)).astype(bf16)
+        for j in range(bands // 128):
+            at = 16 * (k * bands // 128 + j)
+            out_ref[:, at : at + 16, :] = part[:, 128 * j : 128 * j + 128].reshape(PEERS, 16, 128)
 
 
 def own_intersections(search, coeff, extra):
-    some = 256
-    full2 = lambda k: (0, 0)
-    full3 = lambda k: (0, 0, 0)
     return pl.pallas_call(
         intersect_kernel,
-        grid=(BANDS // some,),
-        in_specs=[
-            pl.BlockSpec((HALF * W, 128), full2),
-            pl.BlockSpec((256, 512), full2),
-            pl.BlockSpec((some, 2048), lambda k: (k, 0)),
-            pl.BlockSpec((PEERS, 8, 128), full3),
-        ],
-        out_specs=[
-            pl.BlockSpec((PEERS, ROWS, 128), full3),
-            pl.BlockSpec((BLOCK, 2048), full2),
-        ],
+        in_specs=vmem(2) + hbm(1),
+        out_specs=vmem(2),
         out_shape=[
             jax.ShapeDtypeStruct((PEERS, ROWS, 128), bf16),
             jax.ShapeDtypeStruct((BLOCK, 2048), bf16),
         ],
         scratch_shapes=[
-            pltpu.VMEM((HALF * W, 128), f32),
+            pltpu.VMEM((BANDS, 2048), bf16),
+            pltpu.VMEM((HALF * LINE, 128), f32),
             pltpu.VMEM((2 * BLOCK, 2048), bf16),
-        ],
-        compiler_params=pltpu.CompilerParams(vmem_limit_bytes=48 << 20),
+            pltpu.SemaphoreType.DMA((FETCHES,)),
+        ],
+        compiler_params=pltpu.CompilerParams(vmem_limit_bytes=20 << 20),
         name="intersect",
-    )(search, jnp.asarray(host_unpack(), bf16), coeff, extra)
+    )(search, extra, in_hbm(coeff))
 
 
 def total_kernel(in_ref, out_ref):
@@ -482,7 +521,7 @@
         in_specs=vmem(1),
         out_specs=vmem(1)[0],
         out_shape=jax.ShapeDtypeStruct((PEERS, ROWS, 128), bf16),
-        compiler_params=pltpu.CompilerParams(vmem_limit_bytes=40 << 20),
+        compiler_params=pltpu.CompilerParams(vmem_limit_bytes=6 << 20),
         name="total",
     )(arrived)
 
@@ -491,103 +530,128 @@
     return ((values + G // 2) & (G - 1)) - G // 2
 
 
+def row_of(ref, base, lane_wanted, peer_wanted):
+    lane = iota((128, 256), 0)
+    choose = jnp.where(lane == lane_wanted, 1.0, 0.0).astype(bf16)
+    parts = ref[:, base : base + 8, :].astype(f32).reshape(PEERS * 8, 128).astype(bf16)
+    here = jnp.where((iota((PEERS * 8, 256), 0) >> 3) == peer_wanted, dot(parts, choose), 0.0)
+    return jnp.sum(here, 0, keepdims=True)
+
+
+def prepare_kernel(
+    image_ref, first_ref, pos_ref, before_ref, after_ref, start_ref, end_ref,
+    ritz_ref, tangent_ref, spring_ref,
+):
+    column, at = iota((128, 256), 1), iota((PEERS * 8, 256), 1)
+    ritz_ref[...] = row_of(
+        first_ref, 128, 32 + OWN * (column // HALF) + column % OWN, at % HALF // OWN
+    )
+    pos = pos_ref[...]
+    image = image_ref[0]
+    before = jnp.where(image == 0, start_ref[...], before_ref[...])
+    after = jnp.where(image == image_ref[1] - 1, end_ref[...], after_ref[...])
+    ahead = wrap_offset(after - pos).astype(f32)
+    behind = wrap_offset(pos - before).astype(f32)
+    raw = ahead + behind
+    entries = pos.shape[0] * pos.shape[1]
+
+    def mean_square(value):
+        return jnp.sum(jnp.sum(value * value, 1, keepdims=True), 0, keepdims=True) / entries
+
+    tangent = raw * lax.rsqrt(mean_square(raw) + epsilon) * (1.0 / math.sqrt(entries))
+    length_ahead = jnp.sqrt(entries * (mean_square(ahead) + epsilon))
+    length_behind = jnp.sqrt(entries * (mean_square(behind) + epsilon))
+    tangent_ref[...] = tangent
+    spring_ref[...] = spring_constant * (length_ahead - length_behind) * tangent
+
+
+def prepared(image, arrived, pos, before, after, start_pos, end_pos):
+    return pl.pallas_call(
+        prepare_kernel,
+        in_specs=[pl.BlockSpec(memory_space=pltpu.SMEM)] + vmem(6),
+        out_specs=vmem(3),
+        out_shape=[
+            jax.ShapeDtypeStruct((1, 256), f32),
+            jax.ShapeDtypeStruct((3, 256), f32),
+            jax.ShapeDtypeStruct((3, 256), f32),
+        ],
+        compiler_params=pltpu.CompilerParams(vmem_limit_bytes=6 << 20),
+        name="prepare",
+    )(image, arrived, pos, before, after, start_pos, end_pos)
+
+
 def project_kernel(
-    image_ref, whole_ref, first_ref, coeff_ref, flat_ref, pos_ref, before_ref, after_ref,
-    start_ref, end_ref, out_ref, ritz_ref, push_ref, along_ref, inter_ref,
+    whole_ref, flat_ref, tangent_ref, spring_ref, coeff_hbm,
+    out_hbm, push_ref, along_ref, coeff_ref, inter_ref, done_ref, sems, fetch_sems,
 ):
-    step = pl.program_id(0)
-
-    @pl.when(step == 0)
-    def _():
-        for j in range(8):
-            inter_ref[:, 128 * j : 128 * j + 128] = whole_ref[:, 16 * j : 16 * j + 16, :].reshape(
-                2 * BLOCK, 128
-            )
-
-    projected = dot(inter_ref[...], coeff_ref[...])
-    lanes = projected.shape[1]
+    wide = 2048 // FETCHES
+
+    def fetch(k):
+        at = pl.ds(k * wide, wide)
+        return pltpu.make_async_copy(coeff_hbm.at[:, at], coeff_ref.at[:, at], fetch_sems.at[k])
+
+    for k in range(FETCHES):
+        fetch(k).start()
+    lanes = 256
+    chunks = 2048 // lanes
+    for j in range(8):
+        inter_ref[:, 128 * j : 128 * j + 128] = whole_ref[:, 16 * j : 16 * j + 16, :].reshape(
+            2 * BLOCK, 128
+        )
     first = (iota((BLOCK, 128), 1) & 63) < 32
-    for j in range(lanes // 128):
-        at = slice(128 * j, 128 * j + 128)
-        turned = projected[BLOCK:, at]
-        turned = jnp.where(first, -pltpu.roll(turned, 96, 1), pltpu.roll(turned, 32, 1))
-        out_ref[:, at] = (flat_ref[:, at].astype(f32) - (projected[:BLOCK, at] + turned)).astype(bf16)
-
-    @pl.when(step == pl.num_programs(0) - 1)
-    def _():
-        lane, column = iota((128, 256), 0), iota((128, 256), 1)
-        peer, at = iota((PEERS, 256), 0), iota((PEERS, 256), 1)
-
-        def row_of(ref, base, lane_wanted, peer_wanted):
-            choose = jnp.where(lane == lane_wanted, 1.0, 0.0).astype(bf16)
-            total = jnp.zeros((1, 256), f32)
-            parts = ref[:, base : base + 8, :].astype(f32)
-            for k in range(3):
-                here = dot(parts[:, k, :].astype(bf16), choose)
-                here = jnp.where(peer == peer_wanted, here, 0.0)
-                total = total + jnp.sum(here, 0, keepdims=True)
-            return total
-
-        ritz_ref[...] = row_of(
-            first_ref, 0, 32 + OWN * (column // HALF) + column % OWN, at % HALF // OWN
-        )
-        pos = pos_ref[...]
-        image = image_ref[0]
-        before = jnp.where(image == 0, start_ref[...], before_ref[...])
-        after = jnp.where(image == image_ref[1] - 1, end_ref[...], after_ref[...])
-        ahead = wrap_offset(after - pos).astype(f32)
-        behind = wrap_offset(pos - before).astype(f32)
-        raw = ahead + behind
-        entries = pos.shape[0] * pos.shape[1]
-
-        def mean_square(value):
-            return jnp.sum(jnp.sum(value * value, 1, keepdims=True), 0, keepdims=True) / entries
-
-        tangent = raw * lax.rsqrt(mean_square(raw) + epsilon) * (1.0 / math.sqrt(entries))
-        length_ahead = jnp.sqrt(entries * (mean_square(ahead) + epsilon))
-        length_behind = jnp.sqrt(entries * (mean_square(behind) + epsilon))
-        force = jnp.concatenate(
-            [row_of(whole_ref, 128, 8 * alpha + (column & 7), at // 8) for alpha in range(3)], 0
-        )
-        along = jnp.sum(jnp.sum(force * tangent, 1, keepdims=True), 0, keepdims=True)
-        push_ref[...] = (
-            force - along * tangent + spring_constant * (length_ahead - length_behind) * tangent
-        )
-        along_ref[...] = along
-
-
-def corrected(image, whole, arrived, coeff, flat, pos, before, after, start_pos, end_pos):
-    lanes = 256
-    full2 = lambda k: (0, 0)
-    full3 = lambda k: (0, 0, 0)
-    small = pl.BlockSpec((3, 256), full2)
+
+    def send(k):
+        at = pl.ds(k * lanes, lanes)
+        return pltpu.make_async_copy(done_ref.at[:, at], out_hbm.at[:, at], sems.at[k])
+
+    column, at = iota((128, 256), 1), iota((PEERS * 8, 256), 1)
+    tangent = tangent_ref[...]
+    force = jnp.concatenate(
+        [row_of(whole_ref, 128, 8 * alpha + (column & 7), at >> 3) for alpha in range(3)], 0
+    )
+    along = jnp.sum(jnp.sum(force * tangent, 1, keepdims=True), 0, keepdims=True)
+    push = force - along * tangent + spring_ref[...]
+    for alpha in range(3):
+        push_ref[alpha] = push[alpha : alpha + 1]
+    along_ref[...] = along
+    for k in range(chunks):
+        if k * lanes % wide == 0:
+            fetch(k * lanes // wide).wait()
+        projected = dot(inter_ref[...], coeff_ref[:, k * lanes : (k + 1) * lanes])
+        for j in range(lanes // 128):
+            here = slice(128 * j, 128 * j + 128)
+            at = slice(k * lanes + 128 * j, k * lanes + 128 * j + 128)
+            turned = projected[BLOCK:, here]
+            turned = jnp.where(first, -pltpu.roll(turned, 96, 1), pltpu.roll(turned, 32, 1))
+            done_ref[:, at] = (
+                flat_ref[:, at].astype(f32) - (projected[:BLOCK, here] + turned)
+            ).astype(bf16)
+        send(k).start()
+
+    for k in range(chunks):
+        send(k).wait()
+
+
+def corrected(whole, flat, tangent, spring, coeff):
     return pl.pallas_call(
         project_kernel,
-        grid=(2048 // lanes,),
-        in_specs=[
-            pl.BlockSpec(memory_space=pltpu.SMEM),
-            pl.BlockSpec((PEERS, ROWS, 128), full3),
-            pl.BlockSpec((PEERS, 8, 128), lambda k: (0, 16, 0)),
-            pl.BlockSpec((BANDS, lanes), lambda k: (0, k)),
-            pl.BlockSpec((BLOCK, lanes), lambda k: (0, k)),
-            small, small, small, small, small,
-        ],
-        out_specs=[
-            pl.BlockSpec((BLOCK, lanes), lambda k: (0, k)),
-            pl.BlockSpec((1, 256), full2),
-            pl.BlockSpec((3, 256), full2),
-            pl.BlockSpec((1, 1), full2),
-        ],
+        in_specs=vmem(4) + hbm(1),
+        out_specs=hbm(1) + vmem(2),
         out_shape=[
-            jax.ShapeDtypeStruct((BLOCK, 2048), bf16),
-            jax.ShapeDtypeStruct((1, 256), f32),
-            jax.ShapeDtypeStruct((3, 256), f32),
+            pltpu.HBM((BLOCK, 2048), bf16),
+            jax.ShapeDtypeStruct((3, 1, 256), f32),
             jax.ShapeDtypeStruct((1, 1), f32),
         ],
-        scratch_shapes=[pltpu.VMEM((2 * BLOCK, BANDS), bf16)],
-        compiler_params=pltpu.CompilerParams(vmem_limit_bytes=48 << 20),
+        scratch_shapes=[
+            pltpu.VMEM((BANDS, 2048), bf16),
+            pltpu.VMEM((2 * BLOCK, BANDS), bf16),
+            pltpu.VMEM((BLOCK, 2048), bf16),
+            pltpu.SemaphoreType.DMA((8,)),
+            pltpu.SemaphoreType.DMA((FETCHES,)),
+        ],
+        compiler_params=pltpu.CompilerParams(vmem_limit_bytes=16 << 20),
         name="project",
-    )(image, whole, arrived, coeff, flat, pos, before, after, start_pos, end_pos)
+    )(whole, flat, tangent, spring, in_hbm(coeff))
 
 
 def exchanged(array):
@@ -606,20 +670,30 @@
     kinds = species.reshape(1, -1)
     orbitals = own_orbitals(rotation[0], coeff)
     vectors = exchanged(orbitals.reshape(PEERS, OWN * W, 128))
-    before = passed_along(pos, "img", 1)
-    after = passed_along(pos, "img", -1)
     potential = grid_potential(depth, pos, kinds)
-    search, ritz, density = searched(vectors.reshape(W * OWN * W, 128), potential)
+    search, density, ritz = searched(vectors.reshape(W * OWN * W, 128), potential)
     own_search = exchanged(search.reshape(PEERS, OWN * W, 128))
     extra = force_parts(depth, density, pos, kinds, ritz)
     parts, flat = own_intersections(own_search.reshape(HALF * W, 128), coeff, extra)
     arrived = exchanged(parts)
-    whole = exchanged(totals_for_all(arrived))
+    later = lax.optimization_barrier((pos, parts))[0]
+    before = passed_along(later, "img", 1)
+    after = passed_along(later, "img", -1)
+    arrived, before, after = lax.optimization_barrier((arrived, before, after))
+    mine = totals_for_all(arrived)
+    whole = exchanged(mine)
     image = jnp.stack([lax.axis_index("img"), lax.axis_size("img")]).astype(jnp.int32)
-    correction, ritz_values, push, along = corrected(
-        image, whole, arrived, coeff, flat, pos, before, after, start_pos, end_pos
+    arrived, before, after = lax.optimization_barrier((arrived, before, after, mine))[:3]
+    ritz_values, tangent, spring = prepared(
+        image, arrived, pos, before, after, start_pos, end_pos
     )
-    return (correction.reshape(1, BLOCK, 1, 2048), ritz_values, push[None], along.reshape(1))
+    correction, push, along = corrected(whole, flat, tangent, spring, coeff)
+    return (
+        correction.reshape(1, BLOCK, 1, 2048),
+        ritz_values,
+        push.transpose(1, 0, 2),
+        along.reshape(1),
+    )
 
 
 def solution(mesh):

time: 124 us -> 119 us (0.960)
  blocking collectives: 19.8 us -> 0 us
  waiting for transfers between devices: 19.7 us -> 36 us
  starting transfers between devices: 31.5 us -> 39.7 us
  local copies, waits for them, and re-layouts: 7.08 us -> 0.06 us
  Pallas kernels: 42.8 us -> 39.9 us
    all_to_all x1 -> x0, blocking collectives: 19.8 us -> none  [exchanged(): lax.all_to_all(array, GRID_AXES, split_axis=0, concat_axis=0, tiled=True)]
    all_to_all x3 -> x4, waiting for transfers between devices: 14.4 us -> 30.6 us  [exchanged(): lax.all_to_all(array, GRID_AXES, split_axis=0, concat_axis=0, tiled=True)]
    all_to_all x3 -> x4, starting transfers between devices: 20.6 us -> 29.1 us  [exchanged(): lax.all_to_all(array, GRID_AXES, split_axis=0, concat_axis=0, tiled=True)]
    unnamed x32 -> x21, local copies, waits for them, and re-layouts: 7.08 us -> 0.06 us
    pallas_call x4 -> x5, Pallas kernels: 29.9 us -> 27 us  [the longest x1 9.25 us: searched(): pl.pallas_call(transform_kernel, in_specs=vmem(6), out_specs=hbm(2) + vme...]
  transfers between devices with their start and end apart: 5 -> 6, of which waited for: 3 -> 4; matrix products, arithmetic and copies ran while one was open for 0% -> 0% of each run, Pallas kernels for 10% -> 11%
where the time goes in v2:
time: 119 us; the launch traced here: 117 us
  Pallas kernels  39.9 us (34%)
  starting transfers between devices  39.7 us (33%)
  waiting for transfers between devices  36 us (30%)
    all_to_all x4, waiting for transfers between devices, exchanged(): lax.all_to_all(array, GRID_AXES, split_axis=0, concat_axis=0, tiled=True)  30.6 us
    all_to_all x4, starting transfers between devices, exchanged(): lax.all_to_all(array, GRID_AXES, split_axis=0, concat_axis=0, tiled=True)  29.1 us
    ppermute x2, starting transfers between devices, passed_along(): return lax.ppermute(block, axis, route)  10.6 us
    pallas_call x1, Pallas kernels, searched(): pl.pallas_call(transform_kernel, in_specs=vmem(6), out_specs=hbm(2) + vme...  9.25 us
    pallas_call x1, Pallas kernels, corrected(): pl.pallas_call(project_kernel, in_specs=vmem(4) + hbm(1), out_specs=hbm(1...  6.65 us
    pallas_call x1, Pallas kernels, grid_potential(): pl.pallas_call(potential_kernel, in_specs=[pl.BlockSpec(memory_space=pltp...  5.96 us
    pallas_call x1, Pallas kernels, force_parts(): pl.pallas_call(force_kernel, in_specs=[pl.BlockSpec(memory_space=pltpu.SM...  5.76 us
    ppermute x2, waiting for transfers between devices, passed_along(): return lax.ppermute(block, axis, route)  5.39 us
  transfers between devices with their start and end apart: 6, of which 4 were waited for; matrix products, arithmetic and copies ran while one was open for 0% of the time, Pallas kernels for 11%

profile of v2, /device:TPU:67, one launch (start us, length us, event | category | flops | bytes accessed | tf_op | source)
XLA Modules:
  0.0 116.8 jit_solution(8706487160959753222)
XLA Ops:
  0.6 4.5 %orbitals.1 = bf16[4096,128]{1,0:T(8,128)(2,1)} custom-call(bf16[1024,256]{1,0:T(8,128)(2,1)} %bitcast.28, bf16[1024,2048]{1,0:T(8,128)(2,1)} %bitcast.23), custom_call_target="tpu_custom_call" | custom-call | tf_op jit(solution)/shard_map/orbitals/pallas_call | solution.py:130
  5.2 0.0 copy-start.9
  5.2 0.0 copy-start.7
  5.2 0.0 copy-start.8
  5.2 8.6 %all-to-all-start = ((bf16[32,128,128]{2,1,0:T(8,128)(2,1)}), bf16[32,128,128]{2,1,0:T(8,128)(2,1)S(1)}, u32[]{:S(2)}, u32[]{:S(2)}) async-start(bf16[32,128,128]{2,1,0:T(8,128)(2,1)} %bitcast.26), calls=%async_computation | async-start | bytes 2097152 | tf_op jit(solution)/shard_map/all_to_all | solution.py:658
  13.8 0.0 copy-done.9
  13.8 0.0 copy-start.1
  13.8 0.0 copy-start.2
  13.8 0.0 copy-start.3
  13.8 0.0 copy-start.4
  13.8 0.0 copy-done.7
  13.9 0.0 copy-done.8
  13.9 6.0 %potential.1.pot_ref = f32[4096,128]{1,0:T(8,128)S(1)} custom-call(f32[4]{0:T(128)S(1)} %copy-done.8, s32[3,256]{1,0:T(4,128)S(1)} %bitcast.16, s32[1,256]{1,0:T(1,128)S(1)} %bitcast.21), custom_call_target="tpu_custom_call" | custom-call | tf_op jit(solution)/shard_map/potential/pallas_call | solution.py:196
  19.8 7.9 %all-to-all-done = bf16[32,128,128]{2,1,0:T(8,128)(2,1)S(1)} async-done(((bf16[32,128,128]{2,1,0:T(8,128)(2,1)}), bf16[32,128,128]{2,1,0:T(8,128)(2,1)S(1)}, u32[]{:S(2)}, u32[]{:S(2)}) %all-to-all-start) | async-done | bytes 1048608 | tf_op jit(solution)/shard_map/all_to_all | solution.py:658
  27.7 0.0 copy-done.1
  27.7 0.0 copy-done.2
  27.7 0.0 copy-done.3
  27.7 0.0 copy-done.4
  27.7 9.3 %transform.1 = (bf16[4096,128]{1,0:T(8,128)(2,1)}, f32[4096,128]{1,0:T(8,128)}, f32[8,128]{1,0:T(8,128)S(1)}) custom-call(bf16[4096,128]{1,0:T(8,128)(2,1)S(1)} %bitcast.14, f32[4096,128]{1,0:T(8,128)S(1)} %potential.1.pot_ref, bf16[128,256]{1,0:T(8,128)(2,1)S(1)} %copy-done.1, bf16[128,64]{1,0:T(8,128)(2,1)S(1)} %copy-done.3, ...), custom_call_target="tpu_custom_call" | custom-call | tf_op jit(solution)/shard_map/transform/pallas_call | solution.py:346
  37.0 0.0 copy-start
  37.0 6.7 %all-to-all-start.1 = ((bf16[32,128,128]{2,1,0:T(8,128)(2,1)}), bf16[32,128,128]{2,1,0:T(8,128)(2,1)S(1)}, u32[]{:S(2)}, u32[]{:S(2)}) async-start(bf16[32,128,128]{2,1,0:T(8,128)(2,1)} %bitcast.27), calls=%async_computation.1 | async-start | bytes 2097152 | tf_op jit(solution)/shard_map/all_to_all | solution.py:658
  43.7 0.0 copy-done
  43.7 5.8 %force.1.extra_ref = bf16[32,8,128]{2,1,0:T(8,128)(2,1)S(1)} custom-call(f32[4]{0:T(128)S(1)} %copy-done.8, f32[4096,128]{1,0:T(8,128)S(1)} %copy-done, s32[3,256]{1,0:T(4,128)S(1)} %bitcast.17, s32[1,256]{1,0:T(1,128)S(1)} %bitcast.22, f32[8,128]{1,0:T(8,128)S(1)} %get-tuple-element.24.ritz_ref), custom_call_target="tpu_custom_call" | custom-call | tf_op jit(solution)/shard_map/force/pallas_call | solution.py:420
  49.5 7.8 %all-to-all-done.1 = bf16[32,128,128]{2,1,0:T(8,128)(2,1)S(1)} async-done(((bf16[32,128,128]{2,1,0:T(8,128)(2,1)}), bf16[32,128,128]{2,1,0:T(8,128)(2,1)S(1)}, u32[]{:S(2)}, u32[]{:S(2)}) %all-to-all-start.1) | async-done | bytes 1048608 | tf_op jit(solution)/shard_map/all_to_all | solution.py:658
  57.3 5.2 %intersect.1 = (bf16[32,136,128]{2,1,0:T(8,128)(2,1)}, bf16[256,2048]{1,0:T(8,128)(2,1)S(1)}) custom-call(bf16[4096,128]{1,0:T(8,128)(2,1)S(1)} %bitcast.15, bf16[32,8,128]{2,1,0:T(8,128)(2,1)S(1)} %force.1.extra_ref, bf16[1024,2048]{1,0:T(8,128)(2,1)} %bitcast.24), custom_call_target="tpu_custom_call" | custom-call | tf_op jit(solution)/shard_map/intersect/pallas_call | solution.py:478
  62.5 5.6 %all-to-all-start.2 = ((bf16[32,136,128]{2,1,0:T(8,128)(2,1)}), bf16[32,136,128]{2,1,0:T(8,128)(2,1)S(1)}, u32[]{:S(2)}, u32[]{:S(2)}) async-start(bf16[32,136,128]{2,1,0:T(8,128)(2,1)} %get-tuple-element.25), calls=%async_computation.2 | async-start | bytes 2228224 | tf_op jit(solution)/shard_map/all_to_all | solution.py:658
  68.2 8.7 %collective-permute-start = (s32[3,256]{1,0:T(4,128)S(1)}, s32[3,256]{1,0:T(4,128)S(1)}, u32[]{:S(2)}, u32[]{:S(2)}) collective-permute-start(s32[3,256]{1,0:T(4,128)S(1)} %bitcast.18), channel_id=1, source_target_pairs={{0,32},{32,64},{64,96},{96,128},{128,160},{160,192},{192,224},{1,3... | collective-permute-start | bytes 9224 | tf_op jit(solution)/shard_map/ppermute | solution.py:664
  76.9 1.9 %collective-permute-start.1 = (s32[3,256]{1,0:T(4,128)S(1)}, s32[3,256]{1,0:T(4,128)S(1)}, u32[]{:S(2)}, u32[]{:S(2)}) collective-permute-start(s32[3,256]{1,0:T(4,128)S(1)} %bitcast.19), channel_id=1, source_target_pairs={{32,0},{64,32},{96,64},{128,96},{160,128},{192,160},{224,192},{33,... | collective-permute-start | bytes 9224 | tf_op jit(solution)/shard_map/ppermute | solution.py:664
  78.8 0.0 collective-permute-done.before_ref
  78.8 5.4 %collective-permute-done.1.after_ref = s32[3,256]{1,0:T(4,128)S(1)} collective-permute-done((s32[3,256]{1,0:T(4,128)S(1)}, s32[3,256]{1,0:T(4,128)S(1)}, u32[]{:S(2)}, u32[]{:S(2)}) %collective-permute-start.1) | collective-permute-done | bytes 3104 | tf_op jit(solution)/shard_map/ppermute | solution.py:664
  84.2 0.0 all-to-all-done.2.in_ref.first_ref
  84.2 1.2 %total.1 = bf16[32,136,128]{2,1,0:T(8,128)(2,1)} custom-call(bf16[32,136,128]{2,1,0:T(8,128)(2,1)S(1)} %all-to-all-done.2.in_ref.first_ref), custom_call_target="tpu_custom_call" | custom-call | tf_op jit(solution)/shard_map/total/pallas_call | solution.py:519
  85.5 0.0 copy-start.5
  85.5 0.0 copy-start.6
  85.5 8.2 %all-to-all-start.3 = ((bf16[32,136,128]{2,1,0:T(8,128)(2,1)}), bf16[32,136,128]{2,1,0:T(8,128)(2,1)S(1)}, u32[]{:S(2)}, u32[]{:S(2)}) async-start(bf16[32,136,128]{2,1,0:T(8,128)(2,1)} %total.1), calls=%async_computation.3 | async-start | bytes 2228224 | tf_op jit(solution)/shard_map/all_to_all | solution.py:658
  93.7 0.1 pad_add_fusion.image_ref
  93.7 0.0 copy-done.5
  93.7 0.0 copy-done.6
  93.8 1.3 %prepare.1 = (f32[1,256]{1,0:T(1,128)}, f32[3,256]{1,0:T(4,128)S(1)}, f32[3,256]{1,0:T(4,128)S(1)}) custom-call(s32[2]{0:T(128)S(1)} %pad_add_fusion.image_ref, bf16[32,136,128]{2,1,0:T(8,128)(2,1)S(1)} %all-to-all-done.2.in_ref.first_ref, s32[3,256]{1,0:T(4,128)S(1)} %bitcast.20, s32[3,256]{1,0:T(4,128)S(1)} %collective-permute-done.before_ref, ...), custom_call_target="tpu_custom_call" | custom-call | tf_op jit(solution)/shard_map/prepare/pallas_call | solution.py:569
  95.1 15.0 %all-to-all-done.3.whole_ref = bf16[32,136,128]{2,1,0:T(8,128)(2,1)S(1)} async-done(((bf16[32,136,128]{2,1,0:T(8,128)(2,1)}), bf16[32,136,128]{2,1,0:T(8,128)(2,1)S(1)}, u32[]{:S(2)}, u32[]{:S(2)}) %all-to-all-start.3) | async-done | bytes 1114144 | tf_op jit(solution)/shard_map/all_to_all | solution.py:658
  110.0 6.7 %project.1 = (bf16[256,2048]{1,0:T(8,128)(2,1)}, f32[3,1,256]{2,1,0:T(1,128)}, f32[1,1]{1,0:T(1,128)}) custom-call(bf16[32,136,128]{2,1,0:T(8,128)(2,1)S(1)} %all-to-all-done.3.whole_ref, bf16[256,2048]{1,0:T(8,128)(2,1)S(1)} %get-tuple-element.28.flat_ref, f32[3,256]{1,0:T(4,128)S(1)} %get-tuple-element.34.tangent_ref, ...), custom_call_target="tpu_custom_call" | custom-call | tf_op jit(solution)/shard_map/project/pallas_call | solution.py:636
  (1 shorter events, 0.0 us)
Async XLA Ops:
  5.2 8.6 %copy-start.9 = (s32[1,3,256]{2,0,1:T(1,128)S(1)}, s32[1,3,256]{2,0,1:T(1,128)}, u32[]{:S(2)}) copy-start(s32[1,3,256]{2,0,1:T(1,128)} %param.13) | copy-start | bytes 9220
  5.2 8.7 %copy-start.7 = (s32[256]{0:T(256)S(1)}, s32[256]{0:T(256)}, u32[]{:S(2)}) copy-start(s32[256]{0:T(256)} %param.16) | copy-start | bytes 3076
  5.2 8.7 %copy-start.8 = (f32[4]{0:T(128)S(1)}, f32[4]{0:T(128)}, u32[]{:S(2)}) copy-start(f32[4]{0:T(128)} %depth_ref.3) | copy-start | bytes 52
  5.2 22.5 %all-to-all-start = ((bf16[32,128,128]{2,1,0:T(8,128)(2,1)}), bf16[32,128,128]{2,1,0:T(8,128)(2,1)S(1)}, u32[]{:S(2)}, u32[]{:S(2)}) async-start(bf16[32,128,128]{2,1,0:T(8,128)(2,1)} %bitcast.26), calls=%async_computation | async-start | bytes 2097152 | tf_op jit(solution)/shard_map/all_to_all | solution.py:658
  13.8 13.9 %copy-start.1 = (bf16[128,256]{1,0:T(8,128)(2,1)S(1)}, bf16[128,256]{1,0:T(8,128)(2,1)}, u32[]{:S(2)}) copy-start(bf16[128,256]{1,0:T(8,128)(2,1)} %constant.16.clone.zf_ref) | copy-start | bytes 196612
  13.8 13.9 %copy-start.2 = (bf16[256,128]{1,0:T(8,128)(2,1)S(1)}, bf16[256,128]{1,0:T(8,128)(2,1)}, u32[]{:S(2)}) copy-start(bf16[256,128]{1,0:T(8,128)(2,1)} %constant.19.clone.zi_ref) | copy-start | bytes 196612
  13.8 13.9 %copy-start.3 = (bf16[128,64]{1,0:T(8,128)(2,1)S(1)}, bf16[128,64]{1,0:T(8,128)(2,1)}, u32[]{:S(2)}) copy-start(bf16[128,64]{1,0:T(8,128)(2,1)} %constant.17.clone.left_ref) | copy-start | bytes 49156
  13.8 13.9 %copy-start.4 = (bf16[64,128]{1,0:T(8,128)(2,1)S(1)}, bf16[64,128]{1,0:T(8,128)(2,1)}, u32[]{:S(2)}) copy-start(bf16[64,128]{1,0:T(8,128)(2,1)} %constant.18.clone.left_inv_ref) | copy-start | bytes 49156
  37.0 6.7 %copy-start = (f32[4096,128]{1,0:T(8,128)S(1)}, f32[4096,128]{1,0:T(8,128)}, u32[]{:S(2)}) copy-start(f32[4096,128]{1,0:T(8,128)} %get-tuple-element.23.dens_ref) | copy-start | bytes 6291460
  37.0 20.3 %all-to-all-start.1 = ((bf16[32,128,128]{2,1,0:T(8,128)(2,1)}), bf16[32,128,128]{2,1,0:T(8,128)(2,1)S(1)}, u32[]{:S(2)}, u32[]{:S(2)}) async-start(bf16[32,128,128]{2,1,0:T(8,128)(2,1)} %bitcast.27), calls=%async_computation.1 | async-start | bytes 2097152 | tf_op jit(solution)/shard_map/all_to_all | solution.py:658
  62.5 21.7 %all-to-all-start.2 = ((bf16[32,136,128]{2,1,0:T(8,128)(2,1)}), bf16[32,136,128]{2,1,0:T(8,128)(2,1)S(1)}, u32[]{:S(2)}, u32[]{:S(2)}) async-start(bf16[32,136,128]{2,1,0:T(8,128)(2,1)} %get-tuple-element.25), calls=%async_computation.2 | async-start | bytes 2228224 | tf_op jit(solution)/shard_map/all_to_all | solution.py:658
  68.2 10.7 %collective-permute-start = (s32[3,256]{1,0:T(4,128)S(1)}, s32[3,256]{1,0:T(4,128)S(1)}, u32[]{:S(2)}, u32[]{:S(2)}) collective-permute-start(s32[3,256]{1,0:T(4,128)S(1)} %bitcast.18), channel_id=1, source_target_pairs={{0,32},{32,64},{64,96},{96,128},{128,160},{160,192},{192,224},{1,3... | collective-permute-start | bytes 9224 | tf_op jit(solution)/shard_map/ppermute | solution.py:664
  76.9 7.3 %collective-permute-start.1 = (s32[3,256]{1,0:T(4,128)S(1)}, s32[3,256]{1,0:T(4,128)S(1)}, u32[]{:S(2)}, u32[]{:S(2)}) collective-permute-start(s32[3,256]{1,0:T(4,128)S(1)} %bitcast.19), channel_id=1, source_target_pairs={{32,0},{64,32},{96,64},{128,96},{160,128},{192,160},{224,192},{33,... | collective-permute-start | bytes 9224 | tf_op jit(solution)/shard_map/ppermute | solution.py:664
  85.5 8.3 %copy-start.5 = (s32[3,256]{1,0:T(4,128)S(1)}, s32[3,256]{1,0:T(4,128)}, u32[]{:S(2)}) copy-start(s32[3,256]{1,0:T(4,128)} %start_ref.1) | copy-start | bytes 9220
  85.5 8.3 %copy-start.6 = (s32[3,256]{1,0:T(4,128)S(1)}, s32[3,256]{1,0:T(4,128)}, u32[]{:S(2)}) copy-start(s32[3,256]{1,0:T(4,128)} %end_ref.1) | copy-start | bytes 9220
  85.5 24.6 %all-to-all-start.3 = ((bf16[32,136,128]{2,1,0:T(8,128)(2,1)}), bf16[32,136,128]{2,1,0:T(8,128)(2,1)S(1)}, u32[]{:S(2)}, u32[]{:S(2)}) async-start(bf16[32,136,128]{2,1,0:T(8,128)(2,1)} %total.1), calls=%async_computation.3 | async-start | bytes 2228224 | tf_op jit(solution)/shard_map/all_to_all | solution.py:658

commit v3 on v2

--- a/solution.py
+++ b/solution.py
@@ -676,11 +676,10 @@
     extra = force_parts(depth, density, pos, kinds, ritz)
     parts, flat = own_intersections(own_search.reshape(HALF * W, 128), coeff, extra)
     arrived = exchanged(parts)
-    later = lax.optimization_barrier((pos, parts))[0]
+    mine = totals_for_all(arrived)
+    later = lax.optimization_barrier((pos, mine))[0]
     before = passed_along(later, "img", 1)
     after = passed_along(later, "img", -1)
-    arrived, before, after = lax.optimization_barrier((arrived, before, after))
-    mine = totals_for_all(arrived)
     whole = exchanged(mine)
     image = jnp.stack([lax.axis_index("img"), lax.axis_size("img")]).astype(jnp.int32)
     arrived, before, after = lax.optimization_barrier((arrived, before, after, mine))[:3]

time: 119 us -> 113 us (0.950); the launches traced: 117 us -> 112 us
  blocking collectives: 0 us -> 19.8 us
  waiting for transfers between devices: 36 us -> 21 us
  starting transfers between devices: 39.7 us -> 31.6 us
    all_to_all x0 -> x1, blocking collectives: none -> 19.8 us  [exchanged(): lax.all_to_all(array, GRID_AXES, split_axis=0, concat_axis=0, tiled=True)]
    all_to_all x4 -> x3, waiting for transfers between devices: 30.6 us -> 15.7 us  [exchanged(): lax.all_to_all(array, GRID_AXES, split_axis=0, concat_axis=0, tiled=True)]
    all_to_all x4 -> x3, starting transfers between devices: 29.1 us -> 20.7 us  [exchanged(): lax.all_to_all(array, GRID_AXES, split_axis=0, concat_axis=0, tiled=True)]
  transfers between devices with their start and end apart: 6 -> 5, of which waited for: 4 -> 3; matrix products, arithmetic and copies ran while one was open for 0% -> 0% of each run, Pallas kernels for 11% -> 12%
where the time goes in v3:
time: 113 us; the launch traced here: 112 us
  Pallas kernels  38.8 us (34%)
  starting transfers between devices  31.6 us (28%)
  waiting for transfers between devices  21 us (19%)
  blocking collectives  19.8 us (18%)
    all_to_all x3, starting transfers between devices, exchanged(): lax.all_to_all(array, GRID_AXES, split_axis=0, concat_axis=0, tiled=True)  20.7 us
    all_to_all x1, blocking collectives, exchanged(): lax.all_to_all(array, GRID_AXES, split_axis=0, concat_axis=0, tiled=True)  19.8 us
    all_to_all x3, waiting for transfers between devices, exchanged(): lax.all_to_all(array, GRID_AXES, split_axis=0, concat_axis=0, tiled=True)  15.7 us
    ppermute x2, starting transfers between devices, passed_along(): return lax.ppermute(block, axis, route)  10.9 us
    pallas_call x1, Pallas kernels, searched(): pl.pallas_call(transform_kernel, in_specs=vmem(6), out_specs=hbm(2) + vme...  9.24 us
    pallas_call x1, Pallas kernels, corrected(): pl.pallas_call(project_kernel, in_specs=vmem(4) + hbm(1), out_specs=hbm(1...  6.64 us
    pallas_call x1, Pallas kernels, grid_potential(): pl.pallas_call(potential_kernel, in_specs=[pl.BlockSpec(memory_space=pltp...  5.93 us
    pallas_call x1, Pallas kernels, force_parts(): pl.pallas_call(force_kernel, in_specs=[pl.BlockSpec(memory_space=pltpu.SM...  5.76 us
  transfers between devices with their start and end apart: 5, of which 3 were waited for; matrix products, arithmetic and copies ran while one was open for 0% of the time, Pallas kernels for 12%

profile of v3, /device:TPU:67, one launch (start us, length us, event | category | flops | bytes accessed | tf_op | source)
XLA Modules:
  0.0 112.4 jit_solution(9575482162503227185)
XLA Ops:
  0.6 4.5 %orbitals.1 = bf16[4096,128]{1,0:T(8,128)(2,1)} custom-call(bf16[1024,256]{1,0:T(8,128)(2,1)} %bitcast.28, bf16[1024,2048]{1,0:T(8,128)(2,1)} %bitcast.23), custom_call_target="tpu_custom_call" | custom-call | tf_op jit(solution)/shard_map/orbitals/pallas_call | solution.py:130
  5.2 0.0 copy-start.9
  5.2 0.0 copy-start.7
  5.2 0.0 copy-start.8
  5.2 8.6 %all-to-all-start = ((bf16[32,128,128]{2,1,0:T(8,128)(2,1)}), bf16[32,128,128]{2,1,0:T(8,128)(2,1)S(1)}, u32[]{:S(2)}, u32[]{:S(2)}) async-start(bf16[32,128,128]{2,1,0:T(8,128)(2,1)} %bitcast.26), calls=%async_computation | async-start | bytes 2097152 | tf_op jit(solution)/shard_map/all_to_all | solution.py:658
  13.8 0.0 copy-done.9
  13.8 0.0 copy-start.1
  13.8 0.0 copy-start.2
  13.8 0.0 copy-start.3
  13.8 0.0 copy-start.4
  13.8 0.0 copy-done.7
  13.9 0.0 copy-done.8
  13.9 5.9 %potential.1.pot_ref = f32[4096,128]{1,0:T(8,128)S(1)} custom-call(f32[4]{0:T(128)S(1)} %copy-done.8, s32[3,256]{1,0:T(4,128)S(1)} %bitcast.16, s32[1,256]{1,0:T(1,128)S(1)} %bitcast.21), custom_call_target="tpu_custom_call" | custom-call | tf_op jit(solution)/shard_map/potential/pallas_call | solution.py:196
  19.8 7.9 %all-to-all-done = bf16[32,128,128]{2,1,0:T(8,128)(2,1)S(1)} async-done(((bf16[32,128,128]{2,1,0:T(8,128)(2,1)}), bf16[32,128,128]{2,1,0:T(8,128)(2,1)S(1)}, u32[]{:S(2)}, u32[]{:S(2)}) %all-to-all-start) | async-done | bytes 1048608 | tf_op jit(solution)/shard_map/all_to_all | solution.py:658
  27.7 0.0 copy-done.1
  27.7 0.0 copy-done.2
  27.7 0.0 copy-done.3
  27.7 0.0 copy-done.4
  27.7 9.2 %transform.1 = (bf16[4096,128]{1,0:T(8,128)(2,1)}, f32[4096,128]{1,0:T(8,128)}, f32[8,128]{1,0:T(8,128)S(1)}) custom-call(bf16[4096,128]{1,0:T(8,128)(2,1)S(1)} %bitcast.14, f32[4096,128]{1,0:T(8,128)S(1)} %potential.1.pot_ref, bf16[128,256]{1,0:T(8,128)(2,1)S(1)} %copy-done.1, bf16[128,64]{1,0:T(8,128)(2,1)S(1)} %copy-done.3, ...), custom_call_target="tpu_custom_call" | custom-call | tf_op jit(solution)/shard_map/transform/pallas_call | solution.py:346
  37.0 0.0 copy-start
  37.0 6.7 %all-to-all-start.1 = ((bf16[32,128,128]{2,1,0:T(8,128)(2,1)}), bf16[32,128,128]{2,1,0:T(8,128)(2,1)S(1)}, u32[]{:S(2)}, u32[]{:S(2)}) async-start(bf16[32,128,128]{2,1,0:T(8,128)(2,1)} %bitcast.27), calls=%async_computation.1 | async-start | bytes 2097152 | tf_op jit(solution)/shard_map/all_to_all | solution.py:658
  43.7 0.0 copy-done
  43.7 5.8 %force.1.extra_ref = bf16[32,8,128]{2,1,0:T(8,128)(2,1)S(1)} custom-call(f32[4]{0:T(128)S(1)} %copy-done.8, f32[4096,128]{1,0:T(8,128)S(1)} %copy-done, s32[3,256]{1,0:T(4,128)S(1)} %bitcast.17, s32[1,256]{1,0:T(1,128)S(1)} %bitcast.22, f32[8,128]{1,0:T(8,128)S(1)} %get-tuple-element.21.ritz_ref), custom_call_target="tpu_custom_call" | custom-call | tf_op jit(solution)/shard_map/force/pallas_call | solution.py:420
  49.5 7.8 %all-to-all-done.1 = bf16[32,128,128]{2,1,0:T(8,128)(2,1)S(1)} async-done(((bf16[32,128,128]{2,1,0:T(8,128)(2,1)}), bf16[32,128,128]{2,1,0:T(8,128)(2,1)S(1)}, u32[]{:S(2)}, u32[]{:S(2)}) %all-to-all-start.1) | async-done | bytes 1048608 | tf_op jit(solution)/shard_map/all_to_all | solution.py:658
  57.3 4.2 %intersect.1 = (bf16[32,136,128]{2,1,0:T(8,128)(2,1)S(1)}, bf16[256,2048]{1,0:T(8,128)(2,1)S(1)}) custom-call(bf16[4096,128]{1,0:T(8,128)(2,1)S(1)} %bitcast.15, bf16[32,8,128]{2,1,0:T(8,128)(2,1)S(1)} %force.1.extra_ref, bf16[1024,2048]{1,0:T(8,128)(2,1)} %bitcast.24), custom_call_target="tpu_custom_call" | custom-call | tf_op jit(solution)/shard_map/intersect/pallas_call | solution.py:478
  61.5 19.8 %all_to_all.20.in_ref.first_ref = bf16[32,136,128]{2,1,0:T(8,128)(2,1)S(1)} all-to-all(bf16[32,136,128]{2,1,0:T(8,128)(2,1)S(1)} %get-tuple-element.22), channel_id=1, replica_groups=mesh['img'=8,'band'=8,'pw'=4] {'band','pw'}, dimensions={0} | all-to-all | bytes 2228224 | tf_op jit(solution)/shard_map/all_to_all | solution.py:658
  81.3 1.2 %total.1 = bf16[32,136,128]{2,1,0:T(8,128)(2,1)} custom-call(bf16[32,136,128]{2,1,0:T(8,128)(2,1)S(1)} %all_to_all.20.in_ref.first_ref), custom_call_target="tpu_custom_call" | custom-call | tf_op jit(solution)/shard_map/total/pallas_call | solution.py:519
  82.5 0.0 copy-start.5
  82.5 0.0 copy-start.6
  82.5 5.5 %all-to-all-start.3 = ((bf16[32,136,128]{2,1,0:T(8,128)(2,1)}), bf16[32,136,128]{2,1,0:T(8,128)(2,1)S(1)}, u32[]{:S(2)}, u32[]{:S(2)}) async-start(bf16[32,136,128]{2,1,0:T(8,128)(2,1)} %total.1), calls=%async_computation.3 | async-start | bytes 2228224 | tf_op jit(solution)/shard_map/all_to_all | solution.py:658
  88.0 9.0 %collective-permute-start = (s32[3,256]{1,0:T(4,128)S(1)}, s32[3,256]{1,0:T(4,128)S(1)}, u32[]{:S(2)}, u32[]{:S(2)}) collective-permute-start(s32[3,256]{1,0:T(4,128)S(1)} %bitcast.18), channel_id=1, source_target_pairs={{0,32},{32,64},{64,96},{96,128},{128,160},{160,192},{192,224},{1,3... | collective-permute-start | bytes 9224 | tf_op jit(solution)/shard_map/ppermute | solution.py:664
  96.9 1.9 %collective-permute-start.1 = (s32[3,256]{1,0:T(4,128)S(1)}, s32[3,256]{1,0:T(4,128)S(1)}, u32[]{:S(2)}, u32[]{:S(2)}) collective-permute-start(s32[3,256]{1,0:T(4,128)S(1)} %bitcast.19), channel_id=1, source_target_pairs={{32,0},{64,32},{96,64},{128,96},{160,128},{192,160},{224,192},{33,... | collective-permute-start | bytes 9224 | tf_op jit(solution)/shard_map/ppermute | solution.py:664
  98.9 0.1 pad_add_fusion.image_ref
  98.9 0.0 collective-permute-done.before_ref
  98.9 5.3 %collective-permute-done.1.after_ref = s32[3,256]{1,0:T(4,128)S(1)} collective-permute-done((s32[3,256]{1,0:T(4,128)S(1)}, s32[3,256]{1,0:T(4,128)S(1)}, u32[]{:S(2)}, u32[]{:S(2)}) %collective-permute-start.1) | collective-permute-done | bytes 3104 | tf_op jit(solution)/shard_map/ppermute | solution.py:664
  104.3 0.0 copy-done.5
  104.3 0.0 copy-done.6
  104.3 1.3 %prepare.1 = (f32[1,256]{1,0:T(1,128)}, f32[3,256]{1,0:T(4,128)S(1)}, f32[3,256]{1,0:T(4,128)S(1)}) custom-call(s32[2]{0:T(128)S(1)} %pad_add_fusion.image_ref, bf16[32,136,128]{2,1,0:T(8,128)(2,1)S(1)} %all_to_all.20.in_ref.first_ref, s32[3,256]{1,0:T(4,128)S(1)} %bitcast.20, s32[3,256]{1,0:T(4,128)S(1)} %collective-permute-done.before_ref, ...), custom_call_target="tpu_custom_call" | custom-call | tf_op jit(solution)/shard_map/prepare/pallas_call | solution.py:569
  105.6 0.0 all-to-all-done.3.whole_ref
  105.6 6.6 %project.1 = (bf16[256,2048]{1,0:T(8,128)(2,1)}, f32[3,1,256]{2,1,0:T(1,128)}, f32[1,1]{1,0:T(1,128)}) custom-call(bf16[32,136,128]{2,1,0:T(8,128)(2,1)S(1)} %all-to-all-done.3.whole_ref, bf16[256,2048]{1,0:T(8,128)(2,1)S(1)} %get-tuple-element.23.flat_ref, f32[3,256]{1,0:T(4,128)S(1)} %get-tuple-element.28.tangent_ref, ...), custom_call_target="tpu_custom_call" | custom-call | tf_op jit(solution)/shard_map/project/pallas_call | solution.py:636
  (1 shorter events, 0.0 us)
Async XLA Ops:
  5.2 8.6 %copy-start.9 = (s32[1,3,256]{2,0,1:T(1,128)S(1)}, s32[1,3,256]{2,0,1:T(1,128)}, u32[]{:S(2)}) copy-start(s32[1,3,256]{2,0,1:T(1,128)} %param.13) | copy-start | bytes 9220
  5.2 8.7 %copy-start.7 = (s32[256]{0:T(256)S(1)}, s32[256]{0:T(256)}, u32[]{:S(2)}) copy-start(s32[256]{0:T(256)} %param.16) | copy-start | bytes 3076
  5.2 8.7 %copy-start.8 = (f32[4]{0:T(128)S(1)}, f32[4]{0:T(128)}, u32[]{:S(2)}) copy-start(f32[4]{0:T(128)} %depth_ref.3) | copy-start | bytes 52
  5.2 22.5 %all-to-all-start = ((bf16[32,128,128]{2,1,0:T(8,128)(2,1)}), bf16[32,128,128]{2,1,0:T(8,128)(2,1)S(1)}, u32[]{:S(2)}, u32[]{:S(2)}) async-start(bf16[32,128,128]{2,1,0:T(8,128)(2,1)} %bitcast.26), calls=%async_computation | async-start | bytes 2097152 | tf_op jit(solution)/shard_map/all_to_all | solution.py:658
  13.8 13.9 %copy-start.1 = (bf16[128,256]{1,0:T(8,128)(2,1)S(1)}, bf16[128,256]{1,0:T(8,128)(2,1)}, u32[]{:S(2)}) copy-start(bf16[128,256]{1,0:T(8,128)(2,1)} %constant.16.clone.zf_ref) | copy-start | bytes 196612
  13.8 13.9 %copy-start.2 = (bf16[256,128]{1,0:T(8,128)(2,1)S(1)}, bf16[256,128]{1,0:T(8,128)(2,1)}, u32[]{:S(2)}) copy-start(bf16[256,128]{1,0:T(8,128)(2,1)} %constant.19.clone.zi_ref) | copy-start | bytes 196612
  13.8 13.9 %copy-start.3 = (bf16[128,64]{1,0:T(8,128)(2,1)S(1)}, bf16[128,64]{1,0:T(8,128)(2,1)}, u32[]{:S(2)}) copy-start(bf16[128,64]{1,0:T(8,128)(2,1)} %constant.17.clone.left_ref) | copy-start | bytes 49156
  13.8 13.9 %copy-start.4 = (bf16[64,128]{1,0:T(8,128)(2,1)S(1)}, bf16[64,128]{1,0:T(8,128)(2,1)}, u32[]{:S(2)}) copy-start(bf16[64,128]{1,0:T(8,128)(2,1)} %constant.18.clone.left_inv_ref) | copy-start | bytes 49156
  37.0 6.7 %copy-start = (f32[4096,128]{1,0:T(8,128)S(1)}, f32[4096,128]{1,0:T(8,128)}, u32[]{:S(2)}) copy-start(f32[4096,128]{1,0:T(8,128)} %get-tuple-element.20.dens_ref) | copy-start | bytes 6291460
  37.0 20.3 %all-to-all-start.1 = ((bf16[32,128,128]{2,1,0:T(8,128)(2,1)}), bf16[32,128,128]{2,1,0:T(8,128)(2,1)S(1)}, u32[]{:S(2)}, u32[]{:S(2)}) async-start(bf16[32,128,128]{2,1,0:T(8,128)(2,1)} %bitcast.27), calls=%async_computation.1 | async-start | bytes 2097152 | tf_op jit(solution)/shard_map/all_to_all | solution.py:658
  82.5 21.8 %copy-start.5 = (s32[3,256]{1,0:T(4,128)S(1)}, s32[3,256]{1,0:T(4,128)}, u32[]{:S(2)}) copy-start(s32[3,256]{1,0:T(4,128)} %start_ref.1) | copy-start | bytes 9220
  82.5 21.8 %copy-start.6 = (s32[3,256]{1,0:T(4,128)S(1)}, s32[3,256]{1,0:T(4,128)}, u32[]{:S(2)}) copy-start(s32[3,256]{1,0:T(4,128)} %end_ref.1) | copy-start | bytes 9220
  82.5 23.1 %all-to-all-start.3 = ((bf16[32,136,128]{2,1,0:T(8,128)(2,1)}), bf16[32,136,128]{2,1,0:T(8,128)(2,1)S(1)}, u32[]{:S(2)}, u32[]{:S(2)}) async-start(bf16[32,136,128]{2,1,0:T(8,128)(2,1)} %total.1), calls=%async_computation.3 | async-start | bytes 2228224 | tf_op jit(solution)/shard_map/all_to_all | solution.py:658
  88.0 11.0 %collective-permute-start = (s32[3,256]{1,0:T(4,128)S(1)}, s32[3,256]{1,0:T(4,128)S(1)}, u32[]{:S(2)}, u32[]{:S(2)}) collective-permute-start(s32[3,256]{1,0:T(4,128)S(1)} %bitcast.18), channel_id=1, source_target_pairs={{0,32},{32,64},{64,96},{96,128},{128,160},{160,192},{192,224},{1,3... | collective-permute-start | bytes 9224 | tf_op jit(solution)/shard_map/ppermute | solution.py:664
  96.9 7.3 %collective-permute-start.1 = (s32[3,256]{1,0:T(4,128)S(1)}, s32[3,256]{1,0:T(4,128)S(1)}, u32[]{:S(2)}, u32[]{:S(2)}) collective-permute-start(s32[3,256]{1,0:T(4,128)S(1)} %bitcast.19), channel_id=1, source_target_pairs={{32,0},{64,32},{96,64},{128,96},{160,128},{192,160},{224,192},{33,... | collective-permute-start | bytes 9224 | tf_op jit(solution)/shard_map/ppermute | solution.py:664

commit v4 on v3

--- a/solution.py
+++ b/solution.py
@@ -147,6 +147,25 @@
 
 def in_hbm(array):
     return pltpu.with_memory_space_constraint(array, pltpu.HBM)
+
+
+def near_kernel(coeff_hbm, order_ref, out_ref, sem):
+    half = coeff_hbm.shape[1] // 2
+    fetch = pltpu.make_async_copy(coeff_hbm.at[:, pl.ds(0, half)], out_ref, sem)
+    fetch.start()
+    fetch.wait()
+
+
+def brought_near(coeff, order):
+    return pl.pallas_call(
+        near_kernel,
+        in_specs=hbm(1) + vmem(1),
+        out_specs=vmem(1)[0],
+        out_shape=jax.ShapeDtypeStruct((BANDS, 1024), bf16),
+        scratch_shapes=[pltpu.SemaphoreType.DMA],
+        compiler_params=pltpu.CompilerParams(vmem_limit_bytes=1 << 20),
+        name="near",
+    )(in_hbm(coeff), order)
 
 
 def hbm(count):
@@ -581,17 +600,14 @@
 
 
 def project_kernel(
-    whole_ref, flat_ref, tangent_ref, spring_ref, coeff_hbm,
-    out_hbm, push_ref, along_ref, coeff_ref, inter_ref, done_ref, sems, fetch_sems,
+    whole_ref, tangent_ref, spring_ref, near_ref, coeff_hbm, flat_hbm,
+    out_hbm, push_ref, along_ref, rest_ref, flat_ref, inter_ref, done_ref, sems, rest_sem, flat_sem,
 ):
-    wide = 2048 // FETCHES
-
-    def fetch(k):
-        at = pl.ds(k * wide, wide)
-        return pltpu.make_async_copy(coeff_hbm.at[:, at], coeff_ref.at[:, at], fetch_sems.at[k])
-
-    for k in range(FETCHES):
-        fetch(k).start()
+    search = pltpu.make_async_copy(flat_hbm, flat_ref, flat_sem)
+    search.start()
+    half = near_ref.shape[1]
+    rest = pltpu.make_async_copy(coeff_hbm.at[:, pl.ds(half, half)], rest_ref, rest_sem)
+    rest.start()
     lanes = 256
     chunks = 2048 // lanes
     for j in range(8):
@@ -615,9 +631,13 @@
         push_ref[alpha] = push[alpha : alpha + 1]
     along_ref[...] = along
     for k in range(chunks):
-        if k * lanes % wide == 0:
-            fetch(k * lanes // wide).wait()
-        projected = dot(inter_ref[...], coeff_ref[:, k * lanes : (k + 1) * lanes])
+        if k == 0:
+            search.wait()
+        if k * lanes == half:
+            rest.wait()
+        side_ref = near_ref if k * lanes < half else rest_ref
+        start = k * lanes % half
+        projected = dot(inter_ref[...], side_ref[:, start : start + lanes])
         for j in range(lanes // 128):
             here = slice(128 * j, 128 * j + 128)
             at = slice(k * lanes + 128 * j, k * lanes + 128 * j + 128)
@@ -632,10 +652,10 @@
         send(k).wait()
 
 
-def corrected(whole, flat, tangent, spring, coeff):
+def corrected(whole, flat, tangent, spring, near, coeff):
     return pl.pallas_call(
         project_kernel,
-        in_specs=vmem(4) + hbm(1),
+        in_specs=vmem(4) + hbm(2),
         out_specs=hbm(1) + vmem(2),
         out_shape=[
             pltpu.HBM((BLOCK, 2048), bf16),
@@ -643,15 +663,17 @@
             jax.ShapeDtypeStruct((1, 1), f32),
         ],
         scratch_shapes=[
-            pltpu.VMEM((BANDS, 2048), bf16),
+            pltpu.VMEM((BANDS, 1024), bf16),
+            pltpu.VMEM((BLOCK, 2048), bf16),
             pltpu.VMEM((2 * BLOCK, BANDS), bf16),
             pltpu.VMEM((BLOCK, 2048), bf16),
             pltpu.SemaphoreType.DMA((8,)),
-            pltpu.SemaphoreType.DMA((FETCHES,)),
+            pltpu.SemaphoreType.DMA,
+            pltpu.SemaphoreType.DMA,
         ],
         compiler_params=pltpu.CompilerParams(vmem_limit_bytes=16 << 20),
         name="project",
-    )(whole, flat, tangent, spring, in_hbm(coeff))
+    )(whole, tangent, spring, near, in_hbm(coeff), in_hbm(flat))
 
 
 def exchanged(array):
@@ -670,23 +692,25 @@
     kinds = species.reshape(1, -1)
     orbitals = own_orbitals(rotation[0], coeff)
     vectors = exchanged(orbitals.reshape(PEERS, OWN * W, 128))
-    potential = grid_potential(depth, pos, kinds)
+    later = lax.optimization_barrier((pos, orbitals))[0]
+    before = passed_along(later, "img", 1)
+    after = passed_along(later, "img", -1)
+    own, before, after = lax.optimization_barrier((pos, before, after))
+    potential = grid_potential(depth, own, kinds)
     search, density, ritz = searched(vectors.reshape(W * OWN * W, 128), potential)
     own_search = exchanged(search.reshape(PEERS, OWN * W, 128))
     extra = force_parts(depth, density, pos, kinds, ritz)
     parts, flat = own_intersections(own_search.reshape(HALF * W, 128), coeff, extra)
     arrived = exchanged(parts)
     mine = totals_for_all(arrived)
-    later = lax.optimization_barrier((pos, mine))[0]
-    before = passed_along(later, "img", 1)
-    after = passed_along(later, "img", -1)
     whole = exchanged(mine)
     image = jnp.stack([lax.axis_index("img"), lax.axis_size("img")]).astype(jnp.int32)
     arrived, before, after = lax.optimization_barrier((arrived, before, after, mine))[:3]
     ritz_values, tangent, spring = prepared(
         image, arrived, pos, before, after, start_pos, end_pos
     )
-    correction, push, along = corrected(whole, flat, tangent, spring, coeff)
+    near = brought_near(coeff, tangent)
+    correction, push, along = corrected(whole, flat, tangent, spring, near, coeff)
     return (
         correction.reshape(1, BLOCK, 1, 2048),
         ritz_values,

time: 113 us -> 124 us (1.097)
  waiting for transfers between devices: 21 us -> 27.1 us
  blocking collectives: 19.8 us -> 21.9 us
  Pallas kernels: 38.8 us -> 40.5 us
    all_to_all x3, waiting for transfers between devices: 15.7 us -> 21.9 us  [exchanged(): lax.all_to_all(array, GRID_AXES, split_axis=0, concat_axis=0, tiled=True)]
    all_to_all x3, starting transfers between devices: 20.7 us -> 23.5 us  [exchanged(): lax.all_to_all(array, GRID_AXES, split_axis=0, concat_axis=0, tiled=True)]
    ppermute x2, starting transfers between devices: 10.9 us -> 8.25 us  [passed_along(): return lax.ppermute(block, axis, route)]
    all_to_all x1, blocking collectives: 19.8 us -> 21.9 us  [exchanged(): lax.all_to_all(array, GRID_AXES, split_axis=0, concat_axis=0, tiled=True)]
    pallas_call x1 -> x2, Pallas kernels: 6.64 us -> 8.31 us  [the longest x1 6.71 us: corrected(): pl.pallas_call(project_kernel, in_specs=vmem(4) + hbm(2), out_specs=hbm(1...]
  transfers between devices with their start and end apart: 5 -> 5, of which waited for: 3 -> 4; matrix products, arithmetic and copies ran while one was open for 0% -> 0% of each run, Pallas kernels for 12% -> 12%
where the time goes in v4:
time: 124 us; the launch traced here: 122 us
  Pallas kernels  40.5 us (33%)
  starting transfers between devices  31.7 us (26%)
  waiting for transfers between devices  27.1 us (22%)
  blocking collectives  21.9 us (18%)
    all_to_all x3, starting transfers between devices, exchanged(): lax.all_to_all(array, GRID_AXES, split_axis=0, concat_axis=0, tiled=True)  23.5 us
    all_to_all x1, blocking collectives, exchanged(): lax.all_to_all(array, GRID_AXES, split_axis=0, concat_axis=0, tiled=True)  21.9 us
    all_to_all x3, waiting for transfers between devices, exchanged(): lax.all_to_all(array, GRID_AXES, split_axis=0, concat_axis=0, tiled=True)  21.9 us
    pallas_call x1, Pallas kernels, searched(): pl.pallas_call(transform_kernel, in_specs=vmem(6), out_specs=hbm(2) + vme...  9.27 us
    ppermute x2, starting transfers between devices, passed_along(): return lax.ppermute(block, axis, route)  8.25 us
    pallas_call x1, Pallas kernels, corrected(): pl.pallas_call(project_kernel, in_specs=vmem(4) + hbm(2), out_specs=hbm(1...  6.71 us
    pallas_call x1, Pallas kernels, grid_potential(): pl.pallas_call(potential_kernel, in_specs=[pl.BlockSpec(memory_space=pltp...  5.93 us
    pallas_call x1, Pallas kernels, force_parts(): pl.pallas_call(force_kernel, in_specs=[pl.BlockSpec(memory_space=pltpu.SM...  5.76 us
  transfers between devices with their start and end apart: 5, of which 4 were waited for; matrix products, arithmetic and copies ran while one was open for 0% of the time, Pallas kernels for 12%

profile of v4, /device:TPU:67, one launch (start us, length us, event | category | flops | bytes accessed | tf_op | source)
XLA Modules:
  0.0 122.4 jit_solution(6720900670392046753)
XLA Ops:
  0.6 4.5 %orbitals.1 = bf16[4096,128]{1,0:T(8,128)(2,1)} custom-call(bf16[1024,256]{1,0:T(8,128)(2,1)} %bitcast.29, bf16[1024,2048]{1,0:T(8,128)(2,1)} %bitcast.23), custom_call_target="tpu_custom_call" | custom-call | tf_op jit(solution)/shard_map/orbitals/pallas_call | solution.py:130
  5.2 0.0 copy-start.10
  5.2 0.0 copy-start.8
  5.2 0.0 copy-start.9
  5.2 0.0 copy-start.2
  5.2 0.0 copy-start.3
  5.2 0.0 copy-start.4
  5.2 0.0 copy-start.5
  5.3 8.6 %all-to-all-start = ((bf16[32,128,128]{2,1,0:T(8,128)(2,1)}), bf16[32,128,128]{2,1,0:T(8,128)(2,1)S(1)}, u32[]{:S(2)}, u32[]{:S(2)}) async-start(bf16[32,128,128]{2,1,0:T(8,128)(2,1)} %bitcast.27), calls=%async_computation | async-start | bytes 2097152 | tf_op jit(solution)/shard_map/all_to_all | solution.py:680
  13.8 0.0 copy-done.10
  13.8 6.3 %collective-permute-start = (s32[3,256]{1,0:T(4,128)S(1)}, s32[3,256]{1,0:T(4,128)S(1)}, u32[]{:S(2)}, u32[]{:S(2)}) collective-permute-start(s32[3,256]{1,0:T(4,128)S(1)} %bitcast.16), channel_id=1, source_target_pairs={{0,32},{32,64},{64,96},{96,128},{128,160},{160,192},{192,224},{1,3... | collective-permute-start | bytes 9224 | tf_op jit(solution)/shard_map/ppermute | solution.py:686
  20.2 1.9 %collective-permute-start.1 = (s32[3,256]{1,0:T(4,128)S(1)}, s32[3,256]{1,0:T(4,128)S(1)}, u32[]{:S(2)}, u32[]{:S(2)}) collective-permute-start(s32[3,256]{1,0:T(4,128)S(1)} %bitcast.17), channel_id=1, source_target_pairs={{32,0},{64,32},{96,64},{128,96},{160,128},{192,160},{224,192},{33,... | collective-permute-start | bytes 9224 | tf_op jit(solution)/shard_map/ppermute | solution.py:686
  22.1 2.3 %collective-permute-done.before_ref = s32[3,256]{1,0:T(4,128)S(1)} collective-permute-done((s32[3,256]{1,0:T(4,128)S(1)}, s32[3,256]{1,0:T(4,128)S(1)}, u32[]{:S(2)}, u32[]{:S(2)}) %collective-permute-start) | collective-permute-done | bytes 3104 | tf_op jit(solution)/shard_map/ppermute | solution.py:686
  24.4 2.9 %collective-permute-done.1.after_ref = s32[3,256]{1,0:T(4,128)S(1)} collective-permute-done((s32[3,256]{1,0:T(4,128)S(1)}, s32[3,256]{1,0:T(4,128)S(1)}, u32[]{:S(2)}, u32[]{:S(2)}) %collective-permute-start.1) | collective-permute-done | bytes 3104 | tf_op jit(solution)/shard_map/ppermute | solution.py:686
  27.3 0.0 copy-done.8
  27.3 0.0 copy-done.9
  27.3 5.9 %potential.1.pot_ref = f32[4096,128]{1,0:T(8,128)S(1)} custom-call(f32[4]{0:T(128)S(1)} %copy-done.9, s32[3,256]{1,0:T(4,128)S(1)} %bitcast.18, s32[1,256]{1,0:T(1,128)S(1)} %bitcast.21), custom_call_target="tpu_custom_call" | custom-call | tf_op jit(solution)/shard_map/potential/pallas_call | solution.py:215
  33.3 0.0 all-to-all-done
  33.3 0.0 copy-done.2
  33.3 0.0 copy-done.3
  33.3 0.0 copy-done.4
  33.3 0.0 copy-done.5
  33.3 9.3 %transform.1 = (bf16[4096,128]{1,0:T(8,128)(2,1)}, f32[4096,128]{1,0:T(8,128)}, f32[8,128]{1,0:T(8,128)S(1)}) custom-call(bf16[4096,128]{1,0:T(8,128)(2,1)S(1)} %bitcast.14, f32[4096,128]{1,0:T(8,128)S(1)} %potential.1.pot_ref, bf16[128,256]{1,0:T(8,128)(2,1)S(1)} %copy-done.2, bf16[128,64]{1,0:T(8,128)(2,1)S(1)} %copy-done.4, ...), custom_call_target="tpu_custom_call" | custom-call | tf_op jit(solution)/shard_map/transform/pallas_call | solution.py:365
  42.6 0.0 copy-start
  42.6 10.1 %all-to-all-start.1 = ((bf16[32,128,128]{2,1,0:T(8,128)(2,1)}), bf16[32,128,128]{2,1,0:T(8,128)(2,1)S(1)}, u32[]{:S(2)}, u32[]{:S(2)}) async-start(bf16[32,128,128]{2,1,0:T(8,128)(2,1)} %bitcast.28), calls=%async_computation.1 | async-start | bytes 2097152 | tf_op jit(solution)/shard_map/all_to_all | solution.py:680
  52.7 0.0 copy-done
  52.8 5.8 %force.1.extra_ref = bf16[32,8,128]{2,1,0:T(8,128)(2,1)S(1)} custom-call(f32[4]{0:T(128)S(1)} %copy-done.9, f32[4096,128]{1,0:T(8,128)S(1)} %copy-done, s32[3,256]{1,0:T(4,128)S(1)} %bitcast.19, s32[1,256]{1,0:T(1,128)S(1)} %bitcast.22, f32[8,128]{1,0:T(8,128)S(1)} %get-tuple-element.26.ritz_ref), custom_call_target="tpu_custom_call" | custom-call | tf_op jit(solution)/shard_map/force/pallas_call | solution.py:439
  58.5 7.9 %all-to-all-done.1 = bf16[32,128,128]{2,1,0:T(8,128)(2,1)S(1)} async-done(((bf16[32,128,128]{2,1,0:T(8,128)(2,1)}), bf16[32,128,128]{2,1,0:T(8,128)(2,1)S(1)}, u32[]{:S(2)}, u32[]{:S(2)}) %all-to-all-start.1) | async-done | bytes 1048608 | tf_op jit(solution)/shard_map/all_to_all | solution.py:680
  66.4 4.2 %intersect.1 = (bf16[32,136,128]{2,1,0:T(8,128)(2,1)S(1)}, bf16[256,2048]{1,0:T(8,128)(2,1)S(1)}) custom-call(bf16[4096,128]{1,0:T(8,128)(2,1)S(1)} %bitcast.15, bf16[32,8,128]{2,1,0:T(8,128)(2,1)S(1)} %force.1.extra_ref, bf16[1024,2048]{1,0:T(8,128)(2,1)} %bitcast.24), custom_call_target="tpu_custom_call" | custom-call | tf_op jit(solution)/shard_map/intersect/pallas_call | solution.py:497
  70.6 0.0 copy-start.1
  70.6 21.9 %all_to_all.20.in_ref.first_ref = bf16[32,136,128]{2,1,0:T(8,128)(2,1)S(1)} all-to-all(bf16[32,136,128]{2,1,0:T(8,128)(2,1)S(1)} %get-tuple-element.27), channel_id=1, replica_groups=mesh['img'=8,'band'=8,'pw'=4] {'band','pw'}, dimensions={0} | all-to-all | bytes 2228224 | tf_op jit(solution)/shard_map/all_to_all | solution.py:680
  92.5 0.0 copy-done.1
  92.5 0.0 copy-start.6
  92.5 0.0 copy-start.7
  92.5 1.2 %total.1 = bf16[32,136,128]{2,1,0:T(8,128)(2,1)} custom-call(bf16[32,136,128]{2,1,0:T(8,128)(2,1)S(1)} %all_to_all.20.in_ref.first_ref), custom_call_target="tpu_custom_call" | custom-call | tf_op jit(solution)/shard_map/total/pallas_call | solution.py:538
  93.8 4.8 %all-to-all-start.3 = ((bf16[32,136,128]{2,1,0:T(8,128)(2,1)}), bf16[32,136,128]{2,1,0:T(8,128)(2,1)S(1)}, u32[]{:S(2)}, u32[]{:S(2)}) async-start(bf16[32,136,128]{2,1,0:T(8,128)(2,1)} %total.1), calls=%async_computation.3 | async-start | bytes 2228224 | tf_op jit(solution)/shard_map/all_to_all | solution.py:680
  98.6 0.1 pad_add_fusion.image_ref
  98.6 0.0 copy-done.6
  98.7 0.0 copy-done.7
  98.7 1.3 %prepare.1 = (f32[1,256]{1,0:T(1,128)}, f32[3,256]{1,0:T(4,128)S(1)}, f32[3,256]{1,0:T(4,128)S(1)}) custom-call(s32[2]{0:T(128)S(1)} %pad_add_fusion.image_ref, bf16[32,136,128]{2,1,0:T(8,128)(2,1)S(1)} %all_to_all.20.in_ref.first_ref, s32[3,256]{1,0:T(4,128)S(1)} %bitcast.20, s32[3,256]{1,0:T(4,128)S(1)} %collective-permute-done.before_ref, ...), custom_call_target="tpu_custom_call" | custom-call | tf_op jit(solution)/shard_map/prepare/pallas_call | solution.py:588
  100.0 1.6 %near.1.near_ref = bf16[1024,1024]{1,0:T(8,128)(2,1)S(1)} custom-call(bf16[1024,2048]{1,0:T(8,128)(2,1)} %bitcast.25, f32[3,256]{1,0:T(4,128)S(1)} %get-tuple-element.33.order_ref.tangent_ref), custom_call_target="tpu_custom_call" | custom-call | tf_op jit(solution)/shard_map/near/pallas_call | solution.py:160
  101.6 13.9 %all-to-all-done.3.whole_ref = bf16[32,136,128]{2,1,0:T(8,128)(2,1)S(1)} async-done(((bf16[32,136,128]{2,1,0:T(8,128)(2,1)}), bf16[32,136,128]{2,1,0:T(8,128)(2,1)S(1)}, u32[]{:S(2)}, u32[]{:S(2)}) %all-to-all-start.3) | async-done | bytes 1114144 | tf_op jit(solution)/shard_map/all_to_all | solution.py:680
  115.5 6.7 %project.1 = (bf16[256,2048]{1,0:T(8,128)(2,1)}, f32[3,1,256]{2,1,0:T(1,128)}, f32[1,1]{1,0:T(1,128)}) custom-call(bf16[32,136,128]{2,1,0:T(8,128)(2,1)S(1)} %all-to-all-done.3.whole_ref, f32[3,256]{1,0:T(4,128)S(1)} %get-tuple-element.33.order_ref.tangent_ref, f32[3,256]{1,0:T(4,128)S(1)} %get-tuple-element.34.spring_ref, ...), custom_call_target="tpu_custom_call" | custom-call | tf_op jit(solution)/shard_map/project/pallas_call | solution.py:656
  (1 shorter events, 0.0 us)
Async XLA Ops:
  5.2 8.7 %copy-start.10 = (s32[1,3,256]{2,0,1:T(1,128)S(1)}, s32[1,3,256]{2,0,1:T(1,128)}, u32[]{:S(2)}) copy-start(s32[1,3,256]{2,0,1:T(1,128)} %param.13) | copy-start | bytes 9220
  5.2 22.1 %copy-start.8 = (s32[256]{0:T(256)S(1)}, s32[256]{0:T(256)}, u32[]{:S(2)}) copy-start(s32[256]{0:T(256)} %param.16) | copy-start | bytes 3076
  5.2 22.1 %copy-start.9 = (f32[4]{0:T(128)S(1)}, f32[4]{0:T(128)}, u32[]{:S(2)}) copy-start(f32[4]{0:T(128)} %depth_ref.3) | copy-start | bytes 52
  5.2 28.1 %copy-start.2 = (bf16[128,256]{1,0:T(8,128)(2,1)S(1)}, bf16[128,256]{1,0:T(8,128)(2,1)}, u32[]{:S(2)}) copy-start(bf16[128,256]{1,0:T(8,128)(2,1)} %constant.16.clone.zf_ref) | copy-start | bytes 196612
  5.2 28.1 %copy-start.3 = (bf16[256,128]{1,0:T(8,128)(2,1)S(1)}, bf16[256,128]{1,0:T(8,128)(2,1)}, u32[]{:S(2)}) copy-start(bf16[256,128]{1,0:T(8,128)(2,1)} %constant.19.clone.zi_ref) | copy-start | bytes 196612
  5.2 28.1 %copy-start.4 = (bf16[128,64]{1,0:T(8,128)(2,1)S(1)}, bf16[128,64]{1,0:T(8,128)(2,1)}, u32[]{:S(2)}) copy-start(bf16[128,64]{1,0:T(8,128)(2,1)} %constant.17.clone.left_ref) | copy-start | bytes 49156
  5.2 28.1 %copy-start.5 = (bf16[64,128]{1,0:T(8,128)(2,1)S(1)}, bf16[64,128]{1,0:T(8,128)(2,1)}, u32[]{:S(2)}) copy-start(bf16[64,128]{1,0:T(8,128)(2,1)} %constant.18.clone.left_inv_ref) | copy-start | bytes 49156
  5.3 28.0 %all-to-all-start = ((bf16[32,128,128]{2,1,0:T(8,128)(2,1)}), bf16[32,128,128]{2,1,0:T(8,128)(2,1)S(1)}, u32[]{:S(2)}, u32[]{:S(2)}) async-start(bf16[32,128,128]{2,1,0:T(8,128)(2,1)} %bitcast.27), calls=%async_computation | async-start | bytes 2097152 | tf_op jit(solution)/shard_map/all_to_all | solution.py:680
  13.8 10.5 %collective-permute-start = (s32[3,256]{1,0:T(4,128)S(1)}, s32[3,256]{1,0:T(4,128)S(1)}, u32[]{:S(2)}, u32[]{:S(2)}) collective-permute-start(s32[3,256]{1,0:T(4,128)S(1)} %bitcast.16), channel_id=1, source_target_pairs={{0,32},{32,64},{64,96},{96,128},{128,160},{160,192},{192,224},{1,3... | collective-permute-start | bytes 9224 | tf_op jit(solution)/shard_map/ppermute | solution.py:686
  20.2 7.1 %collective-permute-start.1 = (s32[3,256]{1,0:T(4,128)S(1)}, s32[3,256]{1,0:T(4,128)S(1)}, u32[]{:S(2)}, u32[]{:S(2)}) collective-permute-start(s32[3,256]{1,0:T(4,128)S(1)} %bitcast.17), channel_id=1, source_target_pairs={{32,0},{64,32},{96,64},{128,96},{160,128},{192,160},{224,192},{33,... | collective-permute-start | bytes 9224 | tf_op jit(solution)/shard_map/ppermute | solution.py:686
  42.6 10.2 %copy-start = (f32[4096,128]{1,0:T(8,128)S(1)}, f32[4096,128]{1,0:T(8,128)}, u32[]{:S(2)}) copy-start(f32[4096,128]{1,0:T(8,128)} %get-tuple-element.25.dens_ref) | copy-start | bytes 6291460
  42.6 23.8 %all-to-all-start.1 = ((bf16[32,128,128]{2,1,0:T(8,128)(2,1)}), bf16[32,128,128]{2,1,0:T(8,128)(2,1)S(1)}, u32[]{:S(2)}, u32[]{:S(2)}) async-start(bf16[32,128,128]{2,1,0:T(8,128)(2,1)} %bitcast.28), calls=%async_computation.1 | async-start | bytes 2097152 | tf_op jit(solution)/shard_map/all_to_all | solution.py:680
  70.6 21.9 %copy-start.1 = (bf16[256,2048]{1,0:T(8,128)(2,1)}, bf16[256,2048]{1,0:T(8,128)(2,1)S(1)}, u32[]{:S(2)}) copy-start(bf16[256,2048]{1,0:T(8,128)(2,1)S(1)} %get-tuple-element.35.flat_hbm) | copy-start | bytes 3145732
  92.5 6.1 %copy-start.6 = (s32[3,256]{1,0:T(4,128)S(1)}, s32[3,256]{1,0:T(4,128)}, u32[]{:S(2)}) copy-start(s32[3,256]{1,0:T(4,128)} %start_ref.1) | copy-start | bytes 9220
  92.5 6.1 %copy-start.7 = (s32[3,256]{1,0:T(4,128)S(1)}, s32[3,256]{1,0:T(4,128)}, u32[]{:S(2)}) copy-start(s32[3,256]{1,0:T(4,128)} %end_ref.1) | copy-start | bytes 9220
  93.8 21.7 %all-to-all-start.3 = ((bf16[32,136,128]{2,1,0:T(8,128)(2,1)}), bf16[32,136,128]{2,1,0:T(8,128)(2,1)S(1)}, u32[]{:S(2)}, u32[]{:S(2)}) async-start(bf16[32,136,128]{2,1,0:T(8,128)(2,1)} %total.1), calls=%async_computation.3 | async-start | bytes 2228224 | tf_op jit(solution)/shard_map/all_to_all | solution.py:680

commit v5 on v3

--- a/solution.py
+++ b/solution.py
@@ -82,7 +82,9 @@
 
 
 def orbitals_kernel(
-    rot_hbm, coeff_hbm, out_hbm, coeff_ref, rot_ref, turned_ref, wide_ref, out_ref, sems
+    rot_hbm, coeff_hbm, depth_hbm, pos_hbm, species_hbm, out_hbm, pot_hbm,
+    coeff_ref, rot_ref, turned_ref, wide_ref, out_ref, pot_ref, gy_ref, depth_ref, pos_ref,
+    species_ref, sems, small_sems,
 ):
     lanes = 2048 // CHUNKS
 
@@ -94,6 +96,24 @@
     turned.start()
     for k in range(CHUNKS):
         fetch(k).start()
+    keep = pltpu.make_async_copy(pot_ref, pot_hbm, small_sems.at[3])
+
+    @pl.when(potential_first())
+    def _():
+        small = [
+            pltpu.make_async_copy(source, target, small_sems.at[k])
+            for k, (source, target) in enumerate(
+                [(depth_hbm, depth_ref), (pos_hbm, pos_ref), (species_hbm, species_ref)]
+            )
+        ]
+        for copy in small:
+            copy.start()
+        for copy in small:
+            copy.wait()
+        places = [pos_ref[k] for k in range(3)]
+        write_potential(depth_ref, places, species_ref[...], pot_ref, gy_ref)
+        keep.start()
+
     source, target = iota((256, 256), 0), iota((256, 256), 1)
     same = (source & 63) == (target & 63)
     same &= (source >> 7) == ((target >> 6) & 1)
@@ -125,24 +145,34 @@
     for k in range(parts):
         send(k).wait()
 
-
-def own_orbitals(rotation, coeff):
+    @pl.when(potential_first())
+    def _():
+        keep.wait()
+
+
+def own_orbitals(rotation, coeff, depth, places, species):
     return pl.pallas_call(
         orbitals_kernel,
-        in_specs=hbm(2),
-        out_specs=hbm(1)[0],
-        out_shape=pltpu.HBM((HALF * W, 128), bf16),
+        in_specs=hbm(5),
+        out_specs=hbm(2),
+        out_shape=[pltpu.HBM((HALF * W, 128), bf16), pltpu.HBM((G * G, 128), f32)],
         scratch_shapes=[
             pltpu.VMEM((BANDS, 2048), bf16),
             pltpu.VMEM((BANDS, BLOCK), bf16),
             pltpu.VMEM((BLOCK, BANDS), bf16),
             pltpu.VMEM((HALF * LINE, 128), f32),
             pltpu.VMEM((HALF * W, 128), bf16),
+            pltpu.VMEM((G * G, 128), f32),
+            pltpu.VMEM((G, 256), f32),
+            pltpu.SMEM((SPECIES,), f32),
+            pltpu.VMEM((3, 1, 256), jnp.int32),
+            pltpu.VMEM((1, 256), jnp.int32),
             pltpu.SemaphoreType.DMA((CHUNKS + 5,)),
+            pltpu.SemaphoreType.DMA((4,)),
         ],
         compiler_params=pltpu.CompilerParams(vmem_limit_bytes=20 << 20),
         name="orbitals",
-    )(in_hbm(rotation), in_hbm(coeff))
+    )(*[in_hbm(array) for array in (rotation, coeff, depth, places, species)])
 
 
 def in_hbm(array):
@@ -170,12 +200,12 @@
     return strength
 
 
-def potential_kernel(depth_ref, pos_ref, species_ref, out_ref, gy_ref):
-    strength = strengths(species_ref[...], depth_ref)
-    gauss_x, _ = gaussian(pos_ref[0:1, :], G)
+def write_potential(depth_ref, places, species, out_ref, gy_ref):
+    strength = strengths(species, depth_ref)
+    gauss_x, _ = gaussian(places[0], G)
     gauss_x = gauss_x * strength
-    gy_ref[...], _ = gaussian(pos_ref[1:2, :], G)
-    gauss_z, _ = gaussian(pos_ref[2:3, :], 2 * G)
+    gy_ref[...], _ = gaussian(places[1], G)
+    gauss_z, _ = gaussian(places[2], 2 * G)
     z_high, z_low = split_two(gauss_z)
     per = 8
 
@@ -192,23 +222,46 @@
     lax.fori_loop(0, G // per, some, 0)
 
 
-def grid_potential(depth, pos, species):
+def potential_first():
+    return lax.axis_index("img") % 2 == 1
+
+
+def potential_kernel(depth_ref, pos_ref, species_ref, given_hbm, out_hbm, pot_ref, gy_ref, sem):
+    del given_hbm
+
+    @pl.when(jnp.logical_not(potential_first()))
+    def _():
+        places = [pos_ref[k : k + 1, :] for k in range(3)]
+        write_potential(depth_ref, places, species_ref[...], pot_ref, gy_ref)
+        keep = pltpu.make_async_copy(pot_ref, out_hbm, sem)
+        keep.start()
+        keep.wait()
+
+
+def grid_potential(depth, pos, species, given):
     return pl.pallas_call(
         potential_kernel,
-        in_specs=[pl.BlockSpec(memory_space=pltpu.SMEM)] + vmem(2),
-        out_specs=vmem(1)[0],
-        out_shape=jax.ShapeDtypeStruct((G * G, 128), f32),
-        scratch_shapes=[pltpu.VMEM((G, 256), f32)],
-        compiler_params=pltpu.CompilerParams(vmem_limit_bytes=10 << 20),
+        in_specs=[pl.BlockSpec(memory_space=pltpu.SMEM)] + vmem(2) + hbm(1),
+        out_specs=hbm(1)[0],
+        out_shape=pltpu.HBM((G * G, 128), f32),
+        input_output_aliases={3: 0},
+        scratch_shapes=[
+            pltpu.VMEM((G * G, 128), f32),
+            pltpu.VMEM((G, 256), f32),
+            pltpu.SemaphoreType.DMA,
+        ],
+        compiler_params=pltpu.CompilerParams(vmem_limit_bytes=12 << 20),
         name="potential",
-    )(depth, pos, species)
+    )(depth, pos, species, in_hbm(given))
 
 
 def transform_kernel(
-    orb_ref, pot_ref, zf_ref, left_ref, left_inv_ref, zi_ref,
+    orb_ref, zf_ref, left_ref, left_inv_ref, zi_ref, pot_hbm,
     out_hbm, dens_hbm, ritz_ref,
-    mid_ref, ham_ref, num_ref, den_ref, dens_ref, out_ref, sems,
+    pot_ref, mid_ref, ham_ref, num_ref, den_ref, dens_ref, out_ref, sems,
 ):
+    bring = pltpu.make_async_copy(pot_hbm, pot_ref, sems.at[5])
+    bring.start()
     group = GROUP
     rows = group * OWN * W
 
@@ -228,6 +281,8 @@
         return carry
 
     lax.fori_loop(0, W // group, forward, 0)
+
+    bring.wait()
 
     def space(i, carry):
         parts = []
@@ -345,7 +400,7 @@
     z_fwd, left, left_inv, z_inv = host_tables()
     return pl.pallas_call(
         transform_kernel,
-        in_specs=vmem(6),
+        in_specs=vmem(5) + hbm(1),
         out_specs=hbm(2) + vmem(1),
         out_shape=[
             pltpu.HBM((W * OWN * W, 128), bf16),
@@ -353,17 +408,18 @@
             jax.ShapeDtypeStruct((8, 128), f32),
         ],
         scratch_shapes=[
+            pltpu.VMEM((G * G, 128), f32),
             pltpu.VMEM((OWN * W * PITCH, 128), f32),
             pltpu.VMEM((W * OWN * W, 128), f32),
             pltpu.VMEM((OWN * W, 128), f32),
             pltpu.VMEM((OWN * W, 128), f32),
             pltpu.VMEM((G * G, 128), f32),
             pltpu.VMEM((W * OWN * W, 128), bf16),
-            pltpu.SemaphoreType.DMA((5,)),
+            pltpu.SemaphoreType.DMA((6,)),
         ],
         compiler_params=pltpu.CompilerParams(vmem_limit_bytes=30 << 20),
         name="transform",
-    )(orbitals, potential, z_fwd, left, left_inv, z_inv)
+    )(orbitals, z_fwd, left, left_inv, z_inv, in_hbm(potential))
 
 
 def force_kernel(
@@ -668,9 +724,11 @@
     coeff = coefficients.reshape(BANDS, 2048)
     pos = positions[0]
     kinds = species.reshape(1, -1)
-    orbitals = own_orbitals(rotation[0], coeff)
+    orbitals, given = own_orbitals(
+        rotation[0], coeff, depth, positions.transpose(1, 0, 2), kinds
+    )
     vectors = exchanged(orbitals.reshape(PEERS, OWN * W, 128))
-    potential = grid_potential(depth, pos, kinds)
+    potential = grid_potential(depth, pos, kinds, given)
     search, density, ritz = searched(vectors.reshape(W * OWN * W, 128), potential)
     own_search = exchanged(search.reshape(PEERS, OWN * W, 128))
     extra = force_parts(depth, density, pos, kinds, ritz)

time: 113 us -> 118 us (1.044)
  waiting for transfers between devices: 21 us -> 27 us
  starting transfers between devices: 31.6 us -> 26.2 us
  blocking collectives: 19.8 us -> 22.4 us
    all_to_all x3, waiting for transfers between devices: 15.7 us -> 21.9 us  [exchanged(): lax.all_to_all(array, GRID_AXES, split_axis=0, concat_axis=0, tiled=True)]
    pallas_call x2, Pallas kernels: 13.8 us -> 19.9 us  [the longest x1 10.6 us: own_orbitals(): pl.pallas_call(orbitals_kernel, in_specs=hbm(5), out_specs=hbm(2), out_sh...]
    pallas_call x1, Pallas kernels: 5.93 us -> 0.57 us  [grid_potential(): pl.pallas_call(potential_kernel, in_specs=[pl.BlockSpec(memory_space=pltp...]
    ppermute x2, starting transfers between devices: 10.9 us -> 7.57 us  [passed_along(): return lax.ppermute(block, axis, route)]
    all_to_all x1, blocking collectives: 19.8 us -> 22.4 us  [exchanged(): lax.all_to_all(array, GRID_AXES, split_axis=0, concat_axis=0, tiled=True)]
    all_to_all x3, starting transfers between devices: 20.7 us -> 18.7 us  [exchanged(): lax.all_to_all(array, GRID_AXES, split_axis=0, concat_axis=0, tiled=True)]
  transfers between devices with their start and end apart: 5 -> 5, of which waited for: 3 -> 5; matrix products, arithmetic and copies ran while one was open for 0% -> 0% of each run, Pallas kernels for 12% -> 7%
where the time goes in v5:
time: 118 us; the launch traced here: 116 us
  Pallas kernels  39.6 us (34%)
  waiting for transfers between devices  27 us (23%)
  starting transfers between devices  26.2 us (22%)
  blocking collectives  22.4 us (19%)
    all_to_all x1, blocking collectives, exchanged(): lax.all_to_all(array, GRID_AXES, split_axis=0, concat_axis=0, tiled=True)  22.4 us
    all_to_all x3, waiting for transfers between devices, exchanged(): lax.all_to_all(array, GRID_AXES, split_axis=0, concat_axis=0, tiled=True)  21.9 us
    all_to_all x3, starting transfers between devices, exchanged(): lax.all_to_all(array, GRID_AXES, split_axis=0, concat_axis=0, tiled=True)  18.7 us
    pallas_call x1, Pallas kernels, own_orbitals(): pl.pallas_call(orbitals_kernel, in_specs=hbm(5), out_specs=hbm(2), out_sh...  10.6 us
    pallas_call x1, Pallas kernels, searched(): pl.pallas_call(transform_kernel, in_specs=vmem(5) + hbm(1), out_specs=hbm...  9.26 us
    ppermute x2, starting transfers between devices, passed_along(): return lax.ppermute(block, axis, route)  7.57 us
    pallas_call x1, Pallas kernels, corrected(): pl.pallas_call(project_kernel, in_specs=vmem(4) + hbm(1), out_specs=hbm(1...  6.67 us
    pallas_call x1, Pallas kernels, force_parts(): pl.pallas_call(force_kernel, in_specs=[pl.BlockSpec(memory_space=pltpu.SM...  5.76 us
  transfers between devices with their start and end apart: 5, of which 5 were waited for; matrix products, arithmetic and copies ran while one was open for 0% of the time, Pallas kernels for 7%

profile of v5, /device:TPU:67, one launch (start us, length us, event | category | flops | bytes accessed | tf_op | source)
XLA Modules:
  0.0 116.4 jit_solution(6857079550276850055)
XLA Ops:
  0.6 10.6 %orbitals.1 = (bf16[4096,128]{1,0:T(8,128)(2,1)}, f32[4096,128]{1,0:T(8,128)}) custom-call(bf16[1024,256]{1,0:T(8,128)(2,1)} %bitcast.30, bf16[1024,2048]{1,0:T(8,128)(2,1)} %bitcast.25, f32[4]{0:T(128)} %depth_ref.3, s32[3,1,256]{2,1,0:T(1,128)} %bitcast.31, s32[1,256]{1,0:T(1,128)} %bitcast.22), custom_call_target="tpu_custom_call" | custom-call | tf_op jit(solution)/shard_map/orbitals/pallas_call | solution.py:154
  11.3 0.0 copy-start.9
  11.3 0.0 copy-start.5
  11.3 0.0 copy-start.6
  11.3 8.6 %all-to-all-start = ((bf16[32,128,128]{2,1,0:T(8,128)(2,1)}), bf16[32,128,128]{2,1,0:T(8,128)(2,1)S(1)}, u32[]{:S(2)}, u32[]{:S(2)}) async-start(bf16[32,128,128]{2,1,0:T(8,128)(2,1)} %bitcast.29), calls=%async_computation | async-start | bytes 2097152 | tf_op jit(solution)/shard_map/all_to_all | solution.py:714
  19.9 0.0 copy-done.9
  19.9 0.0 copy-done.5
  19.9 0.0 copy-done.6
  20.0 0.0 copy-start.1
  20.0 0.0 copy-start.2
  20.0 0.0 copy-start.3
  20.0 0.0 copy-start.4
  20.0 0.6 potential.1.pot_hbm
  20.6 10.9 %all-to-all-done = bf16[32,128,128]{2,1,0:T(8,128)(2,1)S(1)} async-done(((bf16[32,128,128]{2,1,0:T(8,128)(2,1)}), bf16[32,128,128]{2,1,0:T(8,128)(2,1)S(1)}, u32[]{:S(2)}, u32[]{:S(2)}) %all-to-all-start) | async-done | bytes 1048608 | tf_op jit(solution)/shard_map/all_to_all | solution.py:714
  31.5 0.0 copy-done.1
  31.5 0.0 copy-done.2
  31.5 0.0 copy-done.3
  31.5 0.0 copy-done.4
  31.5 9.3 %transform.1 = (bf16[4096,128]{1,0:T(8,128)(2,1)}, f32[4096,128]{1,0:T(8,128)}, f32[8,128]{1,0:T(8,128)S(1)}) custom-call(bf16[4096,128]{1,0:T(8,128)(2,1)S(1)} %bitcast.15, bf16[128,256]{1,0:T(8,128)(2,1)S(1)} %copy-done.1, bf16[128,64]{1,0:T(8,128)(2,1)S(1)} %copy-done.3, bf16[64,128]{1,0:T(8,128)(2,1)S(1)} %copy-done.4, bf16[256,128]{1,0:T(8,128)(2,1)S(1)} %copy-done.2, ...), custom_call_target="tpu_custom_call" | custom-call | tf_op jit(solution)/shard_map/transform/pallas_call | solution.py:401
  40.8 0.0 copy-start
  40.8 5.3 %all-to-all-start.1 = ((bf16[32,128,128]{2,1,0:T(8,128)(2,1)}), bf16[32,128,128]{2,1,0:T(8,128)(2,1)S(1)}, u32[]{:S(2)}, u32[]{:S(2)}) async-start(bf16[32,128,128]{2,1,0:T(8,128)(2,1)} %bitcast.28), calls=%async_computation.1 | async-start | bytes 2097152 | tf_op jit(solution)/shard_map/all_to_all | solution.py:714
  46.1 0.0 copy-done
  46.1 5.8 %force.1.extra_ref = bf16[32,8,128]{2,1,0:T(8,128)(2,1)S(1)} custom-call(f32[4]{0:T(128)S(1)} %copy-done.6, f32[4096,128]{1,0:T(8,128)S(1)} %copy-done, s32[3,256]{1,0:T(4,128)S(1)} %bitcast.18, s32[1,256]{1,0:T(1,128)S(1)} %bitcast.24, f32[8,128]{1,0:T(8,128)S(1)} %get-tuple-element.25.ritz_ref), custom_call_target="tpu_custom_call" | custom-call | tf_op jit(solution)/shard_map/force/pallas_call | solution.py:476
  51.9 8.3 %all-to-all-done.1 = bf16[32,128,128]{2,1,0:T(8,128)(2,1)S(1)} async-done(((bf16[32,128,128]{2,1,0:T(8,128)(2,1)}), bf16[32,128,128]{2,1,0:T(8,128)(2,1)S(1)}, u32[]{:S(2)}, u32[]{:S(2)}) %all-to-all-start.1) | async-done | bytes 1048608 | tf_op jit(solution)/shard_map/all_to_all | solution.py:714
  60.2 4.2 %intersect.1 = (bf16[32,136,128]{2,1,0:T(8,128)(2,1)S(1)}, bf16[256,2048]{1,0:T(8,128)(2,1)S(1)}) custom-call(bf16[4096,128]{1,0:T(8,128)(2,1)S(1)} %bitcast.16, bf16[32,8,128]{2,1,0:T(8,128)(2,1)S(1)} %force.1.extra_ref, bf16[1024,2048]{1,0:T(8,128)(2,1)} %bitcast.26), custom_call_target="tpu_custom_call" | custom-call | tf_op jit(solution)/shard_map/intersect/pallas_call | solution.py:534
  64.4 22.4 %all_to_all.20.in_ref.first_ref = bf16[32,136,128]{2,1,0:T(8,128)(2,1)S(1)} all-to-all(bf16[32,136,128]{2,1,0:T(8,128)(2,1)S(1)} %get-tuple-element.26), channel_id=1, replica_groups=mesh['img'=8,'band'=8,'pw'=4] {'band','pw'}, dimensions={0} | all-to-all | bytes 2228224 | tf_op jit(solution)/shard_map/all_to_all | solution.py:714
  86.8 0.0 copy-start.7
  86.8 0.0 copy-start.8
  86.8 1.2 %total.1 = bf16[32,136,128]{2,1,0:T(8,128)(2,1)} custom-call(bf16[32,136,128]{2,1,0:T(8,128)(2,1)S(1)} %all_to_all.20.in_ref.first_ref), custom_call_target="tpu_custom_call" | custom-call | tf_op jit(solution)/shard_map/total/pallas_call | solution.py:575
  88.1 4.7 %all-to-all-start.3 = ((bf16[32,136,128]{2,1,0:T(8,128)(2,1)}), bf16[32,136,128]{2,1,0:T(8,128)(2,1)S(1)}, u32[]{:S(2)}, u32[]{:S(2)}) async-start(bf16[32,136,128]{2,1,0:T(8,128)(2,1)} %total.1), calls=%async_computation.3 | async-start | bytes 2228224 | tf_op jit(solution)/shard_map/all_to_all | solution.py:714
  92.8 5.7 %collective-permute-start = (s32[3,256]{1,0:T(4,128)S(1)}, s32[3,256]{1,0:T(4,128)S(1)}, u32[]{:S(2)}, u32[]{:S(2)}) collective-permute-start(s32[3,256]{1,0:T(4,128)S(1)} %bitcast.19), channel_id=1, source_target_pairs={{0,32},{32,64},{64,96},{96,128},{128,160},{160,192},{192,224},{1,3... | collective-permute-start | bytes 9224 | tf_op jit(solution)/shard_map/ppermute | solution.py:720
  98.5 1.9 %collective-permute-start.1 = (s32[3,256]{1,0:T(4,128)S(1)}, s32[3,256]{1,0:T(4,128)S(1)}, u32[]{:S(2)}, u32[]{:S(2)}) collective-permute-start(s32[3,256]{1,0:T(4,128)S(1)} %bitcast.20), channel_id=1, source_target_pairs={{32,0},{64,32},{96,64},{128,96},{160,128},{192,160},{224,192},{33,... | collective-permute-start | bytes 9224 | tf_op jit(solution)/shard_map/ppermute | solution.py:720
  100.4 0.1 pad_add_fusion.image_ref
  100.5 4.3 %collective-permute-done.before_ref = s32[3,256]{1,0:T(4,128)S(1)} collective-permute-done((s32[3,256]{1,0:T(4,128)S(1)}, s32[3,256]{1,0:T(4,128)S(1)}, u32[]{:S(2)}, u32[]{:S(2)}) %collective-permute-start) | collective-permute-done | bytes 3104 | tf_op jit(solution)/shard_map/ppermute | solution.py:720
  104.8 0.8 collective-permute-done.1.after_ref
  105.6 0.0 copy-done.7
  105.6 0.0 copy-done.8
  105.6 1.3 %prepare.1 = (f32[1,256]{1,0:T(1,128)}, f32[3,256]{1,0:T(4,128)S(1)}, f32[3,256]{1,0:T(4,128)S(1)}) custom-call(s32[2]{0:T(128)S(1)} %pad_add_fusion.image_ref, bf16[32,136,128]{2,1,0:T(8,128)(2,1)S(1)} %all_to_all.20.in_ref.first_ref, s32[3,256]{1,0:T(4,128)S(1)} %bitcast.21, s32[3,256]{1,0:T(4,128)S(1)} %collective-permute-done.before_ref, ...), custom_call_target="tpu_custom_call" | custom-call | tf_op jit(solution)/shard_map/prepare/pallas_call | solution.py:625
  106.9 2.7 %all-to-all-done.3.whole_ref = bf16[32,136,128]{2,1,0:T(8,128)(2,1)S(1)} async-done(((bf16[32,136,128]{2,1,0:T(8,128)(2,1)}), bf16[32,136,128]{2,1,0:T(8,128)(2,1)S(1)}, u32[]{:S(2)}, u32[]{:S(2)}) %all-to-all-start.3) | async-done | bytes 1114144 | tf_op jit(solution)/shard_map/all_to_all | solution.py:714
  109.6 6.7 %project.1 = (bf16[256,2048]{1,0:T(8,128)(2,1)}, f32[3,1,256]{2,1,0:T(1,128)}, f32[1,1]{1,0:T(1,128)}) custom-call(bf16[32,136,128]{2,1,0:T(8,128)(2,1)S(1)} %all-to-all-done.3.whole_ref, bf16[256,2048]{1,0:T(8,128)(2,1)S(1)} %get-tuple-element.27.flat_ref, f32[3,256]{1,0:T(4,128)S(1)} %get-tuple-element.32.tangent_ref, ...), custom_call_target="tpu_custom_call" | custom-call | tf_op jit(solution)/shard_map/project/pallas_call | solution.py:692
  (1 shorter events, 0.0 us)
Async XLA Ops:
  11.3 8.7 %copy-start.9 = (s32[1,3,256]{2,0,1:T(1,128)S(1)}, s32[1,3,256]{2,0,1:T(1,128)}, u32[]{:S(2)}) copy-start(s32[1,3,256]{2,0,1:T(1,128)} %param.13) | copy-start | bytes 9220
  11.3 8.7 %copy-start.5 = (s32[256]{0:T(256)S(1)}, s32[256]{0:T(256)}, u32[]{:S(2)}) copy-start(s32[256]{0:T(256)} %param.16) | copy-start | bytes 3076
  11.3 8.7 %copy-start.6 = (f32[4]{0:T(128)S(1)}, f32[4]{0:T(128)}, u32[]{:S(2)}) copy-start(f32[4]{0:T(128)} %depth_ref.3) | copy-start | bytes 52
  11.3 20.2 %all-to-all-start = ((bf16[32,128,128]{2,1,0:T(8,128)(2,1)}), bf16[32,128,128]{2,1,0:T(8,128)(2,1)S(1)}, u32[]{:S(2)}, u32[]{:S(2)}) async-start(bf16[32,128,128]{2,1,0:T(8,128)(2,1)} %bitcast.29), calls=%async_computation | async-start | bytes 2097152 | tf_op jit(solution)/shard_map/all_to_all | solution.py:714
  20.0 11.5 %copy-start.1 = (bf16[128,256]{1,0:T(8,128)(2,1)S(1)}, bf16[128,256]{1,0:T(8,128)(2,1)}, u32[]{:S(2)}) copy-start(bf16[128,256]{1,0:T(8,128)(2,1)} %constant.16.clone.zf_ref) | copy-start | bytes 196612
  20.0 11.5 %copy-start.2 = (bf16[256,128]{1,0:T(8,128)(2,1)S(1)}, bf16[256,128]{1,0:T(8,128)(2,1)}, u32[]{:S(2)}) copy-start(bf16[256,128]{1,0:T(8,128)(2,1)} %constant.19.clone.zi_ref) | copy-start | bytes 196612
  20.0 11.5 %copy-start.3 = (bf16[128,64]{1,0:T(8,128)(2,1)S(1)}, bf16[128,64]{1,0:T(8,128)(2,1)}, u32[]{:S(2)}) copy-start(bf16[128,64]{1,0:T(8,128)(2,1)} %constant.17.clone.left_ref) | copy-start | bytes 49156
  20.0 11.5 %copy-start.4 = (bf16[64,128]{1,0:T(8,128)(2,1)S(1)}, bf16[64,128]{1,0:T(8,128)(2,1)}, u32[]{:S(2)}) copy-start(bf16[64,128]{1,0:T(8,128)(2,1)} %constant.18.clone.left_inv_ref) | copy-start | bytes 49156
  40.8 5.3 %copy-start = (f32[4096,128]{1,0:T(8,128)S(1)}, f32[4096,128]{1,0:T(8,128)}, u32[]{:S(2)}) copy-start(f32[4096,128]{1,0:T(8,128)} %get-tuple-element.24.dens_ref) | copy-start | bytes 6291460
  40.8 19.4 %all-to-all-start.1 = ((bf16[32,128,128]{2,1,0:T(8,128)(2,1)}), bf16[32,128,128]{2,1,0:T(8,128)(2,1)S(1)}, u32[]{:S(2)}, u32[]{:S(2)}) async-start(bf16[32,128,128]{2,1,0:T(8,128)(2,1)} %bitcast.28), calls=%async_computation.1 | async-start | bytes 2097152 | tf_op jit(solution)/shard_map/all_to_all | solution.py:714
  86.8 18.8 %copy-start.7 = (s32[3,256]{1,0:T(4,128)S(1)}, s32[3,256]{1,0:T(4,128)}, u32[]{:S(2)}) copy-start(s32[3,256]{1,0:T(4,128)} %start_ref.1) | copy-start | bytes 9220
  86.8 18.8 %copy-start.8 = (s32[3,256]{1,0:T(4,128)S(1)}, s32[3,256]{1,0:T(4,128)}, u32[]{:S(2)}) copy-start(s32[3,256]{1,0:T(4,128)} %end_ref.1) | copy-start | bytes 9220
  88.1 21.5 %all-to-all-start.3 = ((bf16[32,136,128]{2,1,0:T(8,128)(2,1)}), bf16[32,136,128]{2,1,0:T(8,128)(2,1)S(1)}, u32[]{:S(2)}, u32[]{:S(2)}) async-start(bf16[32,136,128]{2,1,0:T(8,128)(2,1)} %total.1), calls=%async_computation.3 | async-start | bytes 2228224 | tf_op jit(solution)/shard_map/all_to_all | solution.py:714
  92.8 12.0 %collective-permute-start = (s32[3,256]{1,0:T(4,128)S(1)}, s32[3,256]{1,0:T(4,128)S(1)}, u32[]{:S(2)}, u32[]{:S(2)}) collective-permute-start(s32[3,256]{1,0:T(4,128)S(1)} %bitcast.19), channel_id=1, source_target_pairs={{0,32},{32,64},{64,96},{96,128},{128,160},{160,192},{192,224},{1,3... | collective-permute-start | bytes 9224 | tf_op jit(solution)/shard_map/ppermute | solution.py:720
  98.5 7.1 %collective-permute-start.1 = (s32[3,256]{1,0:T(4,128)S(1)}, s32[3,256]{1,0:T(4,128)S(1)}, u32[]{:S(2)}, u32[]{:S(2)}) collective-permute-start(s32[3,256]{1,0:T(4,128)S(1)} %bitcast.20), channel_id=1, source_target_pairs={{32,0},{64,32},{96,64},{128,96},{160,128},{192,160},{224,192},{33,... | collective-permute-start | bytes 9224 | tf_op jit(solution)/shard_map/ppermute | solution.py:720

commit v6 on v5

--- a/solution.py
+++ b/solution.py
@@ -223,7 +223,7 @@
 
 
 def potential_first():
-    return lax.axis_index("img") % 2 == 1
+    return lax.axis_index("img") % 2 == 0
 
 
 def potential_kernel(depth_ref, pos_ref, species_ref, given_hbm, out_hbm, pot_ref, gy_ref, sem):

time: 118 us -> 109 us (0.924); the launches traced: 116 us -> 109 us
  waiting for transfers between devices: 27 us -> 13.1 us
  starting transfers between devices: 26.2 us -> 37 us
  blocking collectives: 22.4 us -> 17 us
    all_to_all x3, waiting for transfers between devices: 21.9 us -> 8.07 us  [exchanged(): lax.all_to_all(array, GRID_AXES, split_axis=0, concat_axis=0, tiled=True)]
    ppermute x2, starting transfers between devices: 7.57 us -> 18.4 us  [passed_along(): return lax.ppermute(block, axis, route)]
    pallas_call x1, Pallas kernels: 0.57 us -> 7.32 us  [grid_potential(): pl.pallas_call(potential_kernel, in_specs=[pl.BlockSpec(memory_space=pltp...]
    pallas_call x1, Pallas kernels: 10.6 us -> 4.58 us  [own_orbitals(): pl.pallas_call(orbitals_kernel, in_specs=hbm(5), out_specs=hbm(2), out_sh...]
    all_to_all x1, blocking collectives: 22.4 us -> 17 us  [exchanged(): lax.all_to_all(array, GRID_AXES, split_axis=0, concat_axis=0, tiled=True)]
  transfers between devices with their start and end apart: 5 -> 5, of which waited for: 5 -> 3; matrix products, arithmetic and copies ran while one was open for 0% -> 0% of each run, Pallas kernels for 7% -> 13%
where the time goes in v6:
time: 109 us
  Pallas kernels  40.3 us (37%)
  starting transfers between devices  37 us (34%)
  blocking collectives  17 us (16%)
  waiting for transfers between devices  13.1 us (12%)
    all_to_all x3, starting transfers between devices, exchanged(): lax.all_to_all(array, GRID_AXES, split_axis=0, concat_axis=0, tiled=True)  18.6 us
    ppermute x2, starting transfers between devices, passed_along(): return lax.ppermute(block, axis, route)  18.4 us
    all_to_all x1, blocking collectives, exchanged(): lax.all_to_all(array, GRID_AXES, split_axis=0, concat_axis=0, tiled=True)  17 us
    pallas_call x1, Pallas kernels, searched(): pl.pallas_call(transform_kernel, in_specs=vmem(5) + hbm(1), out_specs=hbm...  9.26 us
    all_to_all x3, waiting for transfers between devices, exchanged(): lax.all_to_all(array, GRID_AXES, split_axis=0, concat_axis=0, tiled=True)  8.07 us
    pallas_call x1, Pallas kernels, grid_potential(): pl.pallas_call(potential_kernel, in_specs=[pl.BlockSpec(memory_space=pltp...  7.32 us
    pallas_call x1, Pallas kernels, corrected(): pl.pallas_call(project_kernel, in_specs=vmem(4) + hbm(1), out_specs=hbm(1...  6.67 us
    pallas_call x1, Pallas kernels, force_parts(): pl.pallas_call(force_kernel, in_specs=[pl.BlockSpec(memory_space=pltpu.SM...  5.75 us
  transfers between devices with their start and end apart: 5, of which 3 were waited for; matrix products, arithmetic and copies ran while one was open for 0% of the time, Pallas kernels for 13%

profile of v6, /device:TPU:67, one launch (start us, length us, event | category | flops | bytes accessed | tf_op | source)
XLA Modules:
  0.0 108.6 jit_solution(7234525031651052500)
XLA Ops:
  0.6 4.6 %orbitals.1 = (bf16[4096,128]{1,0:T(8,128)(2,1)}, f32[4096,128]{1,0:T(8,128)}) custom-call(bf16[1024,256]{1,0:T(8,128)(2,1)} %bitcast.30, bf16[1024,2048]{1,0:T(8,128)(2,1)} %bitcast.25, f32[4]{0:T(128)} %depth_ref.3, s32[3,1,256]{2,1,0:T(1,128)} %bitcast.31, s32[1,256]{1,0:T(1,128)} %bitcast.22), custom_call_target="tpu_custom_call" | custom-call | tf_op jit(solution)/shard_map/orbitals/pallas_call | solution.py:154
  5.2 0.0 copy-start.9
  5.2 0.0 copy-start.5
  5.2 0.0 copy-start.6
  5.3 8.6 %all-to-all-start = ((bf16[32,128,128]{2,1,0:T(8,128)(2,1)}), bf16[32,128,128]{2,1,0:T(8,128)(2,1)S(1)}, u32[]{:S(2)}, u32[]{:S(2)}) async-start(bf16[32,128,128]{2,1,0:T(8,128)(2,1)} %bitcast.29), calls=%async_computation | async-start | bytes 2097152 | tf_op jit(solution)/shard_map/all_to_all | solution.py:714
  13.8 0.0 copy-done.9
  13.8 0.0 copy-done.5
  13.8 0.0 copy-done.6
  13.9 0.0 copy-start.1
  13.9 0.0 copy-start.2
  13.9 0.0 copy-start.3
  13.9 0.0 copy-start.4
  13.9 7.3 %potential.1.pot_hbm = f32[4096,128]{1,0:T(8,128)} custom-call(f32[4]{0:T(128)S(1)} %copy-done.6, s32[3,256]{1,0:T(4,128)S(1)} %bitcast.17, s32[1,256]{1,0:T(1,128)S(1)} %bitcast.23, f32[4096,128]{1,0:T(8,128)} %get-tuple-element.22.given_hbm), custom_call_target="tpu_custom_call", output_to_operand_aliasing={{}: (3, {})} | custom-call | tf_op jit(solution)/shard_map/potential/pallas_call | solution.py:242
  21.2 3.2 %all-to-all-done = bf16[32,128,128]{2,1,0:T(8,128)(2,1)S(1)} async-done(((bf16[32,128,128]{2,1,0:T(8,128)(2,1)}), bf16[32,128,128]{2,1,0:T(8,128)(2,1)S(1)}, u32[]{:S(2)}, u32[]{:S(2)}) %all-to-all-start) | async-done | bytes 1048608 | tf_op jit(solution)/shard_map/all_to_all | solution.py:714
  24.4 0.0 copy-done.1
  24.4 0.0 copy-done.2
  24.4 0.0 copy-done.3
  24.5 0.0 copy-done.4
  24.5 9.3 %transform.1 = (bf16[4096,128]{1,0:T(8,128)(2,1)}, f32[4096,128]{1,0:T(8,128)}, f32[8,128]{1,0:T(8,128)S(1)}) custom-call(bf16[4096,128]{1,0:T(8,128)(2,1)S(1)} %bitcast.15, bf16[128,256]{1,0:T(8,128)(2,1)S(1)} %copy-done.1, bf16[128,64]{1,0:T(8,128)(2,1)S(1)} %copy-done.3, bf16[64,128]{1,0:T(8,128)(2,1)S(1)} %copy-done.4, bf16[256,128]{1,0:T(8,128)(2,1)S(1)} %copy-done.2, ...), custom_call_target="tpu_custom_call" | custom-call | tf_op jit(solution)/shard_map/transform/pallas_call | solution.py:401
  33.7 0.0 copy-start
  33.7 5.3 %all-to-all-start.1 = ((bf16[32,128,128]{2,1,0:T(8,128)(2,1)}), bf16[32,128,128]{2,1,0:T(8,128)(2,1)S(1)}, u32[]{:S(2)}, u32[]{:S(2)}) async-start(bf16[32,128,128]{2,1,0:T(8,128)(2,1)} %bitcast.28), calls=%async_computation.1 | async-start | bytes 2097152 | tf_op jit(solution)/shard_map/all_to_all | solution.py:714
  39.1 0.0 copy-done
  39.1 5.8 %force.1.extra_ref = bf16[32,8,128]{2,1,0:T(8,128)(2,1)S(1)} custom-call(f32[4]{0:T(128)S(1)} %copy-done.6, f32[4096,128]{1,0:T(8,128)S(1)} %copy-done, s32[3,256]{1,0:T(4,128)S(1)} %bitcast.18, s32[1,256]{1,0:T(1,128)S(1)} %bitcast.24, f32[8,128]{1,0:T(8,128)S(1)} %get-tuple-element.25.ritz_ref), custom_call_target="tpu_custom_call" | custom-call | tf_op jit(solution)/shard_map/force/pallas_call | solution.py:476
  44.8 4.9 %all-to-all-done.1 = bf16[32,128,128]{2,1,0:T(8,128)(2,1)S(1)} async-done(((bf16[32,128,128]{2,1,0:T(8,128)(2,1)}), bf16[32,128,128]{2,1,0:T(8,128)(2,1)S(1)}, u32[]{:S(2)}, u32[]{:S(2)}) %all-to-all-start.1) | async-done | bytes 1048608 | tf_op jit(solution)/shard_map/all_to_all | solution.py:714
  49.7 4.2 %intersect.1 = (bf16[32,136,128]{2,1,0:T(8,128)(2,1)S(1)}, bf16[256,2048]{1,0:T(8,128)(2,1)S(1)}) custom-call(bf16[4096,128]{1,0:T(8,128)(2,1)S(1)} %bitcast.16, bf16[32,8,128]{2,1,0:T(8,128)(2,1)S(1)} %force.1.extra_ref, bf16[1024,2048]{1,0:T(8,128)(2,1)} %bitcast.26), custom_call_target="tpu_custom_call" | custom-call | tf_op jit(solution)/shard_map/intersect/pallas_call | solution.py:534
  53.9 17.0 %all_to_all.20.in_ref.first_ref = bf16[32,136,128]{2,1,0:T(8,128)(2,1)S(1)} all-to-all(bf16[32,136,128]{2,1,0:T(8,128)(2,1)S(1)} %get-tuple-element.26), channel_id=1, replica_groups=mesh['img'=8,'band'=8,'pw'=4] {'band','pw'}, dimensions={0} | all-to-all | bytes 2228224 | tf_op jit(solution)/shard_map/all_to_all | solution.py:714
  70.9 0.0 copy-start.7
  70.9 0.0 copy-start.8
  70.9 1.2 %total.1 = bf16[32,136,128]{2,1,0:T(8,128)(2,1)} custom-call(bf16[32,136,128]{2,1,0:T(8,128)(2,1)S(1)} %all_to_all.20.in_ref.first_ref), custom_call_target="tpu_custom_call" | custom-call | tf_op jit(solution)/shard_map/total/pallas_call | solution.py:575
  72.2 4.8 %all-to-all-start.3 = ((bf16[32,136,128]{2,1,0:T(8,128)(2,1)}), bf16[32,136,128]{2,1,0:T(8,128)(2,1)S(1)}, u32[]{:S(2)}, u32[]{:S(2)}) async-start(bf16[32,136,128]{2,1,0:T(8,128)(2,1)} %total.1), calls=%async_computation.3 | async-start | bytes 2228224 | tf_op jit(solution)/shard_map/all_to_all | solution.py:714
  76.9 16.5 %collective-permute-start = (s32[3,256]{1,0:T(4,128)S(1)}, s32[3,256]{1,0:T(4,128)S(1)}, u32[]{:S(2)}, u32[]{:S(2)}) collective-permute-start(s32[3,256]{1,0:T(4,128)S(1)} %bitcast.19), channel_id=1, source_target_pairs={{0,32},{32,64},{64,96},{96,128},{128,160},{160,192},{192,224},{1,3... | collective-permute-start | bytes 9224 | tf_op jit(solution)/shard_map/ppermute | solution.py:720
  93.4 1.9 %collective-permute-start.1 = (s32[3,256]{1,0:T(4,128)S(1)}, s32[3,256]{1,0:T(4,128)S(1)}, u32[]{:S(2)}, u32[]{:S(2)}) collective-permute-start(s32[3,256]{1,0:T(4,128)S(1)} %bitcast.20), channel_id=1, source_target_pairs={{32,0},{64,32},{96,64},{128,96},{160,128},{192,160},{224,192},{33,... | collective-permute-start | bytes 9224 | tf_op jit(solution)/shard_map/ppermute | solution.py:720
  95.4 0.1 pad_add_fusion.image_ref
  95.4 0.0 collective-permute-done.before_ref
  95.4 5.0 %collective-permute-done.1.after_ref = s32[3,256]{1,0:T(4,128)S(1)} collective-permute-done((s32[3,256]{1,0:T(4,128)S(1)}, s32[3,256]{1,0:T(4,128)S(1)}, u32[]{:S(2)}, u32[]{:S(2)}) %collective-permute-start.1) | collective-permute-done | bytes 3104 | tf_op jit(solution)/shard_map/ppermute | solution.py:720
  100.5 0.0 copy-done.7
  100.5 0.0 copy-done.8
  100.5 1.3 %prepare.1 = (f32[1,256]{1,0:T(1,128)}, f32[3,256]{1,0:T(4,128)S(1)}, f32[3,256]{1,0:T(4,128)S(1)}) custom-call(s32[2]{0:T(128)S(1)} %pad_add_fusion.image_ref, bf16[32,136,128]{2,1,0:T(8,128)(2,1)S(1)} %all_to_all.20.in_ref.first_ref, s32[3,256]{1,0:T(4,128)S(1)} %bitcast.21, s32[3,256]{1,0:T(4,128)S(1)} %collective-permute-done.before_ref, ...), custom_call_target="tpu_custom_call" | custom-call | tf_op jit(solution)/shard_map/prepare/pallas_call | solution.py:625
  101.8 0.0 all-to-all-done.3.whole_ref
  101.8 6.7 %project.1 = (bf16[256,2048]{1,0:T(8,128)(2,1)}, f32[3,1,256]{2,1,0:T(1,128)}, f32[1,1]{1,0:T(1,128)}) custom-call(bf16[32,136,128]{2,1,0:T(8,128)(2,1)S(1)} %all-to-all-done.3.whole_ref, bf16[256,2048]{1,0:T(8,128)(2,1)S(1)} %get-tuple-element.27.flat_ref, f32[3,256]{1,0:T(4,128)S(1)} %get-tuple-element.32.tangent_ref, ...), custom_call_target="tpu_custom_call" | custom-call | tf_op jit(solution)/shard_map/project/pallas_call | solution.py:692
  (1 shorter events, 0.0 us)
Async XLA Ops:
  5.2 8.6 %copy-start.9 = (s32[1,3,256]{2,0,1:T(1,128)S(1)}, s32[1,3,256]{2,0,1:T(1,128)}, u32[]{:S(2)}) copy-start(s32[1,3,256]{2,0,1:T(1,128)} %param.13) | copy-start | bytes 9220
  5.2 8.6 %copy-start.5 = (s32[256]{0:T(256)S(1)}, s32[256]{0:T(256)}, u32[]{:S(2)}) copy-start(s32[256]{0:T(256)} %param.16) | copy-start | bytes 3076
  5.2 8.6 %copy-start.6 = (f32[4]{0:T(128)S(1)}, f32[4]{0:T(128)}, u32[]{:S(2)}) copy-start(f32[4]{0:T(128)} %depth_ref.3) | copy-start | bytes 52
  5.3 19.2 %all-to-all-start = ((bf16[32,128,128]{2,1,0:T(8,128)(2,1)}), bf16[32,128,128]{2,1,0:T(8,128)(2,1)S(1)}, u32[]{:S(2)}, u32[]{:S(2)}) async-start(bf16[32,128,128]{2,1,0:T(8,128)(2,1)} %bitcast.29), calls=%async_computation | async-start | bytes 2097152 | tf_op jit(solution)/shard_map/all_to_all | solution.py:714
  13.9 10.6 %copy-start.1 = (bf16[128,256]{1,0:T(8,128)(2,1)S(1)}, bf16[128,256]{1,0:T(8,128)(2,1)}, u32[]{:S(2)}) copy-start(bf16[128,256]{1,0:T(8,128)(2,1)} %constant.16.clone.zf_ref) | copy-start | bytes 196612
  13.9 10.6 %copy-start.2 = (bf16[256,128]{1,0:T(8,128)(2,1)S(1)}, bf16[256,128]{1,0:T(8,128)(2,1)}, u32[]{:S(2)}) copy-start(bf16[256,128]{1,0:T(8,128)(2,1)} %constant.19.clone.zi_ref) | copy-start | bytes 196612
  13.9 10.6 %copy-start.3 = (bf16[128,64]{1,0:T(8,128)(2,1)S(1)}, bf16[128,64]{1,0:T(8,128)(2,1)}, u32[]{:S(2)}) copy-start(bf16[128,64]{1,0:T(8,128)(2,1)} %constant.17.clone.left_ref) | copy-start | bytes 49156
  13.9 10.6 %copy-start.4 = (bf16[64,128]{1,0:T(8,128)(2,1)S(1)}, bf16[64,128]{1,0:T(8,128)(2,1)}, u32[]{:S(2)}) copy-start(bf16[64,128]{1,0:T(8,128)(2,1)} %constant.18.clone.left_inv_ref) | copy-start | bytes 49156
  33.7 5.3 %copy-start = (f32[4096,128]{1,0:T(8,128)S(1)}, f32[4096,128]{1,0:T(8,128)}, u32[]{:S(2)}) copy-start(f32[4096,128]{1,0:T(8,128)} %get-tuple-element.24.dens_ref) | copy-start | bytes 6291460
  33.7 16.0 %all-to-all-start.1 = ((bf16[32,128,128]{2,1,0:T(8,128)(2,1)}), bf16[32,128,128]{2,1,0:T(8,128)(2,1)S(1)}, u32[]{:S(2)}, u32[]{:S(2)}) async-start(bf16[32,128,128]{2,1,0:T(8,128)(2,1)} %bitcast.28), calls=%async_computation.1 | async-start | bytes 2097152 | tf_op jit(solution)/shard_map/all_to_all | solution.py:714
  70.9 29.5 %copy-start.7 = (s32[3,256]{1,0:T(4,128)S(1)}, s32[3,256]{1,0:T(4,128)}, u32[]{:S(2)}) copy-start(s32[3,256]{1,0:T(4,128)} %start_ref.1) | copy-start | bytes 9220
  70.9 29.5 %copy-start.8 = (s32[3,256]{1,0:T(4,128)S(1)}, s32[3,256]{1,0:T(4,128)}, u32[]{:S(2)}) copy-start(s32[3,256]{1,0:T(4,128)} %end_ref.1) | copy-start | bytes 9220
  72.2 29.6 %all-to-all-start.3 = ((bf16[32,136,128]{2,1,0:T(8,128)(2,1)}), bf16[32,136,128]{2,1,0:T(8,128)(2,1)S(1)}, u32[]{:S(2)}, u32[]{:S(2)}) async-start(bf16[32,136,128]{2,1,0:T(8,128)(2,1)} %total.1), calls=%async_computation.3 | async-start | bytes 2228224 | tf_op jit(solution)/shard_map/all_to_all | solution.py:714
  76.9 18.5 %collective-permute-start = (s32[3,256]{1,0:T(4,128)S(1)}, s32[3,256]{1,0:T(4,128)S(1)}, u32[]{:S(2)}, u32[]{:S(2)}) collective-permute-start(s32[3,256]{1,0:T(4,128)S(1)} %bitcast.19), channel_id=1, source_target_pairs={{0,32},{32,64},{64,96},{96,128},{128,160},{160,192},{192,224},{1,3... | collective-permute-start | bytes 9224 | tf_op jit(solution)/shard_map/ppermute | solution.py:720
  93.4 7.0 %collective-permute-start.1 = (s32[3,256]{1,0:T(4,128)S(1)}, s32[3,256]{1,0:T(4,128)S(1)}, u32[]{:S(2)}, u32[]{:S(2)}) collective-permute-start(s32[3,256]{1,0:T(4,128)S(1)} %bitcast.20), channel_id=1, source_target_pairs={{32,0},{64,32},{96,64},{128,96},{160,128},{192,160},{224,192},{33,... | collective-permute-start | bytes 9224 | tf_op jit(solution)/shard_map/ppermute | solution.py:720

commit v7 on v6

--- a/solution.py
+++ b/solution.py
@@ -25,6 +25,9 @@
 CHUNKS = 2
 FETCHES = 2
 LINE = W + 1
+SHARES = 8
+EARLY = 4
+EARLY_ROWS = G * G * EARLY // SHARES
 
 kinetic_scale = 0.01
 sigma_cells = 3.0
@@ -96,7 +99,8 @@
     turned.start()
     for k in range(CHUNKS):
         fetch(k).start()
-    keep = pltpu.make_async_copy(pot_ref, pot_hbm, small_sems.at[3])
+    ahead = pl.ds(0, EARLY_ROWS)
+    keep = pltpu.make_async_copy(pot_ref.at[ahead], pot_hbm.at[ahead], small_sems.at[3])
 
     @pl.when(potential_first())
     def _():
@@ -111,7 +115,7 @@
         for copy in small:
             copy.wait()
         places = [pos_ref[k] for k in range(3)]
-        write_potential(depth_ref, places, species_ref[...], pot_ref, gy_ref)
+        write_potential(depth_ref, places, species_ref[...], pot_ref, gy_ref, 0, EARLY)
         keep.start()
 
     source, target = iota((256, 256), 0), iota((256, 256), 1)
@@ -200,14 +204,14 @@
     return strength
 
 
-def write_potential(depth_ref, places, species, out_ref, gy_ref):
+def write_potential(depth_ref, places, species, out_ref, gy_ref, begin, end):
     strength = strengths(species, depth_ref)
     gauss_x, _ = gaussian(places[0], G)
     gauss_x = gauss_x * strength
     gy_ref[...], _ = gaussian(places[1], G)
     gauss_z, _ = gaussian(places[2], 2 * G)
     z_high, z_low = split_two(gauss_z)
-    per = 8
+    per = G // SHARES
 
     def some(i, carry):
         for k in range(per):
@@ -219,7 +223,7 @@
             )
         return carry
 
-    lax.fori_loop(0, G // per, some, 0)
+    lax.fori_loop(begin, end, some, 0)
 
 
 def potential_first():
@@ -228,14 +232,21 @@
 
 def potential_kernel(depth_ref, pos_ref, species_ref, given_hbm, out_hbm, pot_ref, gy_ref, sem):
     del given_hbm
-
-    @pl.when(jnp.logical_not(potential_first()))
+    first = potential_first()
+    places = [pos_ref[k : k + 1, :] for k in range(3)]
+    begin = jnp.where(first, EARLY, 0)
+    write_potential(depth_ref, places, species_ref[...], pot_ref, gy_ref, begin, SHARES)
+    ahead, late = pl.ds(0, EARLY_ROWS), pl.ds(EARLY_ROWS, G * G - EARLY_ROWS)
+    keep_late = pltpu.make_async_copy(pot_ref.at[late], out_hbm.at[late], sem.at[0])
+    keep_late.start()
+
+    @pl.when(jnp.logical_not(first))
     def _():
-        places = [pos_ref[k : k + 1, :] for k in range(3)]
-        write_potential(depth_ref, places, species_ref[...], pot_ref, gy_ref)
-        keep = pltpu.make_async_copy(pot_ref, out_hbm, sem)
+        keep = pltpu.make_async_copy(pot_ref.at[ahead], out_hbm.at[ahead], sem.at[1])
         keep.start()
         keep.wait()
+
+    keep_late.wait()
 
 
 def grid_potential(depth, pos, species, given):
@@ -248,7 +259,7 @@
         scratch_shapes=[
             pltpu.VMEM((G * G, 128), f32),
             pltpu.VMEM((G, 256), f32),
-            pltpu.SemaphoreType.DMA,
+            pltpu.SemaphoreType.DMA((2,)),
         ],
         compiler_params=pltpu.CompilerParams(vmem_limit_bytes=12 << 20),
         name="potential",
@@ -594,50 +605,27 @@
     return jnp.sum(here, 0, keepdims=True)
 
 
-def prepare_kernel(
-    image_ref, first_ref, pos_ref, before_ref, after_ref, start_ref, end_ref,
-    ritz_ref, tangent_ref, spring_ref,
-):
+def prepare_kernel(first_ref, order_ref, ritz_ref):
+    del order_ref
     column, at = iota((128, 256), 1), iota((PEERS * 8, 256), 1)
     ritz_ref[...] = row_of(
         first_ref, 128, 32 + OWN * (column // HALF) + column % OWN, at % HALF // OWN
     )
-    pos = pos_ref[...]
-    image = image_ref[0]
-    before = jnp.where(image == 0, start_ref[...], before_ref[...])
-    after = jnp.where(image == image_ref[1] - 1, end_ref[...], after_ref[...])
-    ahead = wrap_offset(after - pos).astype(f32)
-    behind = wrap_offset(pos - before).astype(f32)
-    raw = ahead + behind
-    entries = pos.shape[0] * pos.shape[1]
-
-    def mean_square(value):
-        return jnp.sum(jnp.sum(value * value, 1, keepdims=True), 0, keepdims=True) / entries
-
-    tangent = raw * lax.rsqrt(mean_square(raw) + epsilon) * (1.0 / math.sqrt(entries))
-    length_ahead = jnp.sqrt(entries * (mean_square(ahead) + epsilon))
-    length_behind = jnp.sqrt(entries * (mean_square(behind) + epsilon))
-    tangent_ref[...] = tangent
-    spring_ref[...] = spring_constant * (length_ahead - length_behind) * tangent
-
-
-def prepared(image, arrived, pos, before, after, start_pos, end_pos):
+
+
+def prepared(arrived, order):
     return pl.pallas_call(
         prepare_kernel,
-        in_specs=[pl.BlockSpec(memory_space=pltpu.SMEM)] + vmem(6),
-        out_specs=vmem(3),
-        out_shape=[
-            jax.ShapeDtypeStruct((1, 256), f32),
-            jax.ShapeDtypeStruct((3, 256), f32),
-            jax.ShapeDtypeStruct((3, 256), f32),
-        ],
+        in_specs=vmem(1) + hbm(1),
+        out_specs=vmem(1)[0],
+        out_shape=jax.ShapeDtypeStruct((1, 256), f32),
         compiler_params=pltpu.CompilerParams(vmem_limit_bytes=6 << 20),
         name="prepare",
-    )(image, arrived, pos, before, after, start_pos, end_pos)
+    )(arrived, in_hbm(order))
 
 
 def project_kernel(
-    whole_ref, flat_ref, tangent_ref, spring_ref, coeff_hbm,
+    image_ref, whole_ref, flat_ref, pos_ref, before_ref, after_ref, start_ref, end_ref, coeff_hbm,
     out_hbm, push_ref, along_ref, coeff_ref, inter_ref, done_ref, sems, fetch_sems,
 ):
     wide = 2048 // FETCHES
@@ -661,12 +649,27 @@
         return pltpu.make_async_copy(done_ref.at[:, at], out_hbm.at[:, at], sems.at[k])
 
     column, at = iota((128, 256), 1), iota((PEERS * 8, 256), 1)
-    tangent = tangent_ref[...]
+    pos = pos_ref[...]
+    image = image_ref[0]
+    before = jnp.where(image == 0, start_ref[...], before_ref[...])
+    after = jnp.where(image == image_ref[1] - 1, end_ref[...], after_ref[...])
+    ahead = wrap_offset(after - pos).astype(f32)
+    behind = wrap_offset(pos - before).astype(f32)
+    raw = ahead + behind
+    entries = pos.shape[0] * pos.shape[1]
+
+    def mean_square(value):
+        return jnp.sum(jnp.sum(value * value, 1, keepdims=True), 0, keepdims=True) / entries
+
+    tangent = raw * lax.rsqrt(mean_square(raw) + epsilon) * (1.0 / math.sqrt(entries))
+    length_ahead = jnp.sqrt(entries * (mean_square(ahead) + epsilon))
+    length_behind = jnp.sqrt(entries * (mean_square(behind) + epsilon))
+    spring = spring_constant * (length_ahead - length_behind) * tangent
     force = jnp.concatenate(
         [row_of(whole_ref, 128, 8 * alpha + (column & 7), at >> 3) for alpha in range(3)], 0
     )
     along = jnp.sum(jnp.sum(force * tangent, 1, keepdims=True), 0, keepdims=True)
-    push = force - along * tangent + spring_ref[...]
+    push = force - along * tangent + spring
     for alpha in range(3):
         push_ref[alpha] = push[alpha : alpha + 1]
     along_ref[...] = along
@@ -688,10 +691,10 @@
         send(k).wait()
 
 
-def corrected(whole, flat, tangent, spring, coeff):
+def corrected(image, whole, flat, pos, before, after, start_pos, end_pos, coeff):
     return pl.pallas_call(
         project_kernel,
-        in_specs=vmem(4) + hbm(1),
+        in_specs=[pl.BlockSpec(memory_space=pltpu.SMEM)] + vmem(7) + hbm(1),
         out_specs=hbm(1) + vmem(2),
         out_shape=[
             pltpu.HBM((BLOCK, 2048), bf16),
@@ -707,7 +710,7 @@
         ],
         compiler_params=pltpu.CompilerParams(vmem_limit_bytes=16 << 20),
         name="project",
-    )(whole, flat, tangent, spring, in_hbm(coeff))
+    )(image, whole, flat, pos, before, after, start_pos, end_pos, in_hbm(coeff))
 
 
 def exchanged(array):
@@ -740,11 +743,10 @@
     after = passed_along(later, "img", -1)
     whole = exchanged(mine)
     image = jnp.stack([lax.axis_index("img"), lax.axis_size("img")]).astype(jnp.int32)
-    arrived, before, after = lax.optimization_barrier((arrived, before, after, mine))[:3]
-    ritz_values, tangent, spring = prepared(
-        image, arrived, pos, before, after, start_pos, end_pos
+    ritz_values = prepared(arrived, mine)
+    correction, push, along = corrected(
+        image, whole, flat, pos, before, after, start_pos, end_pos, coeff
     )
-    correction, push, along = corrected(whole, flat, tangent, spring, coeff)
     return (
         correction.reshape(1, BLOCK, 1, 2048),
         ritz_values,

time: 109 us -> 108 us (level)
  starting transfers between devices: 37 us -> 33.1 us
  blocking collectives: 17 us -> 19.9 us
    ppermute x2, starting transfers between devices: 18.4 us -> 12 us  [passed_along(): return lax.ppermute(block, axis, route)]
    all_to_all x1, blocking collectives: 17 us -> 19.9 us  [exchanged(): lax.all_to_all(array, GRID_AXES, split_axis=0, concat_axis=0, tiled=True)]
    all_to_all x3, starting transfers between devices: 18.6 us -> 21.1 us  [exchanged(): lax.all_to_all(array, GRID_AXES, split_axis=0, concat_axis=0, tiled=True)]
where the time goes in v7:
time: 108 us; the launch traced here: 107 us
  Pallas kernels  40.1 us (37%)
  starting transfers between devices  33.1 us (31%)
  blocking collectives  19.9 us (18%)
  waiting for transfers between devices  13.1 us (12%)
    all_to_all x3, starting transfers between devices, exchanged(): lax.all_to_all(array, GRID_AXES, split_axis=0, concat_axis=0, tiled=True)  21.1 us
    all_to_all x1, blocking collectives, exchanged(): lax.all_to_all(array, GRID_AXES, split_axis=0, concat_axis=0, tiled=True)  19.9 us
    ppermute x2, starting transfers between devices, passed_along(): return lax.ppermute(block, axis, route)  12 us
    pallas_call x1, Pallas kernels, searched(): pl.pallas_call(transform_kernel, in_specs=vmem(5) + hbm(1), out_specs=hbm...  9.28 us
    all_to_all x3, waiting for transfers between devices, exchanged(): lax.all_to_all(array, GRID_AXES, split_axis=0, concat_axis=0, tiled=True)  8.8 us
    pallas_call x1, Pallas kernels, grid_potential(): pl.pallas_call(potential_kernel, in_specs=[pl.BlockSpec(memory_space=pltp...  7.29 us
    pallas_call x1, Pallas kernels, corrected(): pl.pallas_call(project_kernel, in_specs=[pl.BlockSpec(memory_space=pltpu....  6.99 us
    pallas_call x1, Pallas kernels, force_parts(): pl.pallas_call(force_kernel, in_specs=[pl.BlockSpec(memory_space=pltpu.SM...  5.76 us
  transfers between devices with their start and end apart: 5, of which 3 were waited for; matrix products, arithmetic and copies ran while one was open for 0% of the time, Pallas kernels for 13%

profile of v7, /device:TPU:67, one launch (start us, length us, event | category | flops | bytes accessed | tf_op | source)
XLA Modules:
  0.0 107.3 jit_solution(3697164749833416564)
XLA Ops:
  0.6 4.6 %orbitals.1 = (bf16[4096,128]{1,0:T(8,128)(2,1)}, f32[4096,128]{1,0:T(8,128)}) custom-call(bf16[1024,256]{1,0:T(8,128)(2,1)} %bitcast.30, bf16[1024,2048]{1,0:T(8,128)(2,1)} %bitcast.25, f32[4]{0:T(128)} %depth_ref.3, s32[3,1,256]{2,1,0:T(1,128)} %bitcast.31, s32[1,256]{1,0:T(1,128)} %bitcast.22), custom_call_target="tpu_custom_call" | custom-call | tf_op jit(solution)/shard_map/orbitals/pallas_call | solution.py:158
  5.2 0.0 copy-start.9
  5.2 0.0 copy-start.5
  5.2 0.0 copy-start.6
  5.3 8.6 %all-to-all-start = ((bf16[32,128,128]{2,1,0:T(8,128)(2,1)}), bf16[32,128,128]{2,1,0:T(8,128)(2,1)S(1)}, u32[]{:S(2)}, u32[]{:S(2)}) async-start(bf16[32,128,128]{2,1,0:T(8,128)(2,1)} %bitcast.29), calls=%async_computation | async-start | bytes 2097152 | tf_op jit(solution)/shard_map/all_to_all | solution.py:717
  13.8 0.0 copy-done.9
  13.8 0.0 copy-done.5
  13.8 0.0 copy-done.6
  13.9 0.0 copy-start.1
  13.9 0.0 copy-start.2
  13.9 0.0 copy-start.3
  13.9 0.0 copy-start.4
  13.9 7.3 %potential.1.pot_hbm = f32[4096,128]{1,0:T(8,128)} custom-call(f32[4]{0:T(128)S(1)} %copy-done.6, s32[3,256]{1,0:T(4,128)S(1)} %bitcast.17, s32[1,256]{1,0:T(1,128)S(1)} %bitcast.23, f32[4096,128]{1,0:T(8,128)} %get-tuple-element.16.given_hbm), custom_call_target="tpu_custom_call", output_to_operand_aliasing={{}: (3, {})} | custom-call | tf_op jit(solution)/shard_map/potential/pallas_call | solution.py:253
  21.2 3.6 %all-to-all-done = bf16[32,128,128]{2,1,0:T(8,128)(2,1)S(1)} async-done(((bf16[32,128,128]{2,1,0:T(8,128)(2,1)}), bf16[32,128,128]{2,1,0:T(8,128)(2,1)S(1)}, u32[]{:S(2)}, u32[]{:S(2)}) %all-to-all-start) | async-done | bytes 1048608 | tf_op jit(solution)/shard_map/all_to_all | solution.py:717
  24.8 0.0 copy-done.1
  24.8 0.0 copy-done.2
  24.8 0.0 copy-done.3
  24.8 0.0 copy-done.4
  24.8 9.3 %transform.1 = (bf16[4096,128]{1,0:T(8,128)(2,1)}, f32[4096,128]{1,0:T(8,128)}, f32[8,128]{1,0:T(8,128)S(1)}) custom-call(bf16[4096,128]{1,0:T(8,128)(2,1)S(1)} %bitcast.15, bf16[128,256]{1,0:T(8,128)(2,1)S(1)} %copy-done.1, bf16[128,64]{1,0:T(8,128)(2,1)S(1)} %copy-done.3, bf16[64,128]{1,0:T(8,128)(2,1)S(1)} %copy-done.4, bf16[256,128]{1,0:T(8,128)(2,1)S(1)} %copy-done.2, ...), custom_call_target="tpu_custom_call" | custom-call | tf_op jit(solution)/shard_map/transform/pallas_call | solution.py:412
  34.1 0.0 copy-start
  34.1 7.0 %all-to-all-start.1 = ((bf16[32,128,128]{2,1,0:T(8,128)(2,1)}), bf16[32,128,128]{2,1,0:T(8,128)(2,1)S(1)}, u32[]{:S(2)}, u32[]{:S(2)}) async-start(bf16[32,128,128]{2,1,0:T(8,128)(2,1)} %bitcast.28), calls=%async_computation.1 | async-start | bytes 2097152 | tf_op jit(solution)/shard_map/all_to_all | solution.py:717
  41.1 0.0 copy-done
  41.1 5.8 %force.1.extra_ref = bf16[32,8,128]{2,1,0:T(8,128)(2,1)S(1)} custom-call(f32[4]{0:T(128)S(1)} %copy-done.6, f32[4096,128]{1,0:T(8,128)S(1)} %copy-done, s32[3,256]{1,0:T(4,128)S(1)} %bitcast.18, s32[1,256]{1,0:T(1,128)S(1)} %bitcast.24, f32[8,128]{1,0:T(8,128)S(1)} %get-tuple-element.19.ritz_ref), custom_call_target="tpu_custom_call" | custom-call | tf_op jit(solution)/shard_map/force/pallas_call | solution.py:487
  46.9 5.2 %all-to-all-done.1 = bf16[32,128,128]{2,1,0:T(8,128)(2,1)S(1)} async-done(((bf16[32,128,128]{2,1,0:T(8,128)(2,1)}), bf16[32,128,128]{2,1,0:T(8,128)(2,1)S(1)}, u32[]{:S(2)}, u32[]{:S(2)}) %all-to-all-start.1) | async-done | bytes 1048608 | tf_op jit(solution)/shard_map/all_to_all | solution.py:717
  52.1 4.2 %intersect.1 = (bf16[32,136,128]{2,1,0:T(8,128)(2,1)S(1)}, bf16[256,2048]{1,0:T(8,128)(2,1)S(1)}) custom-call(bf16[4096,128]{1,0:T(8,128)(2,1)S(1)} %bitcast.16, bf16[32,8,128]{2,1,0:T(8,128)(2,1)S(1)} %force.1.extra_ref, bf16[1024,2048]{1,0:T(8,128)(2,1)} %bitcast.26), custom_call_target="tpu_custom_call" | custom-call | tf_op jit(solution)/shard_map/intersect/pallas_call | solution.py:545
  56.3 19.9 %all_to_all.20.in_ref.first_ref = bf16[32,136,128]{2,1,0:T(8,128)(2,1)S(1)} all-to-all(bf16[32,136,128]{2,1,0:T(8,128)(2,1)S(1)} %get-tuple-element.20), channel_id=1, replica_groups=mesh['img'=8,'band'=8,'pw'=4] {'band','pw'}, dimensions={0} | all-to-all | bytes 2228224 | tf_op jit(solution)/shard_map/all_to_all | solution.py:717
  76.2 1.2 %total.1.order_ref = bf16[32,136,128]{2,1,0:T(8,128)(2,1)} custom-call(bf16[32,136,128]{2,1,0:T(8,128)(2,1)S(1)} %all_to_all.20.in_ref.first_ref), custom_call_target="tpu_custom_call" | custom-call | tf_op jit(solution)/shard_map/total/pallas_call | solution.py:586
  77.4 0.0 copy-start.7
  77.4 0.0 copy-start.8
  77.4 5.6 %all-to-all-start.3 = ((bf16[32,136,128]{2,1,0:T(8,128)(2,1)}), bf16[32,136,128]{2,1,0:T(8,128)(2,1)S(1)}, u32[]{:S(2)}, u32[]{:S(2)}) async-start(bf16[32,136,128]{2,1,0:T(8,128)(2,1)} %total.1.order_ref), calls=%async_computation.3 | async-start | bytes 2228224 | tf_op jit(solution)/shard_map/all_to_all | solution.py:717
  83.0 10.1 %collective-permute-start = (s32[3,256]{1,0:T(4,128)S(1)}, s32[3,256]{1,0:T(4,128)S(1)}, u32[]{:S(2)}, u32[]{:S(2)}) collective-permute-start(s32[3,256]{1,0:T(4,128)S(1)} %bitcast.19), channel_id=1, source_target_pairs={{0,32},{32,64},{64,96},{96,128},{128,160},{160,192},{192,224},{1,3... | collective-permute-start | bytes 9224 | tf_op jit(solution)/shard_map/ppermute | solution.py:723
  93.1 1.9 %collective-permute-start.1 = (s32[3,256]{1,0:T(4,128)S(1)}, s32[3,256]{1,0:T(4,128)S(1)}, u32[]{:S(2)}, u32[]{:S(2)}) collective-permute-start(s32[3,256]{1,0:T(4,128)S(1)} %bitcast.20), channel_id=1, source_target_pairs={{32,0},{64,32},{96,64},{128,96},{160,128},{192,160},{224,192},{33,... | collective-permute-start | bytes 9224 | tf_op jit(solution)/shard_map/ppermute | solution.py:723
  95.0 0.1 pad_add_fusion.image_ref
  95.1 0.8 prepare.1
  95.9 0.0 collective-permute-done.before_ref
  95.9 4.3 %collective-permute-done.1.after_ref = s32[3,256]{1,0:T(4,128)S(1)} collective-permute-done((s32[3,256]{1,0:T(4,128)S(1)}, s32[3,256]{1,0:T(4,128)S(1)}, u32[]{:S(2)}, u32[]{:S(2)}) %collective-permute-start.1) | collective-permute-done | bytes 3104 | tf_op jit(solution)/shard_map/ppermute | solution.py:723
  100.1 0.0 all-to-all-done.3.whole_ref
  100.1 0.0 copy-done.7
  100.1 0.0 copy-done.8
  100.1 7.0 %project.1 = (bf16[256,2048]{1,0:T(8,128)(2,1)}, f32[3,1,256]{2,1,0:T(1,128)}, f32[1,1]{1,0:T(1,128)}) custom-call(s32[2]{0:T(128)S(1)} %pad_add_fusion.image_ref, bf16[32,136,128]{2,1,0:T(8,128)(2,1)S(1)} %all-to-all-done.3.whole_ref, bf16[256,2048]{1,0:T(8,128)(2,1)S(1)} %get-tuple-element.21.flat_ref, s32[3,256]{1,0:T(4,128)S(1)} %bitcast.21, ...), custom_call_target="tpu_custom_call" | custom-call | tf_op jit(solution)/shard_map/project/pallas_call | solution.py:695
  (1 shorter events, 0.0 us)
Async XLA Ops:
  5.2 8.6 %copy-start.9 = (s32[1,3,256]{2,0,1:T(1,128)S(1)}, s32[1,3,256]{2,0,1:T(1,128)}, u32[]{:S(2)}) copy-start(s32[1,3,256]{2,0,1:T(1,128)} %param.13) | copy-start | bytes 9220
  5.2 8.6 %copy-start.5 = (s32[256]{0:T(256)S(1)}, s32[256]{0:T(256)}, u32[]{:S(2)}) copy-start(s32[256]{0:T(256)} %param.16) | copy-start | bytes 3076
  5.2 8.6 %copy-start.6 = (f32[4]{0:T(128)S(1)}, f32[4]{0:T(128)}, u32[]{:S(2)}) copy-start(f32[4]{0:T(128)} %depth_ref.3) | copy-start | bytes 52
  5.3 19.5 %all-to-all-start = ((bf16[32,128,128]{2,1,0:T(8,128)(2,1)}), bf16[32,128,128]{2,1,0:T(8,128)(2,1)S(1)}, u32[]{:S(2)}, u32[]{:S(2)}) async-start(bf16[32,128,128]{2,1,0:T(8,128)(2,1)} %bitcast.29), calls=%async_computation | async-start | bytes 2097152 | tf_op jit(solution)/shard_map/all_to_all | solution.py:717
  13.9 10.9 %copy-start.1 = (bf16[128,256]{1,0:T(8,128)(2,1)S(1)}, bf16[128,256]{1,0:T(8,128)(2,1)}, u32[]{:S(2)}) copy-start(bf16[128,256]{1,0:T(8,128)(2,1)} %constant.16.clone.zf_ref) | copy-start | bytes 196612
  13.9 10.9 %copy-start.2 = (bf16[256,128]{1,0:T(8,128)(2,1)S(1)}, bf16[256,128]{1,0:T(8,128)(2,1)}, u32[]{:S(2)}) copy-start(bf16[256,128]{1,0:T(8,128)(2,1)} %constant.19.clone.zi_ref) | copy-start | bytes 196612
  13.9 10.9 %copy-start.3 = (bf16[128,64]{1,0:T(8,128)(2,1)S(1)}, bf16[128,64]{1,0:T(8,128)(2,1)}, u32[]{:S(2)}) copy-start(bf16[128,64]{1,0:T(8,128)(2,1)} %constant.17.clone.left_ref) | copy-start | bytes 49156
  13.9 10.9 %copy-start.4 = (bf16[64,128]{1,0:T(8,128)(2,1)S(1)}, bf16[64,128]{1,0:T(8,128)(2,1)}, u32[]{:S(2)}) copy-start(bf16[64,128]{1,0:T(8,128)(2,1)} %constant.18.clone.left_inv_ref) | copy-start | bytes 49156
  34.1 7.0 %copy-start = (f32[4096,128]{1,0:T(8,128)S(1)}, f32[4096,128]{1,0:T(8,128)}, u32[]{:S(2)}) copy-start(f32[4096,128]{1,0:T(8,128)} %get-tuple-element.18.dens_ref) | copy-start | bytes 6291460
  34.1 18.0 %all-to-all-start.1 = ((bf16[32,128,128]{2,1,0:T(8,128)(2,1)}), bf16[32,128,128]{2,1,0:T(8,128)(2,1)S(1)}, u32[]{:S(2)}, u32[]{:S(2)}) async-start(bf16[32,128,128]{2,1,0:T(8,128)(2,1)} %bitcast.28), calls=%async_computation.1 | async-start | bytes 2097152 | tf_op jit(solution)/shard_map/all_to_all | solution.py:717
  77.4 22.7 %copy-start.7 = (s32[3,256]{1,0:T(4,128)S(1)}, s32[3,256]{1,0:T(4,128)}, u32[]{:S(2)}) copy-start(s32[3,256]{1,0:T(4,128)} %start_ref.1) | copy-start | bytes 9220
  77.4 22.7 %copy-start.8 = (s32[3,256]{1,0:T(4,128)S(1)}, s32[3,256]{1,0:T(4,128)}, u32[]{:S(2)}) copy-start(s32[3,256]{1,0:T(4,128)} %end_ref.1) | copy-start | bytes 9220
  77.4 22.7 %all-to-all-start.3 = ((bf16[32,136,128]{2,1,0:T(8,128)(2,1)}), bf16[32,136,128]{2,1,0:T(8,128)(2,1)S(1)}, u32[]{:S(2)}, u32[]{:S(2)}) async-start(bf16[32,136,128]{2,1,0:T(8,128)(2,1)} %total.1.order_ref), calls=%async_computation.3 | async-start | bytes 2228224 | tf_op jit(solution)/shard_map/all_to_all | solution.py:717
  83.0 12.9 %collective-permute-start = (s32[3,256]{1,0:T(4,128)S(1)}, s32[3,256]{1,0:T(4,128)S(1)}, u32[]{:S(2)}, u32[]{:S(2)}) collective-permute-start(s32[3,256]{1,0:T(4,128)S(1)} %bitcast.19), channel_id=1, source_target_pairs={{0,32},{32,64},{64,96},{96,128},{128,160},{160,192},{192,224},{1,3... | collective-permute-start | bytes 9224 | tf_op jit(solution)/shard_map/ppermute | solution.py:723
  93.1 7.0 %collective-permute-start.1 = (s32[3,256]{1,0:T(4,128)S(1)}, s32[3,256]{1,0:T(4,128)S(1)}, u32[]{:S(2)}, u32[]{:S(2)}) collective-permute-start(s32[3,256]{1,0:T(4,128)S(1)} %bitcast.20), channel_id=1, source_target_pairs={{32,0},{64,32},{96,64},{128,96},{160,128},{192,160},{224,192},{33,... | collective-permute-start | bytes 9224 | tf_op jit(solution)/shard_map/ppermute | solution.py:723

commit v8 on v7

--- a/solution.py
+++ b/solution.py
@@ -25,6 +25,7 @@
 CHUNKS = 2
 FETCHES = 2
 LINE = W + 1
+NEAR = 512
 SHARES = 8
 EARLY = 4
 EARLY_ROWS = G * G * EARLY // SHARES
@@ -181,6 +182,25 @@
 
 def in_hbm(array):
     return pltpu.with_memory_space_constraint(array, pltpu.HBM)
+
+
+def near_kernel(coeff_hbm, order_hbm, out_ref, sem):
+    del order_hbm
+    fetch = pltpu.make_async_copy(coeff_hbm.at[:, pl.ds(0, NEAR)], out_ref, sem)
+    fetch.start()
+    fetch.wait()
+
+
+def brought_near(coeff, order):
+    return pl.pallas_call(
+        near_kernel,
+        in_specs=hbm(2),
+        out_specs=vmem(1)[0],
+        out_shape=jax.ShapeDtypeStruct((BANDS, NEAR), bf16),
+        scratch_shapes=[pltpu.SemaphoreType.DMA],
+        compiler_params=pltpu.CompilerParams(vmem_limit_bytes=1 << 20),
+        name="near",
+    )(in_hbm(coeff), in_hbm(order))
 
 
 def hbm(count):
@@ -625,17 +645,14 @@
 
 
 def project_kernel(
-    image_ref, whole_ref, flat_ref, pos_ref, before_ref, after_ref, start_ref, end_ref, coeff_hbm,
-    out_hbm, push_ref, along_ref, coeff_ref, inter_ref, done_ref, sems, fetch_sems,
+    image_ref, whole_ref, near_ref, pos_ref, before_ref, after_ref, start_ref, end_ref, coeff_hbm,
+    flat_hbm, out_hbm, push_ref, along_ref,
+    rest_ref, flat_ref, inter_ref, part_ref, done_ref, sems, fetch_sems,
 ):
-    wide = 2048 // FETCHES
-
-    def fetch(k):
-        at = pl.ds(k * wide, wide)
-        return pltpu.make_async_copy(coeff_hbm.at[:, at], coeff_ref.at[:, at], fetch_sems.at[k])
-
-    for k in range(FETCHES):
-        fetch(k).start()
+    search = pltpu.make_async_copy(flat_hbm, flat_ref, fetch_sems.at[0])
+    search.start()
+    rest = pltpu.make_async_copy(coeff_hbm.at[:, pl.ds(NEAR, 2048 - NEAR)], rest_ref, fetch_sems.at[1])
+    rest.start()
     lanes = 256
     chunks = 2048 // lanes
     for j in range(8):
@@ -673,28 +690,40 @@
     for alpha in range(3):
         push_ref[alpha] = push[alpha : alpha + 1]
     along_ref[...] = along
-    for k in range(chunks):
-        if k * lanes % wide == 0:
-            fetch(k * lanes // wide).wait()
-        projected = dot(inter_ref[...], coeff_ref[:, k * lanes : (k + 1) * lanes])
+
+    def part_of(source_ref, start):
+        projected = dot(inter_ref[...], source_ref[:, start : start + lanes])
+        parts = []
         for j in range(lanes // 128):
             here = slice(128 * j, 128 * j + 128)
-            at = slice(k * lanes + 128 * j, k * lanes + 128 * j + 128)
             turned = projected[BLOCK:, here]
             turned = jnp.where(first, -pltpu.roll(turned, 96, 1), pltpu.roll(turned, 32, 1))
-            done_ref[:, at] = (
-                flat_ref[:, at].astype(f32) - (projected[:BLOCK, here] + turned)
-            ).astype(bf16)
+            parts.append(projected[:BLOCK, here] + turned)
+        return jnp.concatenate(parts, 1)
+
+    for k in range(NEAR // lanes):
+        here = slice(k * lanes, (k + 1) * lanes)
+        part_ref[:, here] = part_of(near_ref, k * lanes)
+    search.wait()
+    rest.wait()
+    for k in range(NEAR // lanes):
+        here = slice(k * lanes, (k + 1) * lanes)
+        done_ref[:, here] = (flat_ref[:, here].astype(f32) - part_ref[:, here]).astype(bf16)
+        send(k).start()
+    for k in range(NEAR // lanes, chunks):
+        here = slice(k * lanes, (k + 1) * lanes)
+        part = part_of(rest_ref, k * lanes - NEAR)
+        done_ref[:, here] = (flat_ref[:, here].astype(f32) - part).astype(bf16)
         send(k).start()
 
     for k in range(chunks):
         send(k).wait()
 
 
-def corrected(image, whole, flat, pos, before, after, start_pos, end_pos, coeff):
+def corrected(image, whole, near, pos, before, after, start_pos, end_pos, coeff, flat):
     return pl.pallas_call(
         project_kernel,
-        in_specs=[pl.BlockSpec(memory_space=pltpu.SMEM)] + vmem(7) + hbm(1),
+        in_specs=[pl.BlockSpec(memory_space=pltpu.SMEM)] + vmem(7) + hbm(2),
         out_specs=hbm(1) + vmem(2),
         out_shape=[
             pltpu.HBM((BLOCK, 2048), bf16),
@@ -702,15 +731,17 @@
             jax.ShapeDtypeStruct((1, 1), f32),
         ],
         scratch_shapes=[
-            pltpu.VMEM((BANDS, 2048), bf16),
+            pltpu.VMEM((BANDS, 2048 - NEAR), bf16),
+            pltpu.VMEM((BLOCK, 2048), bf16),
             pltpu.VMEM((2 * BLOCK, BANDS), bf16),
+            pltpu.VMEM((BLOCK, NEAR), f32),
             pltpu.VMEM((BLOCK, 2048), bf16),
             pltpu.SemaphoreType.DMA((8,)),
-            pltpu.SemaphoreType.DMA((FETCHES,)),
+            pltpu.SemaphoreType.DMA((2,)),
         ],
         compiler_params=pltpu.CompilerParams(vmem_limit_bytes=16 << 20),
         name="project",
-    )(image, whole, flat, pos, before, after, start_pos, end_pos, in_hbm(coeff))
+    )(image, whole, near, pos, before, after, start_pos, end_pos, in_hbm(coeff), in_hbm(flat))
 
 
 def exchanged(array):
@@ -744,8 +775,9 @@
     whole = exchanged(mine)
     image = jnp.stack([lax.axis_index("img"), lax.axis_size("img")]).astype(jnp.int32)
     ritz_values = prepared(arrived, mine)
+    near = brought_near(coeff, mine)
     correction, push, along = corrected(
-        image, whole, flat, pos, before, after, start_pos, end_pos, coeff
+        image, whole, near, pos, before, after, start_pos, end_pos, coeff, flat
     )
     return (
         correction.reshape(1, BLOCK, 1, 2048),

time: 108 us -> 107 us (level)
  waiting for transfers between devices: 13.1 us -> 11.8 us
    ppermute x2, waiting for transfers between devices: 4.26 us -> 2.99 us  [passed_along(): return lax.ppermute(block, axis, route)]
    pallas_call x0 -> x1, Pallas kernels: none -> 1.23 us  [brought_near(): pl.pallas_call(near_kernel, in_specs=hbm(2), out_specs=vmem(1)[0], out_sh...]
  transfers between devices with their start and end apart: 5 -> 5, of which waited for: 3 -> 3; matrix products, arithmetic and copies ran while one was open for 0% -> 0% of each run, Pallas kernels for 13% -> 14%
where the time goes in v8:
time: 107 us; the launch traced here: 106 us
  Pallas kernels  40.7 us (38%)
  starting transfers between devices  33 us (31%)
  blocking collectives  19.9 us (19%)
  waiting for transfers between devices  11.8 us (11%)
    all_to_all x3, starting transfers between devices, exchanged(): lax.all_to_all(array, GRID_AXES, split_axis=0, concat_axis=0, tiled=True)  21 us
    all_to_all x1, blocking collectives, exchanged(): lax.all_to_all(array, GRID_AXES, split_axis=0, concat_axis=0, tiled=True)  19.9 us
    ppermute x2, starting transfers between devices, passed_along(): return lax.ppermute(block, axis, route)  12 us
    pallas_call x1, Pallas kernels, searched(): pl.pallas_call(transform_kernel, in_specs=vmem(5) + hbm(1), out_specs=hbm...  9.28 us
    all_to_all x3, waiting for transfers between devices, exchanged(): lax.all_to_all(array, GRID_AXES, split_axis=0, concat_axis=0, tiled=True)  8.79 us
    pallas_call x1, Pallas kernels, grid_potential(): pl.pallas_call(potential_kernel, in_specs=[pl.BlockSpec(memory_space=pltp...  7.3 us
    pallas_call x1, Pallas kernels, corrected(): pl.pallas_call(project_kernel, in_specs=[pl.BlockSpec(memory_space=pltpu....  6.32 us
    pallas_call x1, Pallas kernels, force_parts(): pl.pallas_call(force_kernel, in_specs=[pl.BlockSpec(memory_space=pltpu.SM...  5.76 us
  transfers between devices with their start and end apart: 5, of which 3 were waited for; matrix products, arithmetic and copies ran while one was open for 0% of the time, Pallas kernels for 14%

profile of v8, /device:TPU:67, one launch (start us, length us, event | category | flops | bytes accessed | tf_op | source)
XLA Modules:
  0.0 106.5 jit_solution(9694899243910077574)
XLA Ops:
  0.6 4.6 %orbitals.1 = (bf16[4096,128]{1,0:T(8,128)(2,1)}, f32[4096,128]{1,0:T(8,128)}) custom-call(bf16[1024,256]{1,0:T(8,128)(2,1)} %bitcast.31, bf16[1024,2048]{1,0:T(8,128)(2,1)} %bitcast.25, f32[4]{0:T(128)} %depth_ref.3, s32[3,1,256]{2,1,0:T(1,128)} %bitcast.32, s32[1,256]{1,0:T(1,128)} %bitcast.22), custom_call_target="tpu_custom_call" | custom-call | tf_op jit(solution)/shard_map/orbitals/pallas_call | solution.py:159
  5.2 0.0 copy-start.10
  5.2 0.0 copy-start.6
  5.2 0.0 copy-start.7
  5.3 8.6 %all-to-all-start = ((bf16[32,128,128]{2,1,0:T(8,128)(2,1)}), bf16[32,128,128]{2,1,0:T(8,128)(2,1)S(1)}, u32[]{:S(2)}, u32[]{:S(2)}) async-start(bf16[32,128,128]{2,1,0:T(8,128)(2,1)} %bitcast.30), calls=%async_computation | async-start | bytes 2097152 | tf_op jit(solution)/shard_map/all_to_all | solution.py:748
  13.8 0.0 copy-done.10
  13.8 0.0 copy-done.6
  13.8 0.0 copy-done.7
  13.9 0.0 copy-start.2
  13.9 0.0 copy-start.3
  13.9 0.0 copy-start.4
  13.9 0.0 copy-start.5
  13.9 7.3 %potential.1.pot_hbm = f32[4096,128]{1,0:T(8,128)} custom-call(f32[4]{0:T(128)S(1)} %copy-done.7, s32[3,256]{1,0:T(4,128)S(1)} %bitcast.17, s32[1,256]{1,0:T(1,128)S(1)} %bitcast.23, f32[4096,128]{1,0:T(8,128)} %get-tuple-element.16.given_hbm), custom_call_target="tpu_custom_call", output_to_operand_aliasing={{}: (3, {})} | custom-call | tf_op jit(solution)/shard_map/potential/pallas_call | solution.py:273
  21.2 3.6 %all-to-all-done = bf16[32,128,128]{2,1,0:T(8,128)(2,1)S(1)} async-done(((bf16[32,128,128]{2,1,0:T(8,128)(2,1)}), bf16[32,128,128]{2,1,0:T(8,128)(2,1)S(1)}, u32[]{:S(2)}, u32[]{:S(2)}) %all-to-all-start) | async-done | bytes 1048608 | tf_op jit(solution)/shard_map/all_to_all | solution.py:748
  24.8 0.0 copy-done.2
  24.8 0.0 copy-done.3
  24.8 0.0 copy-done.4
  24.8 0.0 copy-done.5
  24.8 9.3 %transform.1 = (bf16[4096,128]{1,0:T(8,128)(2,1)}, f32[4096,128]{1,0:T(8,128)}, f32[8,128]{1,0:T(8,128)S(1)}) custom-call(bf16[4096,128]{1,0:T(8,128)(2,1)S(1)} %bitcast.15, bf16[128,256]{1,0:T(8,128)(2,1)S(1)} %copy-done.2, bf16[128,64]{1,0:T(8,128)(2,1)S(1)} %copy-done.4, bf16[64,128]{1,0:T(8,128)(2,1)S(1)} %copy-done.5, bf16[256,128]{1,0:T(8,128)(2,1)S(1)} %copy-done.3, ...), custom_call_target="tpu_custom_call" | custom-call | tf_op jit(solution)/shard_map/transform/pallas_call | solution.py:432
  34.1 0.0 copy-start
  34.1 7.0 %all-to-all-start.1 = ((bf16[32,128,128]{2,1,0:T(8,128)(2,1)}), bf16[32,128,128]{2,1,0:T(8,128)(2,1)S(1)}, u32[]{:S(2)}, u32[]{:S(2)}) async-start(bf16[32,128,128]{2,1,0:T(8,128)(2,1)} %bitcast.29), calls=%async_computation.1 | async-start | bytes 2097152 | tf_op jit(solution)/shard_map/all_to_all | solution.py:748
  41.1 0.0 copy-done
  41.1 5.8 %force.1.extra_ref = bf16[32,8,128]{2,1,0:T(8,128)(2,1)S(1)} custom-call(f32[4]{0:T(128)S(1)} %copy-done.7, f32[4096,128]{1,0:T(8,128)S(1)} %copy-done, s32[3,256]{1,0:T(4,128)S(1)} %bitcast.18, s32[1,256]{1,0:T(1,128)S(1)} %bitcast.24, f32[8,128]{1,0:T(8,128)S(1)} %get-tuple-element.19.ritz_ref), custom_call_target="tpu_custom_call" | custom-call | tf_op jit(solution)/shard_map/force/pallas_call | solution.py:507
  46.9 5.2 %all-to-all-done.1 = bf16[32,128,128]{2,1,0:T(8,128)(2,1)S(1)} async-done(((bf16[32,128,128]{2,1,0:T(8,128)(2,1)}), bf16[32,128,128]{2,1,0:T(8,128)(2,1)S(1)}, u32[]{:S(2)}, u32[]{:S(2)}) %all-to-all-start.1) | async-done | bytes 1048608 | tf_op jit(solution)/shard_map/all_to_all | solution.py:748
  52.1 4.2 %intersect.1 = (bf16[32,136,128]{2,1,0:T(8,128)(2,1)S(1)}, bf16[256,2048]{1,0:T(8,128)(2,1)S(1)}) custom-call(bf16[4096,128]{1,0:T(8,128)(2,1)S(1)} %bitcast.16, bf16[32,8,128]{2,1,0:T(8,128)(2,1)S(1)} %force.1.extra_ref, bf16[1024,2048]{1,0:T(8,128)(2,1)} %bitcast.26), custom_call_target="tpu_custom_call" | custom-call | tf_op jit(solution)/shard_map/intersect/pallas_call | solution.py:565
  56.3 0.0 copy-start.1
  56.3 19.9 %all_to_all.20.in_ref.first_ref = bf16[32,136,128]{2,1,0:T(8,128)(2,1)S(1)} all-to-all(bf16[32,136,128]{2,1,0:T(8,128)(2,1)S(1)} %get-tuple-element.20), channel_id=1, replica_groups=mesh['img'=8,'band'=8,'pw'=4] {'band','pw'}, dimensions={0} | all-to-all | bytes 2228224 | tf_op jit(solution)/shard_map/all_to_all | solution.py:748
  76.2 0.0 copy-done.1
  76.2 1.2 %total.1.order_hbm.order_ref = bf16[32,136,128]{2,1,0:T(8,128)(2,1)} custom-call(bf16[32,136,128]{2,1,0:T(8,128)(2,1)S(1)} %all_to_all.20.in_ref.first_ref), custom_call_target="tpu_custom_call" | custom-call | tf_op jit(solution)/shard_map/total/pallas_call | solution.py:606
  77.4 5.4 %all-to-all-start.3 = ((bf16[32,136,128]{2,1,0:T(8,128)(2,1)}), bf16[32,136,128]{2,1,0:T(8,128)(2,1)S(1)}, u32[]{:S(2)}, u32[]{:S(2)}) async-start(bf16[32,136,128]{2,1,0:T(8,128)(2,1)} %total.1.order_hbm.order_ref), calls=%async_computation.3 | async-start | bytes 2228224 | tf_op jit(solution)/shard_map/all_to_all | solution.py:748
  82.9 10.1 %collective-permute-start = (s32[3,256]{1,0:T(4,128)S(1)}, s32[3,256]{1,0:T(4,128)S(1)}, u32[]{:S(2)}, u32[]{:S(2)}) collective-permute-start(s32[3,256]{1,0:T(4,128)S(1)} %bitcast.19), channel_id=1, source_target_pairs={{0,32},{32,64},{64,96},{96,128},{128,160},{160,192},{192,224},{1,3... | collective-permute-start | bytes 9224 | tf_op jit(solution)/shard_map/ppermute | solution.py:754
  93.0 1.9 %collective-permute-start.1 = (s32[3,256]{1,0:T(4,128)S(1)}, s32[3,256]{1,0:T(4,128)S(1)}, u32[]{:S(2)}, u32[]{:S(2)}) collective-permute-start(s32[3,256]{1,0:T(4,128)S(1)} %bitcast.20), channel_id=1, source_target_pairs={{32,0},{64,32},{96,64},{128,96},{160,128},{192,160},{224,192},{33,... | collective-permute-start | bytes 9224 | tf_op jit(solution)/shard_map/ppermute | solution.py:754
  94.9 0.1 pad_add_fusion.image_ref
  95.0 1.2 %near.1.near_ref = bf16[1024,512]{1,0:T(8,128)(2,1)S(1)} custom-call(bf16[1024,2048]{1,0:T(8,128)(2,1)} %bitcast.27, bf16[32,136,128]{2,1,0:T(8,128)(2,1)} %total.1.order_hbm.order_ref), custom_call_target="tpu_custom_call" | custom-call | tf_op jit(solution)/shard_map/near/pallas_call | solution.py:195
  96.2 0.0 copy-start.8
  96.2 0.0 copy-start.9
  96.2 0.8 prepare.1
  97.0 0.0 collective-permute-done.before_ref
  97.0 3.0 %collective-permute-done.1.after_ref = s32[3,256]{1,0:T(4,128)S(1)} collective-permute-done((s32[3,256]{1,0:T(4,128)S(1)}, s32[3,256]{1,0:T(4,128)S(1)}, u32[]{:S(2)}, u32[]{:S(2)}) %collective-permute-start.1) | collective-permute-done | bytes 3104 | tf_op jit(solution)/shard_map/ppermute | solution.py:754
  100.0 0.0 all-to-all-done.3.whole_ref
  100.0 0.0 copy-done.8
  100.0 0.0 copy-done.9
  100.0 6.3 %project.1 = (bf16[256,2048]{1,0:T(8,128)(2,1)}, f32[3,1,256]{2,1,0:T(1,128)}, f32[1,1]{1,0:T(1,128)}) custom-call(s32[2]{0:T(128)S(1)} %pad_add_fusion.image_ref, bf16[32,136,128]{2,1,0:T(8,128)(2,1)S(1)} %all-to-all-done.3.whole_ref, bf16[1024,512]{1,0:T(8,128)(2,1)S(1)} %near.1.near_ref, s32[3,256]{1,0:T(4,128)S(1)} %bitcast.21, ...), custom_call_target="tpu_custom_call" | custom-call | tf_op jit(solution)/shard_map/project/pallas_call | solution.py:724
  (1 shorter events, 0.0 us)
Async XLA Ops:
  5.2 8.6 %copy-start.10 = (s32[1,3,256]{2,0,1:T(1,128)S(1)}, s32[1,3,256]{2,0,1:T(1,128)}, u32[]{:S(2)}) copy-start(s32[1,3,256]{2,0,1:T(1,128)} %param.13) | copy-start | bytes 9220
  5.2 8.6 %copy-start.6 = (s32[256]{0:T(256)S(1)}, s32[256]{0:T(256)}, u32[]{:S(2)}) copy-start(s32[256]{0:T(256)} %param.16) | copy-start | bytes 3076
  5.2 8.6 %copy-start.7 = (f32[4]{0:T(128)S(1)}, f32[4]{0:T(128)}, u32[]{:S(2)}) copy-start(f32[4]{0:T(128)} %depth_ref.3) | copy-start | bytes 52
  5.3 19.5 %all-to-all-start = ((bf16[32,128,128]{2,1,0:T(8,128)(2,1)}), bf16[32,128,128]{2,1,0:T(8,128)(2,1)S(1)}, u32[]{:S(2)}, u32[]{:S(2)}) async-start(bf16[32,128,128]{2,1,0:T(8,128)(2,1)} %bitcast.30), calls=%async_computation | async-start | bytes 2097152 | tf_op jit(solution)/shard_map/all_to_all | solution.py:748
  13.9 10.9 %copy-start.2 = (bf16[128,256]{1,0:T(8,128)(2,1)S(1)}, bf16[128,256]{1,0:T(8,128)(2,1)}, u32[]{:S(2)}) copy-start(bf16[128,256]{1,0:T(8,128)(2,1)} %constant.16.clone.zf_ref) | copy-start | bytes 196612
  13.9 10.9 %copy-start.3 = (bf16[256,128]{1,0:T(8,128)(2,1)S(1)}, bf16[256,128]{1,0:T(8,128)(2,1)}, u32[]{:S(2)}) copy-start(bf16[256,128]{1,0:T(8,128)(2,1)} %constant.19.clone.zi_ref) | copy-start | bytes 196612
  13.9 10.9 %copy-start.4 = (bf16[128,64]{1,0:T(8,128)(2,1)S(1)}, bf16[128,64]{1,0:T(8,128)(2,1)}, u32[]{:S(2)}) copy-start(bf16[128,64]{1,0:T(8,128)(2,1)} %constant.17.clone.left_ref) | copy-start | bytes 49156
  13.9 10.9 %copy-start.5 = (bf16[64,128]{1,0:T(8,128)(2,1)S(1)}, bf16[64,128]{1,0:T(8,128)(2,1)}, u32[]{:S(2)}) copy-start(bf16[64,128]{1,0:T(8,128)(2,1)} %constant.18.clone.left_inv_ref) | copy-start | bytes 49156
  34.1 7.0 %copy-start = (f32[4096,128]{1,0:T(8,128)S(1)}, f32[4096,128]{1,0:T(8,128)}, u32[]{:S(2)}) copy-start(f32[4096,128]{1,0:T(8,128)} %get-tuple-element.18.dens_ref) | copy-start | bytes 6291460
  34.1 18.0 %all-to-all-start.1 = ((bf16[32,128,128]{2,1,0:T(8,128)(2,1)}), bf16[32,128,128]{2,1,0:T(8,128)(2,1)S(1)}, u32[]{:S(2)}, u32[]{:S(2)}) async-start(bf16[32,128,128]{2,1,0:T(8,128)(2,1)} %bitcast.29), calls=%async_computation.1 | async-start | bytes 2097152 | tf_op jit(solution)/shard_map/all_to_all | solution.py:748
  56.3 19.9 %copy-start.1 = (bf16[256,2048]{1,0:T(8,128)(2,1)}, bf16[256,2048]{1,0:T(8,128)(2,1)S(1)}, u32[]{:S(2)}) copy-start(bf16[256,2048]{1,0:T(8,128)(2,1)S(1)} %get-tuple-element.22.flat_hbm) | copy-start | bytes 3145732
  77.4 22.6 %all-to-all-start.3 = ((bf16[32,136,128]{2,1,0:T(8,128)(2,1)}), bf16[32,136,128]{2,1,0:T(8,128)(2,1)S(1)}, u32[]{:S(2)}, u32[]{:S(2)}) async-start(bf16[32,136,128]{2,1,0:T(8,128)(2,1)} %total.1.order_hbm.order_ref), calls=%async_computation.3 | async-start | bytes 2228224 | tf_op jit(solution)/shard_map/all_to_all | solution.py:748
  82.9 14.1 %collective-permute-start = (s32[3,256]{1,0:T(4,128)S(1)}, s32[3,256]{1,0:T(4,128)S(1)}, u32[]{:S(2)}, u32[]{:S(2)}) collective-permute-start(s32[3,256]{1,0:T(4,128)S(1)} %bitcast.19), channel_id=1, source_target_pairs={{0,32},{32,64},{64,96},{96,128},{128,160},{160,192},{192,224},{1,3... | collective-permute-start | bytes 9224 | tf_op jit(solution)/shard_map/ppermute | solution.py:754
  93.0 7.0 %collective-permute-start.1 = (s32[3,256]{1,0:T(4,128)S(1)}, s32[3,256]{1,0:T(4,128)S(1)}, u32[]{:S(2)}, u32[]{:S(2)}) collective-permute-start(s32[3,256]{1,0:T(4,128)S(1)} %bitcast.20), channel_id=1, source_target_pairs={{32,0},{64,32},{96,64},{128,96},{160,128},{192,160},{224,192},{33,... | collective-permute-start | bytes 9224 | tf_op jit(solution)/shard_map/ppermute | solution.py:754
  96.2 3.8 %copy-start.8 = (s32[3,256]{1,0:T(4,128)S(1)}, s32[3,256]{1,0:T(4,128)}, u32[]{:S(2)}) copy-start(s32[3,256]{1,0:T(4,128)} %start_ref.1) | copy-start | bytes 9220
  96.2 3.8 %copy-start.9 = (s32[3,256]{1,0:T(4,128)S(1)}, s32[3,256]{1,0:T(4,128)}, u32[]{:S(2)}) copy-start(s32[3,256]{1,0:T(4,128)} %end_ref.1) | copy-start | bytes 9220

commit v9 on v8

--- a/solution.py
+++ b/solution.py
@@ -27,7 +27,7 @@
 LINE = W + 1
 NEAR = 512
 SHARES = 8
-EARLY = 4
+EARLY = 6
 EARLY_ROWS = G * G * EARLY // SHARES
 
 kinetic_scale = 0.01

time: 107 us -> 106 us (level)
  blocking collectives: 19.9 us -> 17 us
  starting transfers between devices: 33 us -> 35.4 us
    ppermute x2, starting transfers between devices: 12 us -> 16.8 us  [passed_along(): return lax.ppermute(block, axis, route)]
    all_to_all x1, blocking collectives: 19.9 us -> 17 us  [exchanged(): lax.all_to_all(array, GRID_AXES, split_axis=0, concat_axis=0, tiled=True)]
    all_to_all x3, starting transfers between devices: 21 us -> 18.6 us  [exchanged(): lax.all_to_all(array, GRID_AXES, split_axis=0, concat_axis=0, tiled=True)]
where the time goes in v9:
time: 106 us
  Pallas kernels  40.6 us (38%)
  starting transfers between devices  35.4 us (33%)
  blocking collectives  17 us (16%)
  waiting for transfers between devices  11.4 us (11%)
    all_to_all x3, starting transfers between devices, exchanged(): lax.all_to_all(array, GRID_AXES, split_axis=0, concat_axis=0, tiled=True)  18.6 us
    all_to_all x1, blocking collectives, exchanged(): lax.all_to_all(array, GRID_AXES, split_axis=0, concat_axis=0, tiled=True)  17 us
    ppermute x2, starting transfers between devices, passed_along(): return lax.ppermute(block, axis, route)  16.8 us
    pallas_call x1, Pallas kernels, searched(): pl.pallas_call(transform_kernel, in_specs=vmem(5) + hbm(1), out_specs=hbm...  9.28 us
    all_to_all x3, waiting for transfers between devices, exchanged(): lax.all_to_all(array, GRID_AXES, split_axis=0, concat_axis=0, tiled=True)  8.41 us
    pallas_call x1, Pallas kernels, grid_potential(): pl.pallas_call(potential_kernel, in_specs=[pl.BlockSpec(memory_space=pltp...  7.3 us
    pallas_call x1, Pallas kernels, corrected(): pl.pallas_call(project_kernel, in_specs=[pl.BlockSpec(memory_space=pltpu....  6.32 us
    pallas_call x1, Pallas kernels, force_parts(): pl.pallas_call(force_kernel, in_specs=[pl.BlockSpec(memory_space=pltpu.SM...  5.76 us
  transfers between devices with their start and end apart: 5, of which 3 were waited for; matrix products, arithmetic and copies ran while one was open for 0% of the time, Pallas kernels for 14%

profile of v9, /device:TPU:67, one launch (start us, length us, event | category | flops | bytes accessed | tf_op | source)
XLA Modules:
  0.0 105.6 jit_solution(17909695665851111624)
XLA Ops:
  0.6 4.6 %orbitals.1 = (bf16[4096,128]{1,0:T(8,128)(2,1)}, f32[4096,128]{1,0:T(8,128)}) custom-call(bf16[1024,256]{1,0:T(8,128)(2,1)} %bitcast.31, bf16[1024,2048]{1,0:T(8,128)(2,1)} %bitcast.25, f32[4]{0:T(128)} %depth_ref.3, s32[3,1,256]{2,1,0:T(1,128)} %bitcast.32, s32[1,256]{1,0:T(1,128)} %bitcast.22), custom_call_target="tpu_custom_call" | custom-call | tf_op jit(solution)/shard_map/orbitals/pallas_call | solution.py:159
  5.2 0.0 copy-start.10
  5.2 0.0 copy-start.6
  5.2 0.0 copy-start.7
  5.3 8.6 %all-to-all-start = ((bf16[32,128,128]{2,1,0:T(8,128)(2,1)}), bf16[32,128,128]{2,1,0:T(8,128)(2,1)S(1)}, u32[]{:S(2)}, u32[]{:S(2)}) async-start(bf16[32,128,128]{2,1,0:T(8,128)(2,1)} %bitcast.30), calls=%async_computation | async-start | bytes 2097152 | tf_op jit(solution)/shard_map/all_to_all | solution.py:748
  13.8 0.0 copy-done.10
  13.8 0.0 copy-done.6
  13.8 0.0 copy-done.7
  13.9 0.0 copy-start.2
  13.9 0.0 copy-start.3
  13.9 0.0 copy-start.4
  13.9 0.0 copy-start.5
  13.9 7.3 %potential.1.pot_hbm = f32[4096,128]{1,0:T(8,128)} custom-call(f32[4]{0:T(128)S(1)} %copy-done.7, s32[3,256]{1,0:T(4,128)S(1)} %bitcast.17, s32[1,256]{1,0:T(1,128)S(1)} %bitcast.23, f32[4096,128]{1,0:T(8,128)} %get-tuple-element.16.given_hbm), custom_call_target="tpu_custom_call", output_to_operand_aliasing={{}: (3, {})} | custom-call | tf_op jit(solution)/shard_map/potential/pallas_call | solution.py:273
  21.2 3.5 %all-to-all-done = bf16[32,128,128]{2,1,0:T(8,128)(2,1)S(1)} async-done(((bf16[32,128,128]{2,1,0:T(8,128)(2,1)}), bf16[32,128,128]{2,1,0:T(8,128)(2,1)S(1)}, u32[]{:S(2)}, u32[]{:S(2)}) %all-to-all-start) | async-done | bytes 1048608 | tf_op jit(solution)/shard_map/all_to_all | solution.py:748
  24.8 0.0 copy-done.2
  24.8 0.0 copy-done.3
  24.8 0.0 copy-done.4
  24.8 0.0 copy-done.5
  24.8 9.3 %transform.1 = (bf16[4096,128]{1,0:T(8,128)(2,1)}, f32[4096,128]{1,0:T(8,128)}, f32[8,128]{1,0:T(8,128)S(1)}) custom-call(bf16[4096,128]{1,0:T(8,128)(2,1)S(1)} %bitcast.15, bf16[128,256]{1,0:T(8,128)(2,1)S(1)} %copy-done.2, bf16[128,64]{1,0:T(8,128)(2,1)S(1)} %copy-done.4, bf16[64,128]{1,0:T(8,128)(2,1)S(1)} %copy-done.5, bf16[256,128]{1,0:T(8,128)(2,1)S(1)} %copy-done.3, ...), custom_call_target="tpu_custom_call" | custom-call | tf_op jit(solution)/shard_map/transform/pallas_call | solution.py:432
  34.1 0.0 copy-start
  34.1 5.2 %all-to-all-start.1 = ((bf16[32,128,128]{2,1,0:T(8,128)(2,1)}), bf16[32,128,128]{2,1,0:T(8,128)(2,1)S(1)}, u32[]{:S(2)}, u32[]{:S(2)}) async-start(bf16[32,128,128]{2,1,0:T(8,128)(2,1)} %bitcast.29), calls=%async_computation.1 | async-start | bytes 2097152 | tf_op jit(solution)/shard_map/all_to_all | solution.py:748
  39.3 0.0 copy-done
  39.3 5.8 %force.1.extra_ref = bf16[32,8,128]{2,1,0:T(8,128)(2,1)S(1)} custom-call(f32[4]{0:T(128)S(1)} %copy-done.7, f32[4096,128]{1,0:T(8,128)S(1)} %copy-done, s32[3,256]{1,0:T(4,128)S(1)} %bitcast.18, s32[1,256]{1,0:T(1,128)S(1)} %bitcast.24, f32[8,128]{1,0:T(8,128)S(1)} %get-tuple-element.19.ritz_ref), custom_call_target="tpu_custom_call" | custom-call | tf_op jit(solution)/shard_map/force/pallas_call | solution.py:507
  45.1 4.9 %all-to-all-done.1 = bf16[32,128,128]{2,1,0:T(8,128)(2,1)S(1)} async-done(((bf16[32,128,128]{2,1,0:T(8,128)(2,1)}), bf16[32,128,128]{2,1,0:T(8,128)(2,1)S(1)}, u32[]{:S(2)}, u32[]{:S(2)}) %all-to-all-start.1) | async-done | bytes 1048608 | tf_op jit(solution)/shard_map/all_to_all | solution.py:748
  50.0 4.2 %intersect.1 = (bf16[32,136,128]{2,1,0:T(8,128)(2,1)S(1)}, bf16[256,2048]{1,0:T(8,128)(2,1)S(1)}) custom-call(bf16[4096,128]{1,0:T(8,128)(2,1)S(1)} %bitcast.16, bf16[32,8,128]{2,1,0:T(8,128)(2,1)S(1)} %force.1.extra_ref, bf16[1024,2048]{1,0:T(8,128)(2,1)} %bitcast.26), custom_call_target="tpu_custom_call" | custom-call | tf_op jit(solution)/shard_map/intersect/pallas_call | solution.py:565
  54.1 0.0 copy-start.1
  54.2 17.0 %all_to_all.20.in_ref.first_ref = bf16[32,136,128]{2,1,0:T(8,128)(2,1)S(1)} all-to-all(bf16[32,136,128]{2,1,0:T(8,128)(2,1)S(1)} %get-tuple-element.20), channel_id=1, replica_groups=mesh['img'=8,'band'=8,'pw'=4] {'band','pw'}, dimensions={0} | all-to-all | bytes 2228224 | tf_op jit(solution)/shard_map/all_to_all | solution.py:748
  71.2 0.0 copy-done.1
  71.2 1.2 %total.1.order_hbm.order_ref = bf16[32,136,128]{2,1,0:T(8,128)(2,1)} custom-call(bf16[32,136,128]{2,1,0:T(8,128)(2,1)S(1)} %all_to_all.20.in_ref.first_ref), custom_call_target="tpu_custom_call" | custom-call | tf_op jit(solution)/shard_map/total/pallas_call | solution.py:606
  72.4 4.8 %all-to-all-start.3 = ((bf16[32,136,128]{2,1,0:T(8,128)(2,1)}), bf16[32,136,128]{2,1,0:T(8,128)(2,1)S(1)}, u32[]{:S(2)}, u32[]{:S(2)}) async-start(bf16[32,136,128]{2,1,0:T(8,128)(2,1)} %total.1.order_hbm.order_ref), calls=%async_computation.3 | async-start | bytes 2228224 | tf_op jit(solution)/shard_map/all_to_all | solution.py:748
  77.2 14.9 %collective-permute-start = (s32[3,256]{1,0:T(4,128)S(1)}, s32[3,256]{1,0:T(4,128)S(1)}, u32[]{:S(2)}, u32[]{:S(2)}) collective-permute-start(s32[3,256]{1,0:T(4,128)S(1)} %bitcast.19), channel_id=1, source_target_pairs={{0,32},{32,64},{64,96},{96,128},{128,160},{160,192},{192,224},{1,3... | collective-permute-start | bytes 9224 | tf_op jit(solution)/shard_map/ppermute | solution.py:754
  92.1 1.9 %collective-permute-start.1 = (s32[3,256]{1,0:T(4,128)S(1)}, s32[3,256]{1,0:T(4,128)S(1)}, u32[]{:S(2)}, u32[]{:S(2)}) collective-permute-start(s32[3,256]{1,0:T(4,128)S(1)} %bitcast.20), channel_id=1, source_target_pairs={{32,0},{64,32},{96,64},{128,96},{160,128},{192,160},{224,192},{33,... | collective-permute-start | bytes 9224 | tf_op jit(solution)/shard_map/ppermute | solution.py:754
  94.0 0.1 pad_add_fusion.image_ref
  94.1 1.2 %near.1.near_ref = bf16[1024,512]{1,0:T(8,128)(2,1)S(1)} custom-call(bf16[1024,2048]{1,0:T(8,128)(2,1)} %bitcast.27, bf16[32,136,128]{2,1,0:T(8,128)(2,1)} %total.1.order_hbm.order_ref), custom_call_target="tpu_custom_call" | custom-call | tf_op jit(solution)/shard_map/near/pallas_call | solution.py:195
  95.4 0.0 copy-start.8
  95.4 0.0 copy-start.9
  95.4 0.8 prepare.1
  96.2 0.0 collective-permute-done.before_ref
  96.2 3.0 %collective-permute-done.1.after_ref = s32[3,256]{1,0:T(4,128)S(1)} collective-permute-done((s32[3,256]{1,0:T(4,128)S(1)}, s32[3,256]{1,0:T(4,128)S(1)}, u32[]{:S(2)}, u32[]{:S(2)}) %collective-permute-start.1) | collective-permute-done | bytes 3104 | tf_op jit(solution)/shard_map/ppermute | solution.py:754
  99.2 0.0 all-to-all-done.3.whole_ref
  99.2 0.0 copy-done.8
  99.2 0.0 copy-done.9
  99.2 6.3 %project.1 = (bf16[256,2048]{1,0:T(8,128)(2,1)}, f32[3,1,256]{2,1,0:T(1,128)}, f32[1,1]{1,0:T(1,128)}) custom-call(s32[2]{0:T(128)S(1)} %pad_add_fusion.image_ref, bf16[32,136,128]{2,1,0:T(8,128)(2,1)S(1)} %all-to-all-done.3.whole_ref, bf16[1024,512]{1,0:T(8,128)(2,1)S(1)} %near.1.near_ref, s32[3,256]{1,0:T(4,128)S(1)} %bitcast.21, ...), custom_call_target="tpu_custom_call" | custom-call | tf_op jit(solution)/shard_map/project/pallas_call | solution.py:724
  (1 shorter events, 0.0 us)
Async XLA Ops:
  5.2 8.6 %copy-start.10 = (s32[1,3,256]{2,0,1:T(1,128)S(1)}, s32[1,3,256]{2,0,1:T(1,128)}, u32[]{:S(2)}) copy-start(s32[1,3,256]{2,0,1:T(1,128)} %param.13) | copy-start | bytes 9220
  5.2 8.6 %copy-start.6 = (s32[256]{0:T(256)S(1)}, s32[256]{0:T(256)}, u32[]{:S(2)}) copy-start(s32[256]{0:T(256)} %param.16) | copy-start | bytes 3076
  5.2 8.6 %copy-start.7 = (f32[4]{0:T(128)S(1)}, f32[4]{0:T(128)}, u32[]{:S(2)}) copy-start(f32[4]{0:T(128)} %depth_ref.3) | copy-start | bytes 52
  5.3 19.5 %all-to-all-start = ((bf16[32,128,128]{2,1,0:T(8,128)(2,1)}), bf16[32,128,128]{2,1,0:T(8,128)(2,1)S(1)}, u32[]{:S(2)}, u32[]{:S(2)}) async-start(bf16[32,128,128]{2,1,0:T(8,128)(2,1)} %bitcast.30), calls=%async_computation | async-start | bytes 2097152 | tf_op jit(solution)/shard_map/all_to_all | solution.py:748
  13.9 10.9 %copy-start.2 = (bf16[128,256]{1,0:T(8,128)(2,1)S(1)}, bf16[128,256]{1,0:T(8,128)(2,1)}, u32[]{:S(2)}) copy-start(bf16[128,256]{1,0:T(8,128)(2,1)} %constant.16.clone.zf_ref) | copy-start | bytes 196612
  13.9 10.9 %copy-start.3 = (bf16[256,128]{1,0:T(8,128)(2,1)S(1)}, bf16[256,128]{1,0:T(8,128)(2,1)}, u32[]{:S(2)}) copy-start(bf16[256,128]{1,0:T(8,128)(2,1)} %constant.19.clone.zi_ref) | copy-start | bytes 196612
  13.9 10.9 %copy-start.4 = (bf16[128,64]{1,0:T(8,128)(2,1)S(1)}, bf16[128,64]{1,0:T(8,128)(2,1)}, u32[]{:S(2)}) copy-start(bf16[128,64]{1,0:T(8,128)(2,1)} %constant.17.clone.left_ref) | copy-start | bytes 49156
  13.9 10.9 %copy-start.5 = (bf16[64,128]{1,0:T(8,128)(2,1)S(1)}, bf16[64,128]{1,0:T(8,128)(2,1)}, u32[]{:S(2)}) copy-start(bf16[64,128]{1,0:T(8,128)(2,1)} %constant.18.clone.left_inv_ref) | copy-start | bytes 49156
  34.1 5.3 %copy-start = (f32[4096,128]{1,0:T(8,128)S(1)}, f32[4096,128]{1,0:T(8,128)}, u32[]{:S(2)}) copy-start(f32[4096,128]{1,0:T(8,128)} %get-tuple-element.18.dens_ref) | copy-start | bytes 6291460
  34.1 15.9 %all-to-all-start.1 = ((bf16[32,128,128]{2,1,0:T(8,128)(2,1)}), bf16[32,128,128]{2,1,0:T(8,128)(2,1)S(1)}, u32[]{:S(2)}, u32[]{:S(2)}) async-start(bf16[32,128,128]{2,1,0:T(8,128)(2,1)} %bitcast.29), calls=%async_computation.1 | async-start | bytes 2097152 | tf_op jit(solution)/shard_map/all_to_all | solution.py:748
  54.1 17.0 %copy-start.1 = (bf16[256,2048]{1,0:T(8,128)(2,1)}, bf16[256,2048]{1,0:T(8,128)(2,1)S(1)}, u32[]{:S(2)}) copy-start(bf16[256,2048]{1,0:T(8,128)(2,1)S(1)} %get-tuple-element.22.flat_hbm) | copy-start | bytes 3145732
  72.4 26.7 %all-to-all-start.3 = ((bf16[32,136,128]{2,1,0:T(8,128)(2,1)}), bf16[32,136,128]{2,1,0:T(8,128)(2,1)S(1)}, u32[]{:S(2)}, u32[]{:S(2)}) async-start(bf16[32,136,128]{2,1,0:T(8,128)(2,1)} %total.1.order_hbm.order_ref), calls=%async_computation.3 | async-start | bytes 2228224 | tf_op jit(solution)/shard_map/all_to_all | solution.py:748
  77.2 18.9 %collective-permute-start = (s32[3,256]{1,0:T(4,128)S(1)}, s32[3,256]{1,0:T(4,128)S(1)}, u32[]{:S(2)}, u32[]{:S(2)}) collective-permute-start(s32[3,256]{1,0:T(4,128)S(1)} %bitcast.19), channel_id=1, source_target_pairs={{0,32},{32,64},{64,96},{96,128},{128,160},{160,192},{192,224},{1,3... | collective-permute-start | bytes 9224 | tf_op jit(solution)/shard_map/ppermute | solution.py:754
  92.1 7.0 %collective-permute-start.1 = (s32[3,256]{1,0:T(4,128)S(1)}, s32[3,256]{1,0:T(4,128)S(1)}, u32[]{:S(2)}, u32[]{:S(2)}) collective-permute-start(s32[3,256]{1,0:T(4,128)S(1)} %bitcast.20), channel_id=1, source_target_pairs={{32,0},{64,32},{96,64},{128,96},{160,128},{192,160},{224,192},{33,... | collective-permute-start | bytes 9224 | tf_op jit(solution)/shard_map/ppermute | solution.py:754
  95.4 3.8 %copy-start.8 = (s32[3,256]{1,0:T(4,128)S(1)}, s32[3,256]{1,0:T(4,128)}, u32[]{:S(2)}) copy-start(s32[3,256]{1,0:T(4,128)} %start_ref.1) | copy-start | bytes 9220
  95.4 3.8 %copy-start.9 = (s32[3,256]{1,0:T(4,128)S(1)}, s32[3,256]{1,0:T(4,128)}, u32[]{:S(2)}) copy-start(s32[3,256]{1,0:T(4,128)} %end_ref.1) | copy-start | bytes 9220
